TPU v7x, 1024 devices: a whole 4x8x16 slice. The times are simulated.
1024 devices in a mesh: dp: 16 (over z), shard: 64 (over x, y, core).
Axes of the slice: x: 4, y: 8, z: 16, core: 2. Of those that a mesh axis runs over, the one named last changes fastest.
Arguments:
- grads: bfloat16 [16, 512, 256, 256], P('dp', None, 'shard'), may hold values from -24 to 24
- owner_table: int32 [16, 128], replicated, may hold values from 0 to 31, as said below
- block_counts: int32 [16, 64], replicated, may hold values from 0 to 2, as said below
- prev_left: float32 [2048, 256, 256], P(('dp', 'shard')), as said below
- prev_right: float32 [2048, 256, 256], P(('dp', 'shard')), as said below
Outputs:
- updates: bfloat16 [512, 256, 256], P(None, 'shard')
Inputs may be any that keep to these rules, and one draw needn't show every extreme that they name: `owner_table`: for group d and owner o, entries o * 2 to o * 2 + block_counts[d, o] - 1 of row d name blocks of the group, and these live entries together name each of the group's 32 blocks exactly once; the other entries name arbitrary blocks of the group. `block_counts`: each row sums to 32; in every row some owner has exactly 2 blocks. `prev_left`: each slot's matrix is symmetric positive semidefinite. `prev_right`: each slot's matrix is symmetric positive semidefinite.
All inputs are finite; a program needn't handle non-finite values.
Results may differ from a plain program's by a relative error of at most 0.02.
Values may be sent and summed in bfloat16 or wider, within the bound.
No kernel may reach another device: no remote copies, remote signals or barrier semaphores. Data moves between devices by JAX's collectives and lax.ppermute only.
A program may use at most 32 MiB of HBM per device.

v0:
```python
import jax
import jax.numpy as jnp
from jax import lax
from jax.sharding import PartitionSpec as P

CAP = 2


stat_decay = 0.9
eps_small = 1e-06


def inverse_root(factor):
    size_now = factor.shape[0]
    unit_matrix = jnp.eye(size_now, dtype=jnp.float32)
    norm_scale = size_now * jnp.sqrt(jnp.mean(factor * factor) + eps_small)
    start = factor / norm_scale
    first = (1.25 * unit_matrix - 0.25 * start).astype(jnp.bfloat16)
    square = jnp.dot(first, first, preferred_element_type=jnp.float32).astype(jnp.bfloat16)
    fourth = jnp.dot(square, square, preferred_element_type=jnp.float32).astype(jnp.bfloat16)
    next_state = jnp.dot(fourth, start.astype(jnp.bfloat16), preferred_element_type=jnp.float32)
    second = (1.25 * unit_matrix - 0.25 * next_state).astype(jnp.bfloat16)
    return jnp.dot(first, second, preferred_element_type=jnp.float32).astype(jnp.bfloat16)


def precondition(grad_block, left_prev, right_prev):
    left_factor = stat_decay * left_prev + (1.0 - stat_decay) * jnp.dot(
        grad_block, grad_block.T, preferred_element_type=jnp.float32
    )
    right_factor = stat_decay * right_prev + (1.0 - stat_decay) * jnp.dot(
        grad_block.T, grad_block, preferred_element_type=jnp.float32
    )
    root_left = inverse_root(left_factor)
    root_right = inverse_root(right_factor)
    half_done = jnp.dot(root_left, grad_block, preferred_element_type=jnp.float32).astype(
        jnp.bfloat16
    )
    precond = jnp.dot(half_done, root_right, preferred_element_type=jnp.float32)
    grad_wide = grad_block.astype(jnp.float32)
    grad_norm = jnp.sqrt(jnp.mean(grad_wide * grad_wide) + eps_small)
    cond_norm = jnp.sqrt(jnp.mean(precond * precond) + eps_small)
    return (precond * (grad_norm / cond_norm)).astype(jnp.bfloat16)


def refresh(arrived, prev_left, prev_right):
    return jax.vmap(precondition)(arrived, prev_left, prev_right)


def body(grads, owner_table, block_counts, prev_left, prev_right):
    owners = lax.axis_size("shard")
    groups = lax.axis_size("dp")
    my_group = lax.axis_index("dp")
    blocks = grads.shape[1]
    row_count = grads.shape[2]
    block_width = grads.shape[3]
    per_group = blocks // groups
    slot_total = owners * CAP
    slot_ids = jnp.arange(slot_total, dtype=jnp.int32)
    is_live = (slot_ids % CAP)[None, :] < block_counts[:, slot_ids // CAP]
    matches = (
        owner_table[:, None, :] == jnp.arange(per_group, dtype=jnp.int32)[None, :, None]
    ) & is_live[:, None, :]
    earliest = jnp.min(jnp.where(matches, slot_ids[None, None, :], slot_total), axis=2)
    has_slot = earliest < slot_total
    earliest = jnp.minimum(earliest, slot_total - 1)
    pick_index = earliest % CAP * owners + earliest // CAP
    local_terms = grads[0].astype(jnp.float32)
    summed = lax.psum_scatter(
        local_terms.astype(jnp.bfloat16), "dp", scatter_dimension=0, tiled=True
    )
    table_row = owner_table[my_group].reshape(owners, CAP).T
    outgoing = jnp.take(summed, table_row, axis=0)
    arrived = lax.all_to_all(outgoing, "shard", split_axis=1, concat_axis=1, tiled=True).reshape(
        CAP, block_width, block_width
    )
    fresh = refresh(arrived, prev_left, prev_right)
    returned = lax.all_to_all(
        fresh.reshape(CAP, owners, row_count, block_width),
        "shard",
        split_axis=1,
        concat_axis=1,
        tiled=True,
    )
    chosen = jnp.take(
        returned.reshape(CAP * owners, row_count, block_width), pick_index[my_group], axis=0
    )
    chosen = jnp.where(has_slot[my_group][:, None, None], chosen, jnp.zeros_like(chosen))
    return lax.all_gather(chosen, "dp", axis=0, tiled=True)


def solution(mesh):
    return jax.shard_map(
        body,
        mesh=mesh,
        in_specs=(
            P("dp", None, "shard", None),
            P(),
            P(),
            P(("dp", "shard"), None, None),
            P(("dp", "shard"), None, None),
        ),
        out_specs=P(None, "shard", None),
        check_vma=False,
    )
```

profile of v0, /device:TPU:6, one launch (start us, length us, event | category | flops | bytes accessed | tf_op | source)
XLA Modules:
  0.0 289.6 jit_solution(9677551481337451374)
XLA Ops:
  6.5 0.0 all-reduce.3.cloned.1.call-start
  6.5 0.7 all-reduce.3.cloned.1.call-update
  7.3 0.0 copy-start.3
  7.3 0.7 copy-done.3
  8.0 0.1 reshape_squeeze.3
  8.1 0.0 copy-start.2
  8.1 0.1 copy.26
  8.2 0.1 reshape.160
  8.3 0.5 copy-done.2
  8.8 0.1 copy.24
  8.9 0.6 gather_fusion
  9.6 0.1 compare_bitcast_fusion
  9.7 0.1 copy.25
  9.8 1.3 dynamic-slice
  11.7 0.3 select_reduce_fusion
  12.1 151.8 %all-reduce.3.cloned.1.call-done = bf16[512,4,256]{2,1,0:T(4,128)(2,1)} async-done(((bf16[512,4,256]{2,1,0:T(4,128)(2,1)}), bf16[512,4,256]{2,1,0:T(4,128)(2,1)}) %all-reduce.3.cloned.1.call-update) | async-done | bytes 1048592
  163.9 0.9 constant_dynamic-slice_fusion.7
  164.8 0.8 gather_fusion.1
  165.6 0.9 copy_select_fusion
  166.6 10.5 %all-to-all-start = ((bf16[2,64,4,256]{3,2,0,1:T(4,128)(2,1)}), bf16[2,64,4,256]{3,2,0,1:T(4,128)(2,1)S(1)}, u32[]{:S(2)}, u32[]{:S(2)}) async-start(bf16[2,64,4,256]{3,2,0,1:T(4,128)(2,1)} %copy_select_fusion), calls=%async_computation | async-start | bytes 524288 | tf_op jit(solution)/shard_map/all_to_all | solution.py:73
  177.1 0.0 copy-start
  177.1 11.5 %all-to-all-done = bf16[2,64,4,256]{3,2,0,1:T(4,128)(2,1)S(1)} async-done(((bf16[2,64,4,256]{3,2,0,1:T(4,128)(2,1)}), bf16[2,64,4,256]{3,2,0,1:T(4,128)(2,1)S(1)}, u32[]{:S(2)}, u32[]{:S(2)}) %all-to-all-start) | async-done | bytes 262176 | tf_op jit(solution)/shard_map/all_to_all | solution.py:73
  188.6 0.1 copy.28
  188.7 0.1 reshape.147
  188.8 0.0 copy-start.1
  188.8 0.4 multiply_reduce_fusion.2
  189.2 0.6 copy-done.1
  189.8 0.4 multiply_reduce_fusion.3
  190.2 0.2 subtract_convert_fusion
  190.4 0.5 convolution_convert_fusion.1
  190.9 0.3 fusion.5
  191.2 0.5 convolution_convert_fusion.5
  191.7 0.3 fusion.4
  192.1 0.4 convolution_convert_fusion.3
  192.4 0.5 multiply_reduce_fusion
  192.9 0.3 multiply_reduce_fusion.1
  193.2 0.1 multiply_convert_fusion
  193.3 0.1 reshape.148
  193.4 0.8 copy.30
  194.2 6.5 %all-to-all-start.1 = ((bf16[2,64,4,256]{3,2,0,1:T(4,128)(2,1)}), bf16[2,64,4,256]{3,2,0,1:T(4,128)(2,1)S(1)}, u32[]{:S(2)}, u32[]{:S(2)}) async-start(bf16[2,64,4,256]{3,2,0,1:T(4,128)(2,1)} %copy.30), calls=%async_computation.1 | async-start | bytes 524288 | tf_op jit(solution)/shard_map/all_to_all | solution.py:77
  200.7 0.0 all-gather.2.cloned.1.call-start
  200.8 11.4 %all-to-all-done.1 = bf16[2,64,4,256]{3,2,0,1:T(4,128)(2,1)S(1)} async-done(((bf16[2,64,4,256]{3,2,0,1:T(4,128)(2,1)}), bf16[2,64,4,256]{3,2,0,1:T(4,128)(2,1)S(1)}, u32[]{:S(2)}, u32[]{:S(2)}) %all-to-all-start.1) | async-done | bytes 262176 | tf_op jit(solution)/shard_map/all_to_all | solution.py:77
  212.2 0.1 copy.31
  212.3 0.6 gather_fusion.2
  212.9 0.8 select_select_fusion
  213.7 0.0 all-gather.2.cloned.1.call-update
  213.7 66.4 %all-gather.2.cloned.1.call-done = bf16[512,4,256]{2,1,0:T(4,128)(2,1)} async-done(((bf16[32,4,256]{2,1,0:T(4,128)(2,1)}), bf16[512,4,256]{2,1,0:T(4,128)(2,1)}) %all-gather.2.cloned.1.call-update) | async-done | bytes 1048592 | tf_op jit(solution)/shard_map/all_gather | solution.py:88
  280.2 2.6 copy.37
  (17 shorter events, 0.2 us)
Async XLA Ops:
  6.5 157.4 %all-reduce.3.cloned.1.call-start = ((), (), s32[]{:S(2)}) async-start(), calls=%async_computation.3 | async-start | bytes 2097152
  7.3 0.7 copy-start.3
  8.1 0.7 copy-start.2
  166.6 22.0 %all-to-all-start = ((bf16[2,64,4,256]{3,2,0,1:T(4,128)(2,1)}), bf16[2,64,4,256]{3,2,0,1:T(4,128)(2,1)S(1)}, u32[]{:S(2)}, u32[]{:S(2)}) async-start(bf16[2,64,4,256]{3,2,0,1:T(4,128)(2,1)} %copy_select_fusion), calls=%async_computation | async-start | bytes 524288 | tf_op jit(solution)/shard_map/all_to_all | solution.py:73
  177.1 11.7 %copy-start = (f32[2,256,256]{2,1,0:T(8,128)S(1)}, f32[2,256,256]{2,1,0:T(8,128)}, u32[]{:S(2)}) copy-start(f32[2,256,256]{2,1,0:T(8,128)} %param.9) | copy-start | bytes 1572868
  188.8 1.0 copy-start.1
  194.2 18.0 %all-to-all-start.1 = ((bf16[2,64,4,256]{3,2,0,1:T(4,128)(2,1)}), bf16[2,64,4,256]{3,2,0,1:T(4,128)(2,1)S(1)}, u32[]{:S(2)}, u32[]{:S(2)}) async-start(bf16[2,64,4,256]{3,2,0,1:T(4,128)(2,1)} %copy.30), calls=%async_computation.1 | async-start | bytes 524288 | tf_op jit(solution)/shard_map/all_to_all | solution.py:77
  200.7 79.5 %all-gather.2.cloned.1.call-start = ((), (), s32[]{:S(2)}) async-start(), calls=%async_computation.2 | async-start | bytes 1114112 | tf_op jit(solution)/shard_map/all_gather | solution.py:88
Sparse Core Ops, SparseCore 0:
  9.7 154.2 all-reduce.2
  213.9 66.2 all-gather.1
where the time goes:
time: 290 us
  waiting for transfers between devices  242 us (83%)
  starting transfers between devices  17 us (6%)
  between operations  14.3 us (5%)
  local copies, waits for them, and re-layouts  10.3 us (4%)
  matrix products  3.24 us (1%)
  other arithmetic  2.91 us (1%)
    unnamed x3, waiting for transfers between devices  153 us
    all_gather x1, waiting for transfers between devices, body(): return lax.all_gather(chosen, 'dp', axis=0, tiled=True)  66.4 us
    all_to_all x1, waiting for transfers between devices, body(): lax.all_to_all(outgoing, 'shard', split_axis=1, concat_axis=1, tiled=True)  11.5 us
    all_to_all x1, waiting for transfers between devices, body(): lax.all_to_all(fresh.reshape(CAP, owners, row_count, block_width), 'shard...  11.4 us
    all_to_all x1, starting transfers between devices, body(): lax.all_to_all(outgoing, 'shard', split_axis=1, concat_axis=1, tiled=True)  10.5 us
    unnamed x12, local copies, waits for them, and re-layouts  6.67 us
    all_to_all x1, starting transfers between devices, body(): lax.all_to_all(fresh.reshape(CAP, owners, row_count, block_width), 'shard...  6.46 us
  transfers between devices with their start and end apart: 4, of which 4 were waited for; matrix products, arithmetic and copies ran while one was open for 1% of the time, Pallas kernels for 0%

commit v1 on v0

--- a/solution.py
+++ b/solution.py
@@ -46,46 +46,76 @@
     return jax.vmap(precondition)(arrived, prev_left, prev_right)
 
 
+def shifted(value, step):
+    size = lax.axis_size("dp")
+    return lax.ppermute(value, "dp", [(i, (i + step) % size) for i in range(size)])
+
+
+def every_other(size):
+    return [list(range(start, size, 2)) for start in range(2)]
+
+
 def body(grads, owner_table, block_counts, prev_left, prev_right):
     owners = lax.axis_size("shard")
     groups = lax.axis_size("dp")
     my_group = lax.axis_index("dp")
+    parity = my_group % 2
     blocks = grads.shape[1]
     row_count = grads.shape[2]
     block_width = grads.shape[3]
     per_group = blocks // groups
+    half = per_group // 2
     slot_total = owners * CAP
     slot_ids = jnp.arange(slot_total, dtype=jnp.int32)
-    is_live = (slot_ids % CAP)[None, :] < block_counts[:, slot_ids // CAP]
+    my_table = lax.dynamic_index_in_dim(owner_table, my_group, 0, keepdims=False)
+    my_counts = lax.dynamic_index_in_dim(block_counts, my_group, 0, keepdims=False)
+    is_live = (slot_ids % CAP).reshape(owners, CAP) < my_counts[:, None]
+    is_live = is_live.reshape(slot_total)
     matches = (
-        owner_table[:, None, :] == jnp.arange(per_group, dtype=jnp.int32)[None, :, None]
-    ) & is_live[:, None, :]
-    earliest = jnp.min(jnp.where(matches, slot_ids[None, None, :], slot_total), axis=2)
+        my_table[None, :] == jnp.arange(per_group, dtype=jnp.int32)[:, None]
+    ) & is_live[None, :]
+    earliest = jnp.min(jnp.where(matches, slot_ids[None, :], slot_total), axis=1)
     has_slot = earliest < slot_total
     earliest = jnp.minimum(earliest, slot_total - 1)
-    pick_index = earliest % CAP * owners + earliest // CAP
-    local_terms = grads[0].astype(jnp.float32)
-    summed = lax.psum_scatter(
-        local_terms.astype(jnp.bfloat16), "dp", scatter_dimension=0, tiled=True
+
+    by_parity = grads.reshape(groups // 2, 2, per_group, row_count, block_width)
+    mine = lax.dynamic_index_in_dim(by_parity, parity, 1, keepdims=False)
+    other = lax.dynamic_index_in_dim(by_parity, 1 - parity, 1, keepdims=False)
+    from_above = shifted(other[:, :half], -1)
+    from_below = shifted(other[:, half:], 1)
+    paired = mine.astype(jnp.float32) + jnp.concatenate(
+        [from_above, from_below], axis=1
+    ).astype(jnp.float32)
+    parts = lax.all_to_all(
+        paired.astype(jnp.bfloat16),
+        "dp",
+        0,
+        0,
+        tiled=True,
+        axis_index_groups=every_other(groups),
     )
-    table_row = owner_table[my_group].reshape(owners, CAP).T
-    outgoing = jnp.take(summed, table_row, axis=0)
-    arrived = lax.all_to_all(outgoing, "shard", split_axis=1, concat_axis=1, tiled=True).reshape(
-        CAP, block_width, block_width
+    summed = jnp.sum(parts.astype(jnp.float32), axis=0).astype(jnp.bfloat16)
+    outgoing = jnp.take(summed, my_table, axis=0, mode="clip")
+    arrived = lax.all_to_all(
+        outgoing.reshape(owners, CAP, row_count, block_width), "shard", 0, 0, tiled=True
     )
+    arrived = jnp.swapaxes(arrived, 0, 1).reshape(CAP, block_width, block_width)
     fresh = refresh(arrived, prev_left, prev_right)
-    returned = lax.all_to_all(
-        fresh.reshape(CAP, owners, row_count, block_width),
-        "shard",
-        split_axis=1,
-        concat_axis=1,
-        tiled=True,
+    fresh = jnp.swapaxes(fresh.reshape(CAP, owners, row_count, block_width), 0, 1)
+    returned = lax.all_to_all(fresh, "shard", 0, 0, tiled=True)
+    chosen = jnp.take(
+        returned.reshape(slot_total, row_count, block_width), earliest, axis=0, mode="clip"
     )
-    chosen = jnp.take(
-        returned.reshape(CAP * owners, row_count, block_width), pick_index[my_group], axis=0
+    chosen = jnp.where(has_slot[:, None, None], chosen, jnp.zeros_like(chosen))
+    same = lax.all_gather(
+        chosen, "dp", axis=0, tiled=False, axis_index_groups=every_other(groups)
     )
-    chosen = jnp.where(has_slot[my_group][:, None, None], chosen, jnp.zeros_like(chosen))
-    return lax.all_gather(chosen, "dp", axis=0, tiled=True)
+    from_below = shifted(same[:, :half], 1)
+    from_above = shifted(same[:, half:], -1)
+    opposite = jnp.concatenate([from_below, from_above], axis=1)
+    even = jnp.where(parity == 0, same, opposite)
+    odd = jnp.where(parity == 0, opposite, same)
+    return jnp.stack([even, odd], axis=1).reshape(blocks, row_count, block_width)
 
 
 def solution(mesh):

time: 290 us -> 158 us (0.54)
  waiting for transfers between devices: 242 us -> 64.8 us
  starting transfers between devices: 17 us -> 48 us
  blocking collectives: 0 us -> 29.7 us
  between operations: 14.3 us -> 0.31 us
    unnamed x3 -> x0, waiting for transfers between devices: 153 us -> none
    all_gather x1 -> x0, waiting for transfers between devices: 66.4 us -> none  [body(): return lax.all_gather(chosen, 'dp', axis=0, tiled=True)]
    all_gather x0 -> x1, blocking collectives: none -> 29.7 us  [body(): lax.all_gather(chosen, 'dp', axis=0, tiled=False, axis_index_groups=every...]
    all_to_all x2 -> x3, waiting for transfers between devices: 22.9 us -> 51.8 us  [the longest x1 29.9 us: body(): lax.all_to_all(paired.astype(jnp.bfloat16), 'dp', 0, 0, tiled=True, axis_...]
    ppermute x0 -> x4, starting transfers between devices: none -> 27.2 us  [shifted(): lax.ppermute(value, 'dp', [(i, (i + step) % size) for i in range(size)])]
    ppermute x0 -> x4, waiting for transfers between devices: none -> 12.9 us  [shifted(): lax.ppermute(value, 'dp', [(i, (i + step) % size) for i in range(size)])]
    unnamed x12 -> x11, local copies, waits for them, and re-layouts: 6.67 us -> 1.6 us
    all_to_all x2 -> x3, starting transfers between devices: 16.9 us -> 20.8 us  [the longest x1 10.8 us: body(): lax.all_to_all(outgoing.reshape(owners, CAP, row_count, block_width), 'sh...]
  transfers between devices with their start and end apart: 4 -> 7, of which waited for: 4 -> 7; matrix products, arithmetic and copies ran while one was open for 1% -> 1% of each run, Pallas kernels for 0% -> 0%
where the time goes in v1:
time: 158 us; the launch traced here: 157 us
  waiting for transfers between devices  64.8 us (41%)
  starting transfers between devices  48 us (30%)
  blocking collectives  29.7 us (19%)
  local copies, waits for them, and re-layouts  9.06 us (6%)
  matrix products  3.24 us (2%)
  other arithmetic  2.46 us (2%)
    all_to_all x1, waiting for transfers between devices, body(): lax.all_to_all(paired.astype(jnp.bfloat16), 'dp', 0, 0, tiled=True, axis_...  29.9 us
    all_gather x1, blocking collectives, body(): lax.all_gather(chosen, 'dp', axis=0, tiled=False, axis_index_groups=every...  29.7 us
    ppermute x4, starting transfers between devices, shifted(): lax.ppermute(value, 'dp', [(i, (i + step) % size) for i in range(size)])  27.2 us
    ppermute x4, waiting for transfers between devices, shifted(): lax.ppermute(value, 'dp', [(i, (i + step) % size) for i in range(size)])  12.9 us
    all_to_all x1, waiting for transfers between devices, body(): returned = lax.all_to_all(fresh, 'shard', 0, 0, tiled=True)  11.5 us
    all_to_all x1, starting transfers between devices, body(): lax.all_to_all(outgoing.reshape(owners, CAP, row_count, block_width), 'sh...  10.8 us
    all_to_all x1, waiting for transfers between devices, body(): lax.all_to_all(outgoing.reshape(owners, CAP, row_count, block_width), 'sh...  10.5 us
    all_to_all x1, starting transfers between devices, body(): returned = lax.all_to_all(fresh, 'shard', 0, 0, tiled=True)  6.46 us
  transfers between devices with their start and end apart: 7, of which 7 were waited for; matrix products, arithmetic and copies ran while one was open for 1% of the time, Pallas kernels for 0%

profile of v1, /device:TPU:6, one launch (start us, length us, event | category | flops | bytes accessed | tf_op | source)
XLA Modules:
  0.0 157.5 jit_solution(16029165565823319304)
XLA Ops:
  0.0 0.0 copy-start
  0.0 1.3 dynamic-slice_bitcast_fusion
  1.3 0.2 fusion.16
  1.5 18.2 %collective-permute-start = (bf16[8,16,4,256]{3,2,1,0:T(4,128)(2,1)S(1)}, bf16[8,16,4,256]{3,2,1,0:T(4,128)(2,1)S(1)}, u32[]{:S(2)}, u32[]{:S(2)}) collective-permute-start(bf16[8,16,4,256]{3,2,1,0:T(4,128)(2,1)S(1)} %get-tuple-element.9), channel_id=1, source_target_pairs={{0,960},{64,0},{128,64},{192,128},{256,192},{320,256},{384,320},{4... | collective-permute-start | bytes 786440 | tf_op jit(solution)/shard_map/ppermute | solution.py:51
  19.8 1.9 %collective-permute-start.1 = (bf16[8,16,4,256]{3,2,1,0:T(4,128)(2,1)S(1)}, bf16[8,16,4,256]{3,2,1,0:T(4,128)(2,1)S(1)}, u32[]{:S(2)}, u32[]{:S(2)}) collective-permute-start(bf16[8,16,4,256]{3,2,1,0:T(4,128)(2,1)S(1)} %get-tuple-element.10), channel_id=1, source_target_pairs={{0,64},{64,128},{128,192},{192,256},{256,320},{320,384},{384,448},... | collective-permute-start | bytes 786440 | tf_op jit(solution)/shard_map/ppermute | solution.py:51
  21.7 3.6 %collective-permute-done = bf16[8,16,4,256]{3,2,1,0:T(4,128)(2,1)S(1)} collective-permute-done((bf16[8,16,4,256]{3,2,1,0:T(4,128)(2,1)S(1)}, bf16[8,16,4,256]{3,2,1,0:T(4,128)(2,1)S(1)}, u32[]{:S(2)}, u32[]{:S(2)}) %collective-permute-start) | collective-permute-done | bytes 262176 | tf_op jit(solution)/shard_map/ppermute | solution.py:51
  25.3 5.3 %collective-permute-done.1 = bf16[8,16,4,256]{3,2,1,0:T(4,128)(2,1)S(1)} collective-permute-done((bf16[8,16,4,256]{3,2,1,0:T(4,128)(2,1)S(1)}, bf16[8,16,4,256]{3,2,1,0:T(4,128)(2,1)S(1)}, u32[]{:S(2)}, u32[]{:S(2)}) %collective-permute-start.1) | collective-permute-done | bytes 262176 | tf_op jit(solution)/shard_map/ppermute | solution.py:51
  30.6 0.0 copy-done.1
  30.6 1.1 fusion.7
  31.8 3.5 %all-to-all-start = ((bf16[8,32,4,256]{3,2,1,0:T(4,128)(2,1)}), bf16[8,32,4,256]{3,2,1,0:T(4,128)(2,1)S(1)}, u32[]{:S(2)}, u32[]{:S(2)}) async-start(bf16[8,32,4,256]{3,2,1,0:T(4,128)(2,1)} %fusion.7), calls=%async_computation | async-start | bytes 1048576 | tf_op jit(solution)/shard_map/all_to_all | solution.py:89
  35.3 29.9 %all-to-all-done = bf16[8,32,4,256]{3,2,1,0:T(4,128)(2,1)S(1)} async-done(((bf16[8,32,4,256]{3,2,1,0:T(4,128)(2,1)}), bf16[8,32,4,256]{3,2,1,0:T(4,128)(2,1)S(1)}, u32[]{:S(2)}, u32[]{:S(2)}) %all-to-all-start) | async-done | bytes 524320 | tf_op jit(solution)/shard_map/all_to_all | solution.py:89
  65.2 0.3 reduce_sum.48
  65.4 1.5 gather_fusion
  67.0 10.8 %all-to-all-start.1 = ((bf16[64,2,4,256]{3,2,1,0:T(4,128)(2,1)}), bf16[64,2,4,256]{3,2,1,0:T(4,128)(2,1)S(1)}, u32[]{:S(2)}, u32[]{:S(2)}) async-start(bf16[64,2,4,256]{3,2,1,0:T(4,128)(2,1)} %bitcast.5), calls=%async_computation.1 | async-start | bytes 524288 | tf_op jit(solution)/shard_map/all_to_all | solution.py:99
  77.8 0.7 fusion.14
  78.5 0.1 lt.52
  78.6 0.1 lt.53
  78.7 0.1 select_reduce_fusion
  78.9 10.5 %all-to-all-done.1 = bf16[64,2,4,256]{3,2,1,0:T(4,128)(2,1)S(1)} async-done(((bf16[64,2,4,256]{3,2,1,0:T(4,128)(2,1)}), bf16[64,2,4,256]{3,2,1,0:T(4,128)(2,1)S(1)}, u32[]{:S(2)}, u32[]{:S(2)}) %all-to-all-start.1) | async-done | bytes 262176 | tf_op jit(solution)/shard_map/all_to_all | solution.py:99
  89.3 0.1 copy.26
  89.4 0.1 reshape.93
  89.5 0.9 copy-done.2
  90.4 0.4 multiply_reduce_fusion.2
  90.7 0.7 copy-done.3
  91.4 0.4 multiply_reduce_fusion.3
  91.8 0.2 subtract_convert_fusion
  92.0 0.5 convolution_convert_fusion.1
  92.5 0.3 fusion.5
  92.8 0.5 convolution_convert_fusion.5
  93.3 0.3 fusion.4
  93.7 0.4 convolution_convert_fusion.3
  94.0 0.5 multiply_reduce_fusion
  94.5 0.3 multiply_reduce_fusion.1
  94.8 0.1 multiply_convert_fusion
  94.9 0.1 reshape.94
  95.0 0.8 copy.42
  95.8 6.5 %all-to-all-start.2 = ((bf16[64,2,4,256]{3,2,1,0:T(4,128)(2,1)}), bf16[64,2,4,256]{3,2,1,0:T(4,128)(2,1)S(1)}, u32[]{:S(2)}, u32[]{:S(2)}) async-start(bf16[64,2,4,256]{3,2,1,0:T(4,128)(2,1)} %bitcast.41), calls=%async_computation.2 | async-start | bytes 524288 | tf_op jit(solution)/shard_map/all_to_all | solution.py:105
  102.3 11.5 %all-to-all-done.2 = bf16[64,2,4,256]{3,2,1,0:T(4,128)(2,1)S(1)} async-done(((bf16[64,2,4,256]{3,2,1,0:T(4,128)(2,1)}), bf16[64,2,4,256]{3,2,1,0:T(4,128)(2,1)S(1)}, u32[]{:S(2)}, u32[]{:S(2)}) %all-to-all-start.2) | async-done | bytes 262176 | tf_op jit(solution)/shard_map/all_to_all | solution.py:105
  113.8 0.6 gather_fusion.1
  114.4 0.1 bitcast_select_fusion
  114.6 29.7 %all_gather.4 = bf16[8,32,4,256]{3,1,2,0:T(8,128)(2,1)S(1)} all-gather(bf16[1,32,4,256]{3,1,2,0:T(8,128)(2,1)S(1)} %copy.29), channel_id=1, replica_groups={{0,128,256,384,512,640,768,896},{64,192,320,448,576,704,832,960},{1,129..., dimensions={0}, use_global_device_ids=true | all-gather | bytes 589824 | tf_op jit(solution)/shard_map/all_gather | solution.py:110
  144.3 1.9 %collective-permute-start.2 = (bf16[8,16,4,256]{3,1,0,2:T(8,128)(2,1)S(1)}, bf16[8,16,4,256]{3,1,0,2:T(8,128)(2,1)S(1)}, u32[]{:S(2)}, u32[]{:S(2)}) collective-permute-start(bf16[8,16,4,256]{3,1,0,2:T(8,128)(2,1)S(1)} %copy.40), channel_id=1, source_target_pairs={{0,64},{64,128},{128,192},{192,256},{256,320},{320,384},{384,448},... | collective-permute-start | bytes 786440 | tf_op jit(solution)/shard_map/ppermute | solution.py:51
  146.3 5.1 %collective-permute-start.3 = (bf16[8,16,4,256]{3,1,0,2:T(8,128)(2,1)S(1)}, bf16[8,16,4,256]{3,1,0,2:T(8,128)(2,1)S(1)}, u32[]{:S(2)}, u32[]{:S(2)}) collective-permute-start(bf16[8,16,4,256]{3,1,0,2:T(8,128)(2,1)S(1)} %copy.41), channel_id=1, source_target_pairs={{0,960},{64,0},{128,64},{192,128},{256,192},{320,256},{384,320},{4... | collective-permute-start | bytes 786440 | tf_op jit(solution)/shard_map/ppermute | solution.py:51
  151.4 2.4 %collective-permute-done.2 = bf16[8,16,4,256]{3,1,0,2:T(8,128)(2,1)S(1)} collective-permute-done((bf16[8,16,4,256]{3,1,0,2:T(8,128)(2,1)S(1)}, bf16[8,16,4,256]{3,1,0,2:T(8,128)(2,1)S(1)}, u32[]{:S(2)}, u32[]{:S(2)}) %collective-permute-start.2) | collective-permute-done | bytes 262176 | tf_op jit(solution)/shard_map/ppermute | solution.py:51
  153.8 1.6 %collective-permute-done.3 = bf16[8,16,4,256]{3,1,0,2:T(8,128)(2,1)S(1)} collective-permute-done((bf16[8,16,4,256]{3,1,0,2:T(8,128)(2,1)S(1)}, bf16[8,16,4,256]{3,1,0,2:T(8,128)(2,1)S(1)}, u32[]{:S(2)}, u32[]{:S(2)}) %collective-permute-start.3) | collective-permute-done | bytes 262176 | tf_op jit(solution)/shard_map/ppermute | solution.py:51
  155.5 0.1 select_bitcast_fusion.1
  155.6 0.1 pad_maximum_fusion
  155.7 1.8 %copy.35 = bf16[512,4,256]{2,1,0:T(4,128)(2,1)} copy(bf16[512,4,256]{2,0,1:T(8,128)(2,1)S(1)} %bitcast.42) | data formatting | bytes 2097152 | tf_op jit(solution)/shard_map/reshape | solution.py:118
  (19 shorter events, 0.2 us)
Async XLA Ops:
  0.0 35.3 %copy-start = (s32[16,128]{1,0:T(8,128)S(1)}, s32[16,128]{1,0:T(8,128)}, u32[]{:S(2)}) copy-start(s32[16,128]{1,0:T(8,128)} %param.6) | copy-start | bytes 24580
  0.0 30.6 %copy-start.1 = (bf16[1,512,4,256]{3,2,1,0:T(4,128)(2,1)S(1)}, bf16[1,512,4,256]{3,2,1,0:T(4,128)(2,1)}, u32[]{:S(2)}) copy-start(bf16[1,512,4,256]{3,2,1,0:T(4,128)(2,1)} %param.5) | copy-start | bytes 3145732
  1.5 23.8 %collective-permute-start = (bf16[8,16,4,256]{3,2,1,0:T(4,128)(2,1)S(1)}, bf16[8,16,4,256]{3,2,1,0:T(4,128)(2,1)S(1)}, u32[]{:S(2)}, u32[]{:S(2)}) collective-permute-start(bf16[8,16,4,256]{3,2,1,0:T(4,128)(2,1)S(1)} %get-tuple-element.9), channel_id=1, source_target_pairs={{0,960},{64,0},{128,64},{192,128},{256,192},{320,256},{384,320},{4... | collective-permute-start | bytes 786440 | tf_op jit(solution)/shard_map/ppermute | solution.py:51
  19.8 10.9 %collective-permute-start.1 = (bf16[8,16,4,256]{3,2,1,0:T(4,128)(2,1)S(1)}, bf16[8,16,4,256]{3,2,1,0:T(4,128)(2,1)S(1)}, u32[]{:S(2)}, u32[]{:S(2)}) collective-permute-start(bf16[8,16,4,256]{3,2,1,0:T(4,128)(2,1)S(1)} %get-tuple-element.10), channel_id=1, source_target_pairs={{0,64},{64,128},{128,192},{192,256},{256,320},{320,384},{384,448},... | collective-permute-start | bytes 786440 | tf_op jit(solution)/shard_map/ppermute | solution.py:51
  31.8 33.4 %all-to-all-start = ((bf16[8,32,4,256]{3,2,1,0:T(4,128)(2,1)}), bf16[8,32,4,256]{3,2,1,0:T(4,128)(2,1)S(1)}, u32[]{:S(2)}, u32[]{:S(2)}) async-start(bf16[8,32,4,256]{3,2,1,0:T(4,128)(2,1)} %fusion.7), calls=%async_computation | async-start | bytes 1048576 | tf_op jit(solution)/shard_map/all_to_all | solution.py:89
  67.0 22.3 %all-to-all-start.1 = ((bf16[64,2,4,256]{3,2,1,0:T(4,128)(2,1)}), bf16[64,2,4,256]{3,2,1,0:T(4,128)(2,1)S(1)}, u32[]{:S(2)}, u32[]{:S(2)}) async-start(bf16[64,2,4,256]{3,2,1,0:T(4,128)(2,1)} %bitcast.5), calls=%async_computation.1 | async-start | bytes 524288 | tf_op jit(solution)/shard_map/all_to_all | solution.py:99
  89.3 1.0 copy-start.2
  90.4 1.0 copy-start.3
  95.8 18.0 %all-to-all-start.2 = ((bf16[64,2,4,256]{3,2,1,0:T(4,128)(2,1)}), bf16[64,2,4,256]{3,2,1,0:T(4,128)(2,1)S(1)}, u32[]{:S(2)}, u32[]{:S(2)}) async-start(bf16[64,2,4,256]{3,2,1,0:T(4,128)(2,1)} %bitcast.41), calls=%async_computation.2 | async-start | bytes 524288 | tf_op jit(solution)/shard_map/all_to_all | solution.py:105
  144.3 9.5 %collective-permute-start.2 = (bf16[8,16,4,256]{3,1,0,2:T(8,128)(2,1)S(1)}, bf16[8,16,4,256]{3,1,0,2:T(8,128)(2,1)S(1)}, u32[]{:S(2)}, u32[]{:S(2)}) collective-permute-start(bf16[8,16,4,256]{3,1,0,2:T(8,128)(2,1)S(1)} %copy.40), channel_id=1, source_target_pairs={{0,64},{64,128},{128,192},{192,256},{256,320},{320,384},{384,448},... | collective-permute-start | bytes 786440 | tf_op jit(solution)/shard_map/ppermute | solution.py:51
  146.3 9.2 %collective-permute-start.3 = (bf16[8,16,4,256]{3,1,0,2:T(8,128)(2,1)S(1)}, bf16[8,16,4,256]{3,1,0,2:T(8,128)(2,1)S(1)}, u32[]{:S(2)}, u32[]{:S(2)}) collective-permute-start(bf16[8,16,4,256]{3,1,0,2:T(8,128)(2,1)S(1)} %copy.41), channel_id=1, source_target_pairs={{0,960},{64,0},{128,64},{192,128},{256,192},{320,256},{384,320},{4... | collective-permute-start | bytes 786440 | tf_op jit(solution)/shard_map/ppermute | solution.py:51

commit v2 on v1

v2 whole, which is shorter than its diff:
```python
import jax
import jax.numpy as jnp
from jax import lax
from jax.experimental import pallas as pl
from jax.experimental.pallas import tpu as pltpu
from jax.sharding import PartitionSpec as P

CAP = 2
VMEM_GRANT = 12 * 1024 * 1024


stat_decay = 0.9
eps_small = 1e-06

ROWS_ROWS = (((1,), (1,)), ((), ()))
COLS_COLS = (((0,), (0,)), ((), ()))


def product(left, right, dims=(((1,), (0,)), ((), ()))):
    return lax.dot_general(left, right, dims, preferred_element_type=jnp.float32)


def mean_square(value):
    return jnp.sum(value * value, keepdims=True) * (1.0 / value.size)


def refresh_kernel(arrived_ref, left_ref, right_ref, fresh_ref):
    count, size_now, _ = arrived_ref.shape
    rows = lax.broadcasted_iota(jnp.int32, (size_now, size_now), 0)
    cols = lax.broadcasted_iota(jnp.int32, (size_now, size_now), 1)
    diagonal = jnp.where(rows == cols, 1.25, 0.0).astype(jnp.float32)
    grads = [arrived_ref[slot] for slot in range(count)]
    factors = []
    for slot, grad in enumerate(grads):
        factors.append(
            left_ref[slot] + (1.0 - stat_decay) * product(grad, grad, ROWS_ROWS)
        )
        factors.append(
            right_ref[slot] + (1.0 - stat_decay) * product(grad, grad, COLS_COLS)
        )
    scales = [1.0 / (size_now * jnp.sqrt(mean_square(a) + eps_small)) for a in factors]
    starts = [a * s for a, s in zip(factors, scales)]
    firsts = [(diagonal - 0.25 * s).astype(jnp.bfloat16) for s in starts]
    starts = [s.astype(jnp.bfloat16) for s in starts]
    squares = [product(f, f).astype(jnp.bfloat16) for f in firsts]
    fourths = [product(s, s).astype(jnp.bfloat16) for s in squares]
    states = [product(f, s) for f, s in zip(fourths, starts)]
    seconds = [(diagonal - 0.25 * s).astype(jnp.bfloat16) for s in states]
    roots = [product(f, s).astype(jnp.bfloat16) for f, s in zip(firsts, seconds)]
    halves = [
        product(roots[2 * slot], grad).astype(jnp.bfloat16) for slot, grad in enumerate(grads)
    ]
    finals = [product(h, roots[2 * slot + 1]) for slot, h in enumerate(halves)]
    for slot, (grad, final) in enumerate(zip(grads, finals)):
        wide = grad.astype(jnp.float32)
        grad_norm = jnp.sqrt(mean_square(wide) + eps_small)
        cond_norm = jnp.sqrt(mean_square(final) + eps_small)
        fresh_ref[slot] = (final * (grad_norm / cond_norm)).astype(jnp.bfloat16)


def refresh(arrived, prev_left, prev_right):
    count, size_now, _ = arrived.shape
    return pl.pallas_call(
        refresh_kernel,
        out_shape=jax.ShapeDtypeStruct(arrived.shape, jnp.bfloat16),
        cost_estimate=pl.CostEstimate(
            flops=24 * count * size_now**3,
            bytes_accessed=12 * count * size_now**2,
            transcendentals=0,
        ),
        compiler_params=pltpu.CompilerParams(vmem_limit_bytes=VMEM_GRANT),
        name="refresh",
    )(arrived, prev_left, prev_right)


def part_kernel(parity_ref, grads_ref, mine_ref, first_ref, second_ref, sems):
    parity = parity_ref[0]
    half = first_ref.shape[0]
    copies = [
        pltpu.make_async_copy(grads_ref.at[:half, 1 - parity], first_ref, sems.at[0]),
        pltpu.make_async_copy(grads_ref.at[half:, 1 - parity], second_ref, sems.at[1]),
        pltpu.make_async_copy(grads_ref.at[:, parity], mine_ref, sems.at[2]),
    ]
    for copy in copies:
        copy.start()
    for copy in copies:
        copy.wait()


def part(parity, by_parity):
    count = by_parity.shape[0]
    pieces = [
        jax.ShapeDtypeStruct((size,) + by_parity.shape[2:], jnp.bfloat16)
        for size in (count, count // 2, count // 2)
    ]
    return pl.pallas_call(
        part_kernel,
        in_specs=[pl.BlockSpec(memory_space=pltpu.SMEM), pl.BlockSpec(memory_space=pltpu.HBM)],
        out_shape=pieces,
        out_specs=[pl.BlockSpec(memory_space=pltpu.VMEM)] * 3,
        scratch_shapes=[pltpu.SemaphoreType.DMA((3,))],
        compiler_params=pltpu.CompilerParams(vmem_limit_bytes=VMEM_GRANT),
        name="part",
    )(parity, by_parity)


def pair_kernel(mine_ref, first_ref, second_ref, out_ref, sum_ref, sems):
    half = first_ref.shape[0]
    copies = []
    for index in range(2 * half):
        came_ref = first_ref if index < half else second_ref
        sum_ref[index] = (
            mine_ref[index].astype(jnp.float32) + came_ref[index % half].astype(jnp.float32)
        ).astype(jnp.bfloat16)
        copies.append(
            pltpu.make_async_copy(sum_ref.at[index], out_ref.at[index], sems.at[index])
        )
        copies[-1].start()
    for copy in copies:
        copy.wait()


def pair(mine, first, second):
    return pl.pallas_call(
        pair_kernel,
        in_specs=[pl.BlockSpec(memory_space=pltpu.VMEM)] * 3,
        out_specs=pl.BlockSpec(memory_space=pl.ANY),
        out_shape=jax.ShapeDtypeStruct(mine.shape, jnp.bfloat16),
        scratch_shapes=[
            pltpu.VMEM(mine.shape, jnp.bfloat16),
            pltpu.SemaphoreType.DMA((mine.shape[0],)),
        ],
        compiler_params=pltpu.CompilerParams(vmem_limit_bytes=VMEM_GRANT),
        name="pair",
    )(mine, first, second)


def gather_rows_kernel(table_ref, parts_ref, out_ref, sum_ref):
    total = parts_ref[0].astype(jnp.float32)
    for part in range(1, parts_ref.shape[0]):
        total += parts_ref[part].astype(jnp.float32)
    sum_ref[...] = total.astype(jnp.bfloat16)

    def step(slot, carry):
        out_ref[slot] = sum_ref[table_ref[slot]]
        return carry

    lax.fori_loop(0, out_ref.shape[0], step, 0, unroll=8)


def sum_and_gather(table, parts):
    count = table.shape[0]
    return pl.pallas_call(
        gather_rows_kernel,
        in_specs=[
            pl.BlockSpec(memory_space=pltpu.SMEM),
            pl.BlockSpec(memory_space=pltpu.VMEM),
        ],
        out_shape=jax.ShapeDtypeStruct((count,) + parts.shape[2:], jnp.bfloat16),
        scratch_shapes=[pltpu.VMEM(parts.shape[1:], jnp.bfloat16)],
        compiler_params=pltpu.CompilerParams(vmem_limit_bytes=VMEM_GRANT),
        name="sum_and_gather",
    )(table, parts)


def choose_kernel(picks_ref, returned_ref, chosen_ref):
    for block in range(chosen_ref.shape[0]):
        pick = picks_ref[block]
        found = returned_ref[jnp.maximum(pick, 0)]
        chosen_ref[block] = jnp.where(pick >= 0, found, jnp.zeros_like(found))


def choose(picks, returned):
    return pl.pallas_call(
        choose_kernel,
        in_specs=[
            pl.BlockSpec(memory_space=pltpu.SMEM),
            pl.BlockSpec(memory_space=pltpu.VMEM),
        ],
        out_shape=jax.ShapeDtypeStruct(picks.shape + returned.shape[1:], jnp.bfloat16),
        compiler_params=pltpu.CompilerParams(vmem_limit_bytes=VMEM_GRANT),
        name="choose",
    )(picks, returned)


def place_kernel(parity_ref, same_ref, low_ref, high_ref, out_ref, sems):
    parity = parity_ref[0]
    half = low_ref.shape[0]
    copies = [
        pltpu.make_async_copy(same_ref, out_ref.at[:, parity], sems.at[0]),
        pltpu.make_async_copy(low_ref, out_ref.at[:half, 1 - parity], sems.at[1]),
        pltpu.make_async_copy(high_ref, out_ref.at[half:, 1 - parity], sems.at[2]),
    ]
    for copy in copies:
        copy.start()
    for copy in copies:
        copy.wait()


def place(parity, same, low, high):
    return pl.pallas_call(
        place_kernel,
        in_specs=[pl.BlockSpec(memory_space=pltpu.SMEM)]
        + [pl.BlockSpec(memory_space=pltpu.VMEM)] * 3,
        out_specs=pl.BlockSpec(memory_space=pl.ANY),
        out_shape=jax.ShapeDtypeStruct((same.shape[0], 2) + same.shape[1:], jnp.bfloat16),
        scratch_shapes=[pltpu.SemaphoreType.DMA((3,))],
        compiler_params=pltpu.CompilerParams(vmem_limit_bytes=VMEM_GRANT),
        name="place",
    )(parity, same, low, high)


def shifted(value, step):
    size = lax.axis_size("dp")
    return lax.ppermute(value, "dp", [(i, (i + step) % size) for i in range(size)])


def every_other(size):
    return [list(range(start, size, 2)) for start in range(2)]


def body(grads, owner_table, block_counts, prev_left, prev_right):
    owners = lax.axis_size("shard")
    groups = lax.axis_size("dp")
    my_group = lax.axis_index("dp")
    parity = my_group % 2
    blocks = grads.shape[1]
    row_count = grads.shape[2]
    block_width = grads.shape[3]
    per_group = blocks // groups
    half = groups // 4
    slot_total = owners * CAP
    slot_ids = jnp.arange(slot_total, dtype=jnp.int32)
    my_table = lax.dynamic_index_in_dim(owner_table, my_group, 0, keepdims=False)
    my_counts = lax.dynamic_index_in_dim(block_counts, my_group, 0, keepdims=False)
    is_live = (slot_ids % CAP).reshape(owners, CAP) < my_counts[:, None]
    is_live = is_live.reshape(slot_total)
    matches = (
        my_table[None, :] == jnp.arange(per_group, dtype=jnp.int32)[:, None]
    ) & is_live[None, :]
    earliest = jnp.min(jnp.where(matches, slot_ids[None, :], slot_total), axis=1)
    picks = jnp.where(earliest < slot_total, earliest, -1)

    by_parity = grads.reshape(groups // 2, 2, per_group, row_count, block_width)
    mine, first, second = part(parity.reshape(1), by_parity)
    paired = pair(mine, shifted(first, -1), shifted(second, 1))
    parts = lax.all_to_all(
        paired,
        "dp",
        0,
        0,
        tiled=True,
        axis_index_groups=every_other(groups),
    )
    outgoing = sum_and_gather(my_table, parts)
    arrived = lax.all_to_all(
        outgoing.reshape(owners, CAP, row_count, block_width), "shard", 0, 0, tiled=True
    )
    arrived = jnp.swapaxes(arrived, 0, 1).reshape(CAP, block_width, block_width)
    fresh = refresh(arrived, stat_decay * prev_left, stat_decay * prev_right)
    fresh = jnp.swapaxes(fresh.reshape(CAP, owners, row_count, block_width), 0, 1)
    returned = lax.all_to_all(fresh, "shard", 0, 0, tiled=True)
    chosen = choose(picks, returned.reshape(slot_total, row_count, block_width))
    same = lax.all_gather(
        chosen, "dp", axis=0, tiled=False, axis_index_groups=every_other(groups)
    )
    low = shifted(same[:half], 1)
    high = shifted(same[half:], -1)
    placed = place(parity.reshape(1), same, low, high)
    return placed.reshape(blocks, row_count, block_width)


def solution(mesh):
    return jax.shard_map(
        body,
        mesh=mesh,
        in_specs=(
            P("dp", None, "shard", None),
            P(),
            P(),
            P(("dp", "shard"), None, None),
            P(("dp", "shard"), None, None),
        ),
        out_specs=P(None, "shard", None),
        check_vma=False,
    )
```

time: 158 us -> 153 us (0.968)
  Pallas kernels: 0 us -> 5.88 us
  local copies, waits for them, and re-layouts: 9.06 us -> 3.38 us
  matrix products: 3.24 us -> 0 us
  other arithmetic: 2.46 us -> 0.22 us
    pallas_call x0 -> x6, Pallas kernels: none -> 5.88 us  [the longest x1 1.76 us: refresh(): pl.pallas_call(refresh_kernel, out_shape=jax.ShapeDtypeStruct(arrived.sha...]
    dot_general x8 -> x0, matrix products: 3.24 us -> none  [the longest x2 0.99 us: inverse_root(): jnp.dot(square, square, preferred_element_type=jnp.float32)]
    gather x2 -> x0, local copies, waits for them, and re-layouts: 2.14 us -> none  [the longest x1 1.52 us: body(): outgoing = jnp.take(summed, my_table, axis=0, mode='clip')]
    reshape x1 -> x0, local copies, waits for them, and re-layouts: 1.78 us -> none  [body(): jnp.stack([even, odd], axis=1).reshape(blocks, row_count, block_width)]
where the time goes in v2:
time: 153 us; the launch traced here: 152 us
  waiting for transfers between devices  64.7 us (42%)
  starting transfers between devices  48 us (31%)
  blocking collectives  29.6 us (19%)
  Pallas kernels  5.88 us (4%)
  local copies, waits for them, and re-layouts  3.38 us (2%)
    all_to_all x1, waiting for transfers between devices, body(): lax.all_to_all(paired, 'dp', 0, 0, tiled=True, axis_index_groups=every_ot...  29.9 us
    all_gather x1, blocking collectives, body(): lax.all_gather(chosen, 'dp', axis=0, tiled=False, axis_index_groups=every...  29.6 us
    ppermute x4, starting transfers between devices, shifted(): lax.ppermute(value, 'dp', [(i, (i + step) % size) for i in range(size)])  27.2 us
    ppermute x4, waiting for transfers between devices, shifted(): lax.ppermute(value, 'dp', [(i, (i + step) % size) for i in range(size)])  13 us
    all_to_all x1, waiting for transfers between devices, body(): returned = lax.all_to_all(fresh, 'shard', 0, 0, tiled=True)  11.4 us
    all_to_all x1, starting transfers between devices, body(): lax.all_to_all(outgoing.reshape(owners, CAP, row_count, block_width), 'sh...  10.8 us
    all_to_all x1, waiting for transfers between devices, body(): lax.all_to_all(outgoing.reshape(owners, CAP, row_count, block_width), 'sh...  10.5 us
    all_to_all x1, starting transfers between devices, body(): returned = lax.all_to_all(fresh, 'shard', 0, 0, tiled=True)  6.46 us
  transfers between devices with their start and end apart: 7, of which 7 were waited for; matrix products, arithmetic and copies ran while one was open for 1% of the time, Pallas kernels for 0%

profile of v2, /device:TPU:6, one launch (start us, length us, event | category | flops | bytes accessed | tf_op | source)
XLA Modules:
  0.0 152.0 jit_solution(11405830286864731507)
XLA Ops:
  0.0 0.0 copy-start
  0.0 0.0 copy-start.1
  0.0 1.2 copy-done.1
  1.2 0.1 part.1
  1.4 18.2 %collective-permute-start = (bf16[4,32,4,256]{3,2,1,0:T(4,128)(2,1)S(1)}, bf16[4,32,4,256]{3,2,1,0:T(4,128)(2,1)S(1)}, u32[]{:S(2)}, u32[]{:S(2)}) collective-permute-start(bf16[4,32,4,256]{3,2,1,0:T(4,128)(2,1)S(1)} %get-tuple-element.9), channel_id=1, source_target_pairs={{0,960},{64,0},{128,64},{192,128},{256,192},{320,256},{384,320},{4... | collective-permute-start | bytes 786440 | tf_op jit(solution)/shard_map/ppermute | solution.py:215
  19.6 1.9 %collective-permute-start.1 = (bf16[4,32,4,256]{3,2,1,0:T(4,128)(2,1)S(1)}, bf16[4,32,4,256]{3,2,1,0:T(4,128)(2,1)S(1)}, u32[]{:S(2)}, u32[]{:S(2)}) collective-permute-start(bf16[4,32,4,256]{3,2,1,0:T(4,128)(2,1)S(1)} %get-tuple-element.10), channel_id=1, source_target_pairs={{0,64},{64,128},{128,192},{192,256},{256,320},{320,384},{384,448},... | collective-permute-start | bytes 786440 | tf_op jit(solution)/shard_map/ppermute | solution.py:215
  21.5 3.6 %collective-permute-done.first_ref = bf16[4,32,4,256]{3,2,1,0:T(4,128)(2,1)S(1)} collective-permute-done((bf16[4,32,4,256]{3,2,1,0:T(4,128)(2,1)S(1)}, bf16[4,32,4,256]{3,2,1,0:T(4,128)(2,1)S(1)}, u32[]{:S(2)}, u32[]{:S(2)}) %collective-permute-start) | collective-permute-done | bytes 262176 | tf_op jit(solution)/shard_map/ppermute | solution.py:215
  25.1 5.3 %collective-permute-done.1.second_ref = bf16[4,32,4,256]{3,2,1,0:T(4,128)(2,1)S(1)} collective-permute-done((bf16[4,32,4,256]{3,2,1,0:T(4,128)(2,1)S(1)}, bf16[4,32,4,256]{3,2,1,0:T(4,128)(2,1)S(1)}, u32[]{:S(2)}, u32[]{:S(2)}) %collective-permute-start.1) | collective-permute-done | bytes 262176 | tf_op jit(solution)/shard_map/ppermute | solution.py:215
  30.5 0.9 pair.1
  31.3 3.5 %all-to-all-start = ((bf16[8,32,4,256]{3,2,1,0:T(4,128)(2,1)}), bf16[8,32,4,256]{3,2,1,0:T(4,128)(2,1)S(1)}, u32[]{:S(2)}, u32[]{:S(2)}) async-start(bf16[8,32,4,256]{3,2,1,0:T(4,128)(2,1)} %pair.1), calls=%async_computation | async-start | bytes 1048576 | tf_op jit(solution)/shard_map/all_to_all | solution.py:247
  34.8 0.0 copy-done
  34.9 0.0 copy-start.2
  34.9 0.0 copy-start.3
  34.9 29.9 %all-to-all-done.parts_ref = bf16[8,32,4,256]{3,2,1,0:T(4,128)(2,1)S(1)} async-done(((bf16[8,32,4,256]{3,2,1,0:T(4,128)(2,1)}), bf16[8,32,4,256]{3,2,1,0:T(4,128)(2,1)S(1)}, u32[]{:S(2)}, u32[]{:S(2)}) %all-to-all-start) | async-done | bytes 524320 | tf_op jit(solution)/shard_map/all_to_all | solution.py:247
  64.8 1.5 %sum_and_gather.1 = bf16[128,4,256]{2,1,0:T(4,128)(2,1)} custom-call(s32[128]{0:T(128)S(1)} %dynamic-slice_bitcast_fusion.1.table_ref, bf16[8,32,4,256]{3,2,1,0:T(4,128)(2,1)S(1)} %all-to-all-done.parts_ref), custom_call_target="tpu_custom_call" | custom-call | tf_op jit(solution)/shard_map/sum_and_gather/pallas_call | solution.py:153
  66.3 10.8 %all-to-all-start.1 = ((bf16[64,2,4,256]{3,2,1,0:T(4,128)(2,1)}), bf16[64,2,4,256]{3,2,1,0:T(4,128)(2,1)S(1)}, u32[]{:S(2)}, u32[]{:S(2)}) async-start(bf16[64,2,4,256]{3,2,1,0:T(4,128)(2,1)} %bitcast.4), calls=%async_computation.1 | async-start | bytes 524288 | tf_op jit(solution)/shard_map/all_to_all | solution.py:256
  77.1 0.7 dynamic-slice_bitcast_fusion
  77.8 0.1 lt.41
  77.9 0.1 lt.42
  78.0 0.0 copy-done.2
  78.0 0.0 copy-done.3
  78.1 0.1 broadcast_multiply_fusion
  78.2 10.5 %all-to-all-done.1 = bf16[64,2,4,256]{3,2,1,0:T(4,128)(2,1)S(1)} async-done(((bf16[64,2,4,256]{3,2,1,0:T(4,128)(2,1)}), bf16[64,2,4,256]{3,2,1,0:T(4,128)(2,1)S(1)}, u32[]{:S(2)}, u32[]{:S(2)}) %all-to-all-start.1) | async-done | bytes 262176 | tf_op jit(solution)/shard_map/all_to_all | solution.py:256
  88.7 0.1 copy.12
  88.8 0.1 reshape.45.arrived_ref
  88.8 1.8 %refresh.1 = bf16[2,256,256]{2,1,0:T(8,128)(2,1)S(1)} custom-call(bf16[2,256,256]{2,1,0:T(8,128)(2,1)S(1)} %reshape.45.arrived_ref, f32[2,256,256]{2,1,0:T(8,128)S(1)} %get-tuple-element.14.left_ref, f32[2,256,256]{2,1,0:T(8,128)S(1)} %get-tuple-element.13.right_ref), custom_call_target="tpu_custom_call" | custom-call | flops 805306368 | bytes 1572864 | tf_op jit(solution)/shard_map/refresh/pallas_call | solution.py:63
  90.6 0.1 reshape.46
  90.7 0.8 copy.15
  91.5 6.5 %all-to-all-start.2 = ((bf16[64,2,4,256]{3,2,1,0:T(4,128)(2,1)}), bf16[64,2,4,256]{3,2,1,0:T(4,128)(2,1)S(1)}, u32[]{:S(2)}, u32[]{:S(2)}) async-start(bf16[64,2,4,256]{3,2,1,0:T(4,128)(2,1)} %bitcast.15), calls=%async_computation.2 | async-start | bytes 524288 | tf_op jit(solution)/shard_map/all_to_all | solution.py:262
  97.9 0.1 select_reduce_fusion
  98.1 11.4 %all-to-all-done.2 = bf16[64,2,4,256]{3,2,1,0:T(4,128)(2,1)S(1)} async-done(((bf16[64,2,4,256]{3,2,1,0:T(4,128)(2,1)}), bf16[64,2,4,256]{3,2,1,0:T(4,128)(2,1)S(1)}, u32[]{:S(2)}, u32[]{:S(2)}) %all-to-all-start.2) | async-done | bytes 262176 | tf_op jit(solution)/shard_map/all_to_all | solution.py:262
  109.5 0.6 choose.1
  110.1 29.6 %all-gather = bf16[256,4,256]{2,1,0:T(4,128)(2,1)S(1)} all-gather(bf16[32,4,256]{2,1,0:T(4,128)(2,1)S(1)} %choose.1), channel_id=2, replica_groups={{0,128,256,384,512,640,768,896},{64,192,320,448,576,704,832,960},{1,129..., dimensions={0}, use_global_device_ids=true | all-gather | bytes 589824 | tf_op jit(solution)/shard_map/all_gather | solution.py:264
  139.7 0.2 fusion.2
  139.9 1.9 %collective-permute-start.2 = (bf16[4,32,4,256]{3,2,1,0:T(4,128)(2,1)S(1)}, bf16[4,32,4,256]{3,2,1,0:T(4,128)(2,1)S(1)}, u32[]{:S(2)}, u32[]{:S(2)}) collective-permute-start(bf16[4,32,4,256]{3,2,1,0:T(4,128)(2,1)S(1)} %bitcast.21), channel_id=1, source_target_pairs={{0,64},{64,128},{128,192},{192,256},{256,320},{320,384},{384,448},... | collective-permute-start | bytes 786440 | tf_op jit(solution)/shard_map/ppermute | solution.py:215
  141.8 5.1 %collective-permute-start.3 = (bf16[4,32,4,256]{3,2,1,0:T(4,128)(2,1)S(1)}, bf16[4,32,4,256]{3,2,1,0:T(4,128)(2,1)S(1)}, u32[]{:S(2)}, u32[]{:S(2)}) collective-permute-start(bf16[4,32,4,256]{3,2,1,0:T(4,128)(2,1)S(1)} %bitcast.20), channel_id=1, source_target_pairs={{0,960},{64,0},{128,64},{192,128},{256,192},{320,256},{384,320},{4... | collective-permute-start | bytes 786440 | tf_op jit(solution)/shard_map/ppermute | solution.py:215
  147.0 2.4 %collective-permute-done.2.low_ref = bf16[4,32,4,256]{3,2,1,0:T(4,128)(2,1)S(1)} collective-permute-done((bf16[4,32,4,256]{3,2,1,0:T(4,128)(2,1)S(1)}, bf16[4,32,4,256]{3,2,1,0:T(4,128)(2,1)S(1)}, u32[]{:S(2)}, u32[]{:S(2)}) %collective-permute-start.2) | collective-permute-done | bytes 262176 | tf_op jit(solution)/shard_map/ppermute | solution.py:215
  149.4 1.6 %collective-permute-done.3.high_ref = bf16[4,32,4,256]{3,2,1,0:T(4,128)(2,1)S(1)} collective-permute-done((bf16[4,32,4,256]{3,2,1,0:T(4,128)(2,1)S(1)}, bf16[4,32,4,256]{3,2,1,0:T(4,128)(2,1)S(1)}, u32[]{:S(2)}, u32[]{:S(2)}) %collective-permute-start.3) | collective-permute-done | bytes 262176 | tf_op jit(solution)/shard_map/ppermute | solution.py:215
  151.0 1.0 place.1
  (3 shorter events, 0.0 us)
Async XLA Ops:
  0.0 34.9 %copy-start = (s32[16,128]{1,0:T(8,128)S(1)}, s32[16,128]{1,0:T(8,128)}, u32[]{:S(2)}) copy-start(s32[16,128]{1,0:T(8,128)} %param.6) | copy-start | bytes 24580
  0.0 1.2 copy-start.1
  1.4 23.8 %collective-permute-start = (bf16[4,32,4,256]{3,2,1,0:T(4,128)(2,1)S(1)}, bf16[4,32,4,256]{3,2,1,0:T(4,128)(2,1)S(1)}, u32[]{:S(2)}, u32[]{:S(2)}) collective-permute-start(bf16[4,32,4,256]{3,2,1,0:T(4,128)(2,1)S(1)} %get-tuple-element.9), channel_id=1, source_target_pairs={{0,960},{64,0},{128,64},{192,128},{256,192},{320,256},{384,320},{4... | collective-permute-start | bytes 786440 | tf_op jit(solution)/shard_map/ppermute | solution.py:215
  19.6 10.9 %collective-permute-start.1 = (bf16[4,32,4,256]{3,2,1,0:T(4,128)(2,1)S(1)}, bf16[4,32,4,256]{3,2,1,0:T(4,128)(2,1)S(1)}, u32[]{:S(2)}, u32[]{:S(2)}) collective-permute-start(bf16[4,32,4,256]{3,2,1,0:T(4,128)(2,1)S(1)} %get-tuple-element.10), channel_id=1, source_target_pairs={{0,64},{64,128},{128,192},{192,256},{256,320},{320,384},{384,448},... | collective-permute-start | bytes 786440 | tf_op jit(solution)/shard_map/ppermute | solution.py:215
  31.3 33.4 %all-to-all-start = ((bf16[8,32,4,256]{3,2,1,0:T(4,128)(2,1)}), bf16[8,32,4,256]{3,2,1,0:T(4,128)(2,1)S(1)}, u32[]{:S(2)}, u32[]{:S(2)}) async-start(bf16[8,32,4,256]{3,2,1,0:T(4,128)(2,1)} %pair.1), calls=%async_computation | async-start | bytes 1048576 | tf_op jit(solution)/shard_map/all_to_all | solution.py:247
  34.9 43.2 %copy-start.2 = (f32[2,256,256]{2,1,0:T(8,128)S(1)}, f32[2,256,256]{2,1,0:T(8,128)}, u32[]{:S(2)}) copy-start(f32[2,256,256]{2,1,0:T(8,128)} %param.9) | copy-start | bytes 1572868
  34.9 43.2 %copy-start.3 = (f32[2,256,256]{2,1,0:T(8,128)S(1)}, f32[2,256,256]{2,1,0:T(8,128)}, u32[]{:S(2)}) copy-start(f32[2,256,256]{2,1,0:T(8,128)} %param.8) | copy-start | bytes 1572868
  66.3 22.3 %all-to-all-start.1 = ((bf16[64,2,4,256]{3,2,1,0:T(4,128)(2,1)}), bf16[64,2,4,256]{3,2,1,0:T(4,128)(2,1)S(1)}, u32[]{:S(2)}, u32[]{:S(2)}) async-start(bf16[64,2,4,256]{3,2,1,0:T(4,128)(2,1)} %bitcast.4), calls=%async_computation.1 | async-start | bytes 524288 | tf_op jit(solution)/shard_map/all_to_all | solution.py:256
  91.5 18.0 %all-to-all-start.2 = ((bf16[64,2,4,256]{3,2,1,0:T(4,128)(2,1)}), bf16[64,2,4,256]{3,2,1,0:T(4,128)(2,1)S(1)}, u32[]{:S(2)}, u32[]{:S(2)}) async-start(bf16[64,2,4,256]{3,2,1,0:T(4,128)(2,1)} %bitcast.15), calls=%async_computation.2 | async-start | bytes 524288 | tf_op jit(solution)/shard_map/all_to_all | solution.py:262
  139.9 9.5 %collective-permute-start.2 = (bf16[4,32,4,256]{3,2,1,0:T(4,128)(2,1)S(1)}, bf16[4,32,4,256]{3,2,1,0:T(4,128)(2,1)S(1)}, u32[]{:S(2)}, u32[]{:S(2)}) collective-permute-start(bf16[4,32,4,256]{3,2,1,0:T(4,128)(2,1)S(1)} %bitcast.21), channel_id=1, source_target_pairs={{0,64},{64,128},{128,192},{192,256},{256,320},{320,384},{384,448},... | collective-permute-start | bytes 786440 | tf_op jit(solution)/shard_map/ppermute | solution.py:215
  141.8 9.2 %collective-permute-start.3 = (bf16[4,32,4,256]{3,2,1,0:T(4,128)(2,1)S(1)}, bf16[4,32,4,256]{3,2,1,0:T(4,128)(2,1)S(1)}, u32[]{:S(2)}, u32[]{:S(2)}) collective-permute-start(bf16[4,32,4,256]{3,2,1,0:T(4,128)(2,1)S(1)} %bitcast.20), channel_id=1, source_target_pairs={{0,960},{64,0},{128,64},{192,128},{256,192},{320,256},{384,320},{4... | collective-permute-start | bytes 786440 | tf_op jit(solution)/shard_map/ppermute | solution.py:215

commit v3 on v2

--- a/solution.py
+++ b/solution.py
@@ -243,7 +243,17 @@
 
     by_parity = grads.reshape(groups // 2, 2, per_group, row_count, block_width)
     mine, first, second = part(parity.reshape(1), by_parity)
-    paired = pair(mine, shifted(first, -1), shifted(second, 1))
+    first, second, my_table, picks, old_left, old_right = lax.optimization_barrier(
+        (
+            shifted(first, -1),
+            shifted(second, 1),
+            my_table,
+            picks,
+            stat_decay * prev_left,
+            stat_decay * prev_right,
+        )
+    )
+    paired = pair(mine, first, second)
     parts = lax.all_to_all(
         paired,
         "dp",
@@ -257,7 +267,7 @@
         outgoing.reshape(owners, CAP, row_count, block_width), "shard", 0, 0, tiled=True
     )
     arrived = jnp.swapaxes(arrived, 0, 1).reshape(CAP, block_width, block_width)
-    fresh = refresh(arrived, stat_decay * prev_left, stat_decay * prev_right)
+    fresh = refresh(arrived, old_left, old_right)
     fresh = jnp.swapaxes(fresh.reshape(CAP, owners, row_count, block_width), 0, 1)
     returned = lax.all_to_all(fresh, "shard", 0, 0, tiled=True)
     chosen = choose(picks, returned.reshape(slot_total, row_count, block_width))

time: 153 us -> 151 us (0.987)
  blocking collectives: 29.6 us -> 103 us
  waiting for transfers between devices: 64.7 us -> 10.6 us
  starting transfers between devices: 48 us -> 27.3 us
    all_to_all x0 -> x3, blocking collectives: none -> 73.7 us  [the longest x1 33.7 us: body(): lax.all_to_all(paired, 'dp', 0, 0, tiled=True, axis_index_groups=every_ot...]
    all_to_all x3 -> x0, waiting for transfers between devices: 51.8 us -> none  [the longest x1 29.9 us: body(): lax.all_to_all(paired, 'dp', 0, 0, tiled=True, axis_index_groups=every_ot...]
    all_to_all x3 -> x0, starting transfers between devices: 20.8 us -> none  [the longest x1 10.8 us: body(): lax.all_to_all(outgoing.reshape(owners, CAP, row_count, block_width), 'sh...]
    ppermute x4, waiting for transfers between devices: 13 us -> 10.6 us  [shifted(): lax.ppermute(value, 'dp', [(i, (i + step) % size) for i in range(size)])]
  transfers between devices with their start and end apart: 7 -> 4, of which waited for: 7 -> 4; matrix products, arithmetic and copies ran while one was open for 1% -> 1% of each run, Pallas kernels for 0% -> 0%
where the time goes in v3:
time: 151 us; the launch traced here: 150 us
  blocking collectives  103 us (68%)
  starting transfers between devices  27.3 us (18%)
  waiting for transfers between devices  10.6 us (7%)
  Pallas kernels  5.24 us (3%)
  local copies, waits for them, and re-layouts  2.67 us (2%)
    all_to_all x1, blocking collectives, body(): lax.all_to_all(paired, 'dp', 0, 0, tiled=True, axis_index_groups=every_ot...  33.7 us
    all_gather x1, blocking collectives, body(): lax.all_gather(chosen, 'dp', axis=0, tiled=False, axis_index_groups=every...  29.4 us
    ppermute x4, starting transfers between devices, shifted(): lax.ppermute(value, 'dp', [(i, (i + step) % size) for i in range(size)])  27.3 us
    all_to_all x1, blocking collectives, body(): lax.all_to_all(outgoing.reshape(owners, CAP, row_count, block_width), 'sh...  22.1 us
    all_to_all x1, blocking collectives, body(): returned = lax.all_to_all(fresh, 'shard', 0, 0, tiled=True)  17.8 us
    ppermute x4, waiting for transfers between devices, shifted(): lax.ppermute(value, 'dp', [(i, (i + step) % size) for i in range(size)])  10.6 us
  transfers between devices with their start and end apart: 4, of which 4 were waited for; matrix products, arithmetic and copies ran while one was open for 1% of the time, Pallas kernels for 0%

profile of v3, /device:TPU:6, one launch (start us, length us, event | category | flops | bytes accessed | tf_op | source)
XLA Modules:
  0.0 150.3 jit_solution(18056422738722340726)
XLA Ops:
  0.0 0.0 copy-start
  0.0 0.0 copy-start.1
  0.0 1.2 copy-done.1
  1.2 0.0 copy-start.2
  1.2 0.1 part.1
  1.4 18.4 %collective-permute-start = (bf16[4,32,4,256]{3,2,1,0:T(4,128)(2,1)S(1)}, bf16[4,32,4,256]{3,2,1,0:T(4,128)(2,1)S(1)}, u32[]{:S(2)}, u32[]{:S(2)}) collective-permute-start(bf16[4,32,4,256]{3,2,1,0:T(4,128)(2,1)S(1)} %get-tuple-element.14), channel_id=1, source_target_pairs={{0,960},{64,0},{128,64},{192,128},{256,192},{320,256},{384,320},{4... | collective-permute-start | bytes 786440 | tf_op jit(solution)/shard_map/ppermute | solution.py:215
  19.7 1.9 %collective-permute-start.1 = (bf16[4,32,4,256]{3,2,1,0:T(4,128)(2,1)S(1)}, bf16[4,32,4,256]{3,2,1,0:T(4,128)(2,1)S(1)}, u32[]{:S(2)}, u32[]{:S(2)}) collective-permute-start(bf16[4,32,4,256]{3,2,1,0:T(4,128)(2,1)S(1)} %get-tuple-element.15), channel_id=1, source_target_pairs={{0,64},{64,128},{128,192},{192,256},{256,320},{320,384},{384,448},... | collective-permute-start | bytes 786440 | tf_op jit(solution)/shard_map/ppermute | solution.py:215
  21.6 0.0 copy-done
  21.7 0.7 dynamic-slice_bitcast_fusion
  22.4 0.1 lt.41
  22.4 0.1 lt.42
  22.6 0.1 select_reduce_fusion
  22.7 0.0 copy-done.2
  22.7 1.1 broadcast_multiply_fusion
  23.9 1.4 collective-permute-done.first_ref
  25.3 5.3 %collective-permute-done.1.second_ref = bf16[4,32,4,256]{3,2,1,0:T(4,128)(2,1)S(1)} collective-permute-done((bf16[4,32,4,256]{3,2,1,0:T(4,128)(2,1)S(1)}, bf16[4,32,4,256]{3,2,1,0:T(4,128)(2,1)S(1)}, u32[]{:S(2)}, u32[]{:S(2)}) %collective-permute-start.1) | collective-permute-done | bytes 262176 | tf_op jit(solution)/shard_map/ppermute | solution.py:215
  30.6 0.9 pair.1
  31.5 33.7 %all_to_all.15.parts_ref = bf16[8,32,4,256]{3,2,1,0:T(4,128)(2,1)S(1)} all-to-all(bf16[8,32,4,256]{3,2,1,0:T(4,128)(2,1)S(1)} %pair.1), channel_id=1, replica_groups={{0,128,256,384,512,640,768,896},{64,192,320,448,576,704,832,960},{1,129..., dimensions={0} | all-to-all | bytes 1048576 | tf_op jit(solution)/shard_map/all_to_all | solution.py:257
  65.3 0.8 sum_and_gather.1
  66.1 22.1 %all_to_all.16 = bf16[64,2,4,256]{3,2,1,0:T(4,128)(2,1)S(1)} all-to-all(bf16[64,2,4,256]{3,2,1,0:T(4,128)(2,1)S(1)} %bitcast.19), channel_id=1, replica_groups=mesh['dp'=16,'shard'=64] {'shard'}, dimensions={0} | all-to-all | bytes 524288 | tf_op jit(solution)/shard_map/all_to_all | solution.py:266
  88.3 0.1 copy.12
  88.4 0.1 reshape.45.arrived_ref
  88.4 1.8 %refresh.1 = bf16[2,256,256]{2,1,0:T(8,128)(2,1)S(1)} custom-call(bf16[2,256,256]{2,1,0:T(8,128)(2,1)S(1)} %reshape.45.arrived_ref, f32[2,256,256]{2,1,0:T(8,128)S(1)} %get-tuple-element.21.left_ref, f32[2,256,256]{2,1,0:T(8,128)S(1)} %get-tuple-element.22.right_ref), custom_call_target="tpu_custom_call" | custom-call | flops 805306368 | bytes 1572864 | tf_op jit(solution)/shard_map/refresh/pallas_call | solution.py:63
  90.2 0.1 reshape.46
  90.3 0.1 copy.15
  90.4 17.8 %all_to_all.17 = bf16[64,2,4,256]{3,2,1,0:T(4,128)(2,1)S(1)} all-to-all(bf16[64,2,4,256]{3,2,1,0:T(4,128)(2,1)S(1)} %bitcast.21), channel_id=1, replica_groups=mesh['dp'=16,'shard'=64] {'shard'}, dimensions={0} | all-to-all | bytes 524288 | tf_op jit(solution)/shard_map/all_to_all | solution.py:272
  108.2 0.6 choose.1
  108.8 29.4 %all-gather = bf16[256,4,256]{2,1,0:T(4,128)(2,1)S(1)} all-gather(bf16[32,4,256]{2,1,0:T(4,128)(2,1)S(1)} %choose.1), channel_id=2, replica_groups={{0,128,256,384,512,640,768,896},{64,192,320,448,576,704,832,960},{1,129..., dimensions={0}, use_global_device_ids=true | all-gather | bytes 589824 | tf_op jit(solution)/shard_map/all_gather | solution.py:274
  138.2 0.2 fusion.2
  138.4 1.9 %collective-permute-start.2 = (bf16[4,32,4,256]{3,2,1,0:T(4,128)(2,1)S(1)}, bf16[4,32,4,256]{3,2,1,0:T(4,128)(2,1)S(1)}, u32[]{:S(2)}, u32[]{:S(2)}) collective-permute-start(bf16[4,32,4,256]{3,2,1,0:T(4,128)(2,1)S(1)} %bitcast.23), channel_id=1, source_target_pairs={{0,64},{64,128},{128,192},{192,256},{256,320},{320,384},{384,448},... | collective-permute-start | bytes 786440 | tf_op jit(solution)/shard_map/ppermute | solution.py:215
  140.3 5.1 %collective-permute-start.3 = (bf16[4,32,4,256]{3,2,1,0:T(4,128)(2,1)S(1)}, bf16[4,32,4,256]{3,2,1,0:T(4,128)(2,1)S(1)}, u32[]{:S(2)}, u32[]{:S(2)}) collective-permute-start(bf16[4,32,4,256]{3,2,1,0:T(4,128)(2,1)S(1)} %bitcast.22), channel_id=1, source_target_pairs={{0,960},{64,0},{128,64},{192,128},{256,192},{320,256},{384,320},{4... | collective-permute-start | bytes 786440 | tf_op jit(solution)/shard_map/ppermute | solution.py:215
  145.4 2.4 %collective-permute-done.2.low_ref = bf16[4,32,4,256]{3,2,1,0:T(4,128)(2,1)S(1)} collective-permute-done((bf16[4,32,4,256]{3,2,1,0:T(4,128)(2,1)S(1)}, bf16[4,32,4,256]{3,2,1,0:T(4,128)(2,1)S(1)}, u32[]{:S(2)}, u32[]{:S(2)}) %collective-permute-start.2) | collective-permute-done | bytes 262176 | tf_op jit(solution)/shard_map/ppermute | solution.py:215
  147.8 1.5 collective-permute-done.3.high_ref
  149.3 1.0 place.1
  (3 shorter events, 0.0 us)
Async XLA Ops:
  0.0 21.6 %copy-start = (s32[16,128]{1,0:T(8,128)S(1)}, s32[16,128]{1,0:T(8,128)}, u32[]{:S(2)}) copy-start(s32[16,128]{1,0:T(8,128)} %param.6) | copy-start | bytes 24580
  0.0 1.2 copy-start.1
  1.2 21.5 %copy-start.2 = (f32[2,256,256]{2,1,0:T(8,128)S(1)}, f32[2,256,256]{2,1,0:T(8,128)}, u32[]{:S(2)}) copy-start(f32[2,256,256]{2,1,0:T(8,128)} %param.9) | copy-start | bytes 1572868
  1.4 23.9 %collective-permute-start = (bf16[4,32,4,256]{3,2,1,0:T(4,128)(2,1)S(1)}, bf16[4,32,4,256]{3,2,1,0:T(4,128)(2,1)S(1)}, u32[]{:S(2)}, u32[]{:S(2)}) collective-permute-start(bf16[4,32,4,256]{3,2,1,0:T(4,128)(2,1)S(1)} %get-tuple-element.14), channel_id=1, source_target_pairs={{0,960},{64,0},{128,64},{192,128},{256,192},{320,256},{384,320},{4... | collective-permute-start | bytes 786440 | tf_op jit(solution)/shard_map/ppermute | solution.py:215
  19.7 10.9 %collective-permute-start.1 = (bf16[4,32,4,256]{3,2,1,0:T(4,128)(2,1)S(1)}, bf16[4,32,4,256]{3,2,1,0:T(4,128)(2,1)S(1)}, u32[]{:S(2)}, u32[]{:S(2)}) collective-permute-start(bf16[4,32,4,256]{3,2,1,0:T(4,128)(2,1)S(1)} %get-tuple-element.15), channel_id=1, source_target_pairs={{0,64},{64,128},{128,192},{192,256},{256,320},{320,384},{384,448},... | collective-permute-start | bytes 786440 | tf_op jit(solution)/shard_map/ppermute | solution.py:215
  138.4 9.5 %collective-permute-start.2 = (bf16[4,32,4,256]{3,2,1,0:T(4,128)(2,1)S(1)}, bf16[4,32,4,256]{3,2,1,0:T(4,128)(2,1)S(1)}, u32[]{:S(2)}, u32[]{:S(2)}) collective-permute-start(bf16[4,32,4,256]{3,2,1,0:T(4,128)(2,1)S(1)} %bitcast.23), channel_id=1, source_target_pairs={{0,64},{64,128},{128,192},{192,256},{256,320},{320,384},{384,448},... | collective-permute-start | bytes 786440 | tf_op jit(solution)/shard_map/ppermute | solution.py:215
  140.3 9.0 %collective-permute-start.3 = (bf16[4,32,4,256]{3,2,1,0:T(4,128)(2,1)S(1)}, bf16[4,32,4,256]{3,2,1,0:T(4,128)(2,1)S(1)}, u32[]{:S(2)}, u32[]{:S(2)}) collective-permute-start(bf16[4,32,4,256]{3,2,1,0:T(4,128)(2,1)S(1)} %bitcast.22), channel_id=1, source_target_pairs={{0,960},{64,0},{128,64},{192,128},{256,192},{320,256},{384,320},{4... | collective-permute-start | bytes 786440 | tf_op jit(solution)/shard_map/ppermute | solution.py:215

commit v4 on v3

--- a/solution.py
+++ b/solution.py
@@ -6,6 +6,7 @@
 from jax.sharding import PartitionSpec as P
 
 CAP = 2
+RADIX = 4
 VMEM_GRANT = 12 * 1024 * 1024
 
 
@@ -73,13 +74,20 @@
     )(arrived, prev_left, prev_right)
 
 
-def part_kernel(parity_ref, grads_ref, mine_ref, first_ref, second_ref, sems):
-    parity = parity_ref[0]
-    half = first_ref.shape[0]
+def part_kernel(place_ref, grads_ref, up_ref, down_ref, far_up_ref, far_down_ref, sems):
+    residue = place_ref[0]
+    half = far_up_ref.shape[0]
+    pieces = (
+        (slice(None), 1, up_ref),
+        (slice(None), RADIX - 1, down_ref),
+        (slice(0, half), 2, far_up_ref),
+        (slice(half, None), 2, far_down_ref),
+    )
     copies = [
-        pltpu.make_async_copy(grads_ref.at[:half, 1 - parity], first_ref, sems.at[0]),
-        pltpu.make_async_copy(grads_ref.at[half:, 1 - parity], second_ref, sems.at[1]),
-        pltpu.make_async_copy(grads_ref.at[:, parity], mine_ref, sems.at[2]),
+        pltpu.make_async_copy(
+            grads_ref.at[where, (residue + step) % RADIX], piece_ref, sems.at[index]
+        )
+        for index, (where, step, piece_ref) in enumerate(pieces)
     ]
     for copy in copies:
         copy.start()
@@ -87,52 +95,44 @@
         copy.wait()
 
 
-def part(parity, by_parity):
-    count = by_parity.shape[0]
+def part(residue, by_residue):
+    count = by_residue.shape[0]
     pieces = [
-        jax.ShapeDtypeStruct((size,) + by_parity.shape[2:], jnp.bfloat16)
-        for size in (count, count // 2, count // 2)
+        jax.ShapeDtypeStruct((size,) + by_residue.shape[2:], jnp.bfloat16)
+        for size in (count, count, count // 2, count // 2)
     ]
     return pl.pallas_call(
         part_kernel,
         in_specs=[pl.BlockSpec(memory_space=pltpu.SMEM), pl.BlockSpec(memory_space=pltpu.HBM)],
         out_shape=pieces,
-        out_specs=[pl.BlockSpec(memory_space=pltpu.VMEM)] * 3,
-        scratch_shapes=[pltpu.SemaphoreType.DMA((3,))],
+        out_specs=[pl.BlockSpec(memory_space=pltpu.VMEM)] * 4,
+        scratch_shapes=[pltpu.SemaphoreType.DMA((4,))],
         compiler_params=pltpu.CompilerParams(vmem_limit_bytes=VMEM_GRANT),
         name="part",
-    )(parity, by_parity)
-
-
-def pair_kernel(mine_ref, first_ref, second_ref, out_ref, sum_ref, sems):
-    half = first_ref.shape[0]
-    copies = []
+    )(residue, pltpu.with_memory_space_constraint(by_residue, pltpu.HBM))
+
+
+def combine_kernel(place_ref, grads_ref, up_ref, down_ref, far_up_ref, far_down_ref, out_ref):
+    residue = place_ref[0]
+    half = far_up_ref.shape[0]
     for index in range(2 * half):
-        came_ref = first_ref if index < half else second_ref
-        sum_ref[index] = (
-            mine_ref[index].astype(jnp.float32) + came_ref[index % half].astype(jnp.float32)
-        ).astype(jnp.bfloat16)
-        copies.append(
-            pltpu.make_async_copy(sum_ref.at[index], out_ref.at[index], sems.at[index])
-        )
-        copies[-1].start()
-    for copy in copies:
-        copy.wait()
-
-
-def pair(mine, first, second):
-    return pl.pallas_call(
-        pair_kernel,
-        in_specs=[pl.BlockSpec(memory_space=pltpu.VMEM)] * 3,
-        out_specs=pl.BlockSpec(memory_space=pl.ANY),
-        out_shape=jax.ShapeDtypeStruct(mine.shape, jnp.bfloat16),
-        scratch_shapes=[
-            pltpu.VMEM(mine.shape, jnp.bfloat16),
-            pltpu.SemaphoreType.DMA((mine.shape[0],)),
-        ],
-        compiler_params=pltpu.CompilerParams(vmem_limit_bytes=VMEM_GRANT),
-        name="pair",
-    )(mine, first, second)
+        far_ref = far_up_ref if index < half else far_down_ref
+        total = grads_ref[index, residue].astype(jnp.float32)
+        total += up_ref[index].astype(jnp.float32)
+        total += down_ref[index].astype(jnp.float32)
+        total += far_ref[index % half].astype(jnp.float32)
+        out_ref[index] = total.astype(jnp.bfloat16)
+
+
+def combine(residue, by_residue, pieces):
+    return pl.pallas_call(
+        combine_kernel,
+        in_specs=[pl.BlockSpec(memory_space=pltpu.SMEM)]
+        + [pl.BlockSpec(memory_space=pltpu.VMEM)] * 5,
+        out_shape=jax.ShapeDtypeStruct(pieces[0].shape, jnp.bfloat16),
+        compiler_params=pltpu.CompilerParams(vmem_limit_bytes=VMEM_GRANT),
+        name="combine",
+    )(residue, by_residue, *pieces)
 
 
 def gather_rows_kernel(table_ref, parts_ref, out_ref, sum_ref):
@@ -215,8 +215,8 @@
     return lax.ppermute(value, "dp", [(i, (i + step) % size) for i in range(size)])
 
 
-def every_other(size):
-    return [list(range(start, size, 2)) for start in range(2)]
+def strided(size, stride):
+    return [list(range(start, size, stride)) for start in range(stride)]
 
 
 def body(grads, owner_table, block_counts, prev_left, prev_right):
@@ -241,26 +241,25 @@
     earliest = jnp.min(jnp.where(matches, slot_ids[None, :], slot_total), axis=1)
     picks = jnp.where(earliest < slot_total, earliest, -1)
 
-    by_parity = grads.reshape(groups // 2, 2, per_group, row_count, block_width)
-    mine, first, second = part(parity.reshape(1), by_parity)
-    first, second, my_table, picks, old_left, old_right = lax.optimization_barrier(
+    residue = (my_group % RADIX).reshape(1)
+    by_residue = grads.reshape(groups // RADIX, RADIX, per_group, row_count, block_width)
+    up, down, far_up, far_down = part(residue, by_residue)
+    pieces, my_table, picks, old_left, old_right = lax.optimization_barrier(
         (
-            shifted(first, -1),
-            shifted(second, 1),
+            (shifted(up, 1), shifted(down, -1), shifted(far_up, 2), shifted(far_down, -2)),
             my_table,
             picks,
             stat_decay * prev_left,
             stat_decay * prev_right,
         )
     )
-    paired = pair(mine, first, second)
     parts = lax.all_to_all(
-        paired,
+        combine(residue, by_residue, pieces),
         "dp",
         0,
         0,
         tiled=True,
-        axis_index_groups=every_other(groups),
+        axis_index_groups=strided(groups, RADIX),
     )
     outgoing = sum_and_gather(my_table, parts)
     arrived = lax.all_to_all(
@@ -272,7 +271,7 @@
     returned = lax.all_to_all(fresh, "shard", 0, 0, tiled=True)
     chosen = choose(picks, returned.reshape(slot_total, row_count, block_width))
     same = lax.all_gather(
-        chosen, "dp", axis=0, tiled=False, axis_index_groups=every_other(groups)
+        chosen, "dp", axis=0, tiled=False, axis_index_groups=strided(groups, 2)
     )
     low = shifted(same[:half], 1)
     high = shifted(same[half:], -1)

time: 151 us -> 146 us (0.967)
  blocking collectives: 103 us -> 94.4 us
  starting transfers between devices: 27.3 us -> 34.2 us
  waiting for transfers between devices: 10.6 us -> 8.62 us
    all_to_all x1, blocking collectives: 33.7 us -> 24.9 us  [body(): lax.all_to_all(combine(residue, by_residue, pieces), 'dp', 0, 0, tiled=Tr...]
    ppermute x4 -> x6, starting transfers between devices: 27.3 us -> 34.2 us  [shifted(): lax.ppermute(value, 'dp', [(i, (i + step) % size) for i in range(size)])]
    ppermute x4 -> x6, waiting for transfers between devices: 10.6 us -> 8.62 us  [shifted(): lax.ppermute(value, 'dp', [(i, (i + step) % size) for i in range(size)])]
  transfers between devices with their start and end apart: 4 -> 6, of which waited for: 4 -> 4; matrix products, arithmetic and copies ran while one was open for 1% -> 2% of each run, Pallas kernels for 0% -> 0%
where the time goes in v4:
time: 146 us
  blocking collectives  94.4 us (65%)
  starting transfers between devices  34.2 us (23%)
  waiting for transfers between devices  8.62 us (6%)
  Pallas kernels  5.51 us (4%)
    ppermute x6, starting transfers between devices, shifted(): lax.ppermute(value, 'dp', [(i, (i + step) % size) for i in range(size)])  34.2 us
    all_gather x1, blocking collectives, body(): lax.all_gather(chosen, 'dp', axis=0, tiled=False, axis_index_groups=strid...  29.5 us
    all_to_all x1, blocking collectives, body(): lax.all_to_all(combine(residue, by_residue, pieces), 'dp', 0, 0, tiled=Tr...  24.9 us
    all_to_all x1, blocking collectives, body(): lax.all_to_all(outgoing.reshape(owners, CAP, row_count, block_width), 'sh...  22.1 us
    all_to_all x1, blocking collectives, body(): returned = lax.all_to_all(fresh, 'shard', 0, 0, tiled=True)  17.8 us
    ppermute x6, waiting for transfers between devices, shifted(): lax.ppermute(value, 'dp', [(i, (i + step) % size) for i in range(size)])  8.62 us
  transfers between devices with their start and end apart: 6, of which 4 were waited for; matrix products, arithmetic and copies ran while one was open for 2% of the time, Pallas kernels for 0%

profile of v4, /device:TPU:6, one launch (start us, length us, event | category | flops | bytes accessed | tf_op | source)
XLA Modules:
  0.0 145.7 jit_solution(15504426104881085390)
XLA Ops:
  0.0 0.0 copy-start
  0.0 0.0 copy-start.2
  0.0 1.2 part.1
  1.2 6.1 %collective-permute-start.2 = (bf16[2,32,4,256]{3,2,1,0:T(4,128)(2,1)S(1)}, bf16[2,32,4,256]{3,2,1,0:T(4,128)(2,1)S(1)}, u32[]{:S(2)}, u32[]{:S(2)}) collective-permute-start(bf16[2,32,4,256]{3,2,1,0:T(4,128)(2,1)S(1)} %get-tuple-element.19), channel_id=1, source_target_pairs={{0,128},{64,192},{128,256},{192,320},{256,384},{320,448},{384,512}... | collective-permute-start | bytes 393224 | tf_op jit(solution)/shard_map/ppermute | solution.py:215
  7.3 14.0 %collective-permute-start.3 = (bf16[2,32,4,256]{3,2,1,0:T(4,128)(2,1)S(1)}, bf16[2,32,4,256]{3,2,1,0:T(4,128)(2,1)S(1)}, u32[]{:S(2)}, u32[]{:S(2)}) collective-permute-start(bf16[2,32,4,256]{3,2,1,0:T(4,128)(2,1)S(1)} %get-tuple-element.20), channel_id=1, source_target_pairs={{0,896},{64,960},{128,0},{192,64},{256,128},{320,192},{384,256},{4... | collective-permute-start | bytes 393224 | tf_op jit(solution)/shard_map/ppermute | solution.py:215
  21.4 3.4 %collective-permute-start = (bf16[4,32,4,256]{3,2,1,0:T(4,128)(2,1)S(1)}, bf16[4,32,4,256]{3,2,1,0:T(4,128)(2,1)S(1)}, u32[]{:S(2)}, u32[]{:S(2)}) collective-permute-start(bf16[4,32,4,256]{3,2,1,0:T(4,128)(2,1)S(1)} %get-tuple-element.17), channel_id=1, source_target_pairs={{0,64},{64,128},{128,192},{192,256},{256,320},{320,384},{384,448},... | collective-permute-start | bytes 786440 | tf_op jit(solution)/shard_map/ppermute | solution.py:215
  24.7 3.7 %collective-permute-start.1 = (bf16[4,32,4,256]{3,2,1,0:T(4,128)(2,1)S(1)}, bf16[4,32,4,256]{3,2,1,0:T(4,128)(2,1)S(1)}, u32[]{:S(2)}, u32[]{:S(2)}) collective-permute-start(bf16[4,32,4,256]{3,2,1,0:T(4,128)(2,1)S(1)} %get-tuple-element.18), channel_id=1, source_target_pairs={{0,960},{64,0},{128,64},{192,128},{256,192},{320,256},{384,320},{4... | collective-permute-start | bytes 786440 | tf_op jit(solution)/shard_map/ppermute | solution.py:215
  28.4 0.0 copy-done
  28.5 0.7 dynamic-slice_bitcast_fusion
  29.2 0.1 lt.46
  29.2 0.1 lt.47
  29.4 0.0 copy-done.2
  29.4 0.0 copy-start.1
  29.4 1.2 broadcast_multiply_fusion
  30.6 0.1 select_reduce_fusion
  30.8 0.0 collective-permute-done.2.far_up_ref
  30.8 0.0 collective-permute-done.3.far_down_ref
  30.8 1.4 collective-permute-done.up_ref
  32.2 1.9 %collective-permute-done.1.down_ref = bf16[4,32,4,256]{3,2,1,0:T(4,128)(2,1)S(1)} collective-permute-done((bf16[4,32,4,256]{3,2,1,0:T(4,128)(2,1)S(1)}, bf16[4,32,4,256]{3,2,1,0:T(4,128)(2,1)S(1)}, u32[]{:S(2)}, u32[]{:S(2)}) %collective-permute-start.1) | collective-permute-done | bytes 262176 | tf_op jit(solution)/shard_map/ppermute | solution.py:215
  34.1 0.0 copy-done.1
  34.1 0.2 combine.1
  34.3 24.9 %all_to_all.15.parts_ref = bf16[4,32,4,256]{3,2,1,0:T(4,128)(2,1)S(1)} all-to-all(bf16[4,32,4,256]{3,2,1,0:T(4,128)(2,1)S(1)} %combine.1), channel_id=1, replica_groups={{0,256,512,768},{64,320,576,832},{128,384,640,896},{192,448,704,960},{1..., dimensions={0} | all-to-all | bytes 524288 | tf_op jit(solution)/shard_map/all_to_all | solution.py:256
  59.2 0.8 sum_and_gather.1
  60.0 22.1 %all_to_all.16 = bf16[64,2,4,256]{3,2,1,0:T(4,128)(2,1)S(1)} all-to-all(bf16[64,2,4,256]{3,2,1,0:T(4,128)(2,1)S(1)} %bitcast.20), channel_id=1, replica_groups=mesh['dp'=16,'shard'=64] {'shard'}, dimensions={0} | all-to-all | bytes 524288 | tf_op jit(solution)/shard_map/all_to_all | solution.py:265
  82.2 0.1 copy.12
  82.3 0.1 reshape.48.arrived_ref
  82.3 1.8 %refresh.1 = bf16[2,256,256]{2,1,0:T(8,128)(2,1)S(1)} custom-call(bf16[2,256,256]{2,1,0:T(8,128)(2,1)S(1)} %reshape.48.arrived_ref, f32[2,256,256]{2,1,0:T(8,128)S(1)} %get-tuple-element.27.left_ref, f32[2,256,256]{2,1,0:T(8,128)S(1)} %get-tuple-element.28.right_ref), custom_call_target="tpu_custom_call" | custom-call | flops 805306368 | bytes 1572864 | tf_op jit(solution)/shard_map/refresh/pallas_call | solution.py:64
  84.1 0.1 reshape.49
  84.2 0.1 copy.15
  84.3 17.8 %all_to_all.17 = bf16[64,2,4,256]{3,2,1,0:T(4,128)(2,1)S(1)} all-to-all(bf16[64,2,4,256]{3,2,1,0:T(4,128)(2,1)S(1)} %bitcast.23), channel_id=1, replica_groups=mesh['dp'=16,'shard'=64] {'shard'}, dimensions={0} | all-to-all | bytes 524288 | tf_op jit(solution)/shard_map/all_to_all | solution.py:271
  102.1 0.6 choose.1
  102.7 29.5 %all-gather = bf16[256,4,256]{2,1,0:T(4,128)(2,1)S(1)} all-gather(bf16[32,4,256]{2,1,0:T(4,128)(2,1)S(1)} %choose.1), channel_id=2, replica_groups={{0,128,256,384,512,640,768,896},{64,192,320,448,576,704,832,960},{1,129..., dimensions={0}, use_global_device_ids=true | all-gather | bytes 589824 | tf_op jit(solution)/shard_map/all_gather | solution.py:273
  132.2 0.2 fusion.2
  132.4 3.8 %collective-permute-start.4 = (bf16[4,32,4,256]{3,2,1,0:T(4,128)(2,1)S(1)}, bf16[4,32,4,256]{3,2,1,0:T(4,128)(2,1)S(1)}, u32[]{:S(2)}, u32[]{:S(2)}) collective-permute-start(bf16[4,32,4,256]{3,2,1,0:T(4,128)(2,1)S(1)} %bitcast.25), channel_id=1, source_target_pairs={{0,64},{64,128},{128,192},{192,256},{256,320},{320,384},{384,448},... | collective-permute-start | bytes 786440 | tf_op jit(solution)/shard_map/ppermute | solution.py:215
  136.2 3.3 %collective-permute-start.5 = (bf16[4,32,4,256]{3,2,1,0:T(4,128)(2,1)S(1)}, bf16[4,32,4,256]{3,2,1,0:T(4,128)(2,1)S(1)}, u32[]{:S(2)}, u32[]{:S(2)}) collective-permute-start(bf16[4,32,4,256]{3,2,1,0:T(4,128)(2,1)S(1)} %bitcast.24), channel_id=1, source_target_pairs={{0,960},{64,0},{128,64},{192,128},{256,192},{320,256},{384,320},{4... | collective-permute-start | bytes 786440 | tf_op jit(solution)/shard_map/ppermute | solution.py:215
  139.5 2.4 %collective-permute-done.4.low_ref = bf16[4,32,4,256]{3,2,1,0:T(4,128)(2,1)S(1)} collective-permute-done((bf16[4,32,4,256]{3,2,1,0:T(4,128)(2,1)S(1)}, bf16[4,32,4,256]{3,2,1,0:T(4,128)(2,1)S(1)}, u32[]{:S(2)}, u32[]{:S(2)}) %collective-permute-start.4) | collective-permute-done | bytes 262176 | tf_op jit(solution)/shard_map/ppermute | solution.py:215
  141.9 2.9 %collective-permute-done.5.high_ref = bf16[4,32,4,256]{3,2,1,0:T(4,128)(2,1)S(1)} collective-permute-done((bf16[4,32,4,256]{3,2,1,0:T(4,128)(2,1)S(1)}, bf16[4,32,4,256]{3,2,1,0:T(4,128)(2,1)S(1)}, u32[]{:S(2)}, u32[]{:S(2)}) %collective-permute-start.5) | collective-permute-done | bytes 262176 | tf_op jit(solution)/shard_map/ppermute | solution.py:215
  144.8 1.0 place.1
  (3 shorter events, 0.0 us)
Async XLA Ops:
  0.0 28.4 %copy-start = (s32[16,128]{1,0:T(8,128)S(1)}, s32[16,128]{1,0:T(8,128)}, u32[]{:S(2)}) copy-start(s32[16,128]{1,0:T(8,128)} %param.6) | copy-start | bytes 24580
  0.0 29.4 %copy-start.2 = (f32[2,256,256]{2,1,0:T(8,128)S(1)}, f32[2,256,256]{2,1,0:T(8,128)}, u32[]{:S(2)}) copy-start(f32[2,256,256]{2,1,0:T(8,128)} %param.9) | copy-start | bytes 1572868
  1.2 29.6 %collective-permute-start.2 = (bf16[2,32,4,256]{3,2,1,0:T(4,128)(2,1)S(1)}, bf16[2,32,4,256]{3,2,1,0:T(4,128)(2,1)S(1)}, u32[]{:S(2)}, u32[]{:S(2)}) collective-permute-start(bf16[2,32,4,256]{3,2,1,0:T(4,128)(2,1)S(1)} %get-tuple-element.19), channel_id=1, source_target_pairs={{0,128},{64,192},{128,256},{192,320},{256,384},{320,448},{384,512}... | collective-permute-start | bytes 393224 | tf_op jit(solution)/shard_map/ppermute | solution.py:215
  7.3 23.5 %collective-permute-start.3 = (bf16[2,32,4,256]{3,2,1,0:T(4,128)(2,1)S(1)}, bf16[2,32,4,256]{3,2,1,0:T(4,128)(2,1)S(1)}, u32[]{:S(2)}, u32[]{:S(2)}) collective-permute-start(bf16[2,32,4,256]{3,2,1,0:T(4,128)(2,1)S(1)} %get-tuple-element.20), channel_id=1, source_target_pairs={{0,896},{64,960},{128,0},{192,64},{256,128},{320,192},{384,256},{4... | collective-permute-start | bytes 393224 | tf_op jit(solution)/shard_map/ppermute | solution.py:215
  21.4 10.9 %collective-permute-start = (bf16[4,32,4,256]{3,2,1,0:T(4,128)(2,1)S(1)}, bf16[4,32,4,256]{3,2,1,0:T(4,128)(2,1)S(1)}, u32[]{:S(2)}, u32[]{:S(2)}) collective-permute-start(bf16[4,32,4,256]{3,2,1,0:T(4,128)(2,1)S(1)} %get-tuple-element.17), channel_id=1, source_target_pairs={{0,64},{64,128},{128,192},{192,256},{256,320},{320,384},{384,448},... | collective-permute-start | bytes 786440 | tf_op jit(solution)/shard_map/ppermute | solution.py:215
  24.7 9.4 %collective-permute-start.1 = (bf16[4,32,4,256]{3,2,1,0:T(4,128)(2,1)S(1)}, bf16[4,32,4,256]{3,2,1,0:T(4,128)(2,1)S(1)}, u32[]{:S(2)}, u32[]{:S(2)}) collective-permute-start(bf16[4,32,4,256]{3,2,1,0:T(4,128)(2,1)S(1)} %get-tuple-element.18), channel_id=1, source_target_pairs={{0,960},{64,0},{128,64},{192,128},{256,192},{320,256},{384,320},{4... | collective-permute-start | bytes 786440 | tf_op jit(solution)/shard_map/ppermute | solution.py:215
  29.4 4.7 %copy-start.1 = (bf16[1,512,4,256]{3,2,1,0:T(4,128)(2,1)S(1)}, bf16[1,512,4,256]{3,2,1,0:T(4,128)(2,1)}, u32[]{:S(2)}) copy-start(bf16[1,512,4,256]{3,2,1,0:T(4,128)(2,1)} %param.5) | copy-start | bytes 3145732
  132.4 9.5 %collective-permute-start.4 = (bf16[4,32,4,256]{3,2,1,0:T(4,128)(2,1)S(1)}, bf16[4,32,4,256]{3,2,1,0:T(4,128)(2,1)S(1)}, u32[]{:S(2)}, u32[]{:S(2)}) collective-permute-start(bf16[4,32,4,256]{3,2,1,0:T(4,128)(2,1)S(1)} %bitcast.25), channel_id=1, source_target_pairs={{0,64},{64,128},{128,192},{192,256},{256,320},{320,384},{384,448},... | collective-permute-start | bytes 786440 | tf_op jit(solution)/shard_map/ppermute | solution.py:215
  136.2 8.6 %collective-permute-start.5 = (bf16[4,32,4,256]{3,2,1,0:T(4,128)(2,1)S(1)}, bf16[4,32,4,256]{3,2,1,0:T(4,128)(2,1)S(1)}, u32[]{:S(2)}, u32[]{:S(2)}) collective-permute-start(bf16[4,32,4,256]{3,2,1,0:T(4,128)(2,1)S(1)} %bitcast.24), channel_id=1, source_target_pairs={{0,960},{64,0},{128,64},{192,128},{256,192},{320,256},{384,320},{4... | collective-permute-start | bytes 786440 | tf_op jit(solution)/shard_map/ppermute | solution.py:215

commit v5 on v4

--- a/solution.py
+++ b/solution.py
@@ -183,13 +183,23 @@
     )(picks, returned)
 
 
-def place_kernel(parity_ref, same_ref, low_ref, high_ref, out_ref, sems):
-    parity = parity_ref[0]
-    half = low_ref.shape[0]
+def place_kernel(
+    place_ref, same_ref, above_ref, below_ref, far_low_ref, far_high_ref, out_ref, sems
+):
+    residue = place_ref[0]
+    half = far_low_ref.shape[0]
+    pieces = (
+        (slice(None), 0, same_ref),
+        (slice(None), 1, above_ref),
+        (slice(None), RADIX - 1, below_ref),
+        (slice(0, half), 2, far_low_ref),
+        (slice(half, None), 2, far_high_ref),
+    )
     copies = [
-        pltpu.make_async_copy(same_ref, out_ref.at[:, parity], sems.at[0]),
-        pltpu.make_async_copy(low_ref, out_ref.at[:half, 1 - parity], sems.at[1]),
-        pltpu.make_async_copy(high_ref, out_ref.at[half:, 1 - parity], sems.at[2]),
+        pltpu.make_async_copy(
+            piece_ref, out_ref.at[where, (residue + step) % RADIX], sems.at[index]
+        )
+        for index, (where, step, piece_ref) in enumerate(pieces)
     ]
     for copy in copies:
         copy.start()
@@ -197,17 +207,18 @@
         copy.wait()
 
 
-def place(parity, same, low, high):
+def place(residue, same, *others):
+    shape = (same.shape[0], RADIX) + same.shape[1:]
     return pl.pallas_call(
         place_kernel,
         in_specs=[pl.BlockSpec(memory_space=pltpu.SMEM)]
-        + [pl.BlockSpec(memory_space=pltpu.VMEM)] * 3,
+        + [pl.BlockSpec(memory_space=pltpu.VMEM)] * 5,
         out_specs=pl.BlockSpec(memory_space=pl.ANY),
-        out_shape=jax.ShapeDtypeStruct((same.shape[0], 2) + same.shape[1:], jnp.bfloat16),
-        scratch_shapes=[pltpu.SemaphoreType.DMA((3,))],
+        out_shape=jax.ShapeDtypeStruct(shape, jnp.bfloat16),
+        scratch_shapes=[pltpu.SemaphoreType.DMA((5,))],
         compiler_params=pltpu.CompilerParams(vmem_limit_bytes=VMEM_GRANT),
         name="place",
-    )(parity, same, low, high)
+    )(residue, same, *others)
 
 
 def shifted(value, step):
@@ -223,12 +234,11 @@
     owners = lax.axis_size("shard")
     groups = lax.axis_size("dp")
     my_group = lax.axis_index("dp")
-    parity = my_group % 2
     blocks = grads.shape[1]
     row_count = grads.shape[2]
     block_width = grads.shape[3]
     per_group = blocks // groups
-    half = groups // 4
+    half = groups // RADIX // 2
     slot_total = owners * CAP
     slot_ids = jnp.arange(slot_total, dtype=jnp.int32)
     my_table = lax.dynamic_index_in_dim(owner_table, my_group, 0, keepdims=False)
@@ -271,11 +281,16 @@
     returned = lax.all_to_all(fresh, "shard", 0, 0, tiled=True)
     chosen = choose(picks, returned.reshape(slot_total, row_count, block_width))
     same = lax.all_gather(
-        chosen, "dp", axis=0, tiled=False, axis_index_groups=strided(groups, 2)
-    )
-    low = shifted(same[:half], 1)
-    high = shifted(same[half:], -1)
-    placed = place(parity.reshape(1), same, low, high)
+        chosen, "dp", axis=0, tiled=False, axis_index_groups=strided(groups, RADIX)
+    )
+    placed = place(
+        residue,
+        same,
+        shifted(same, -1),
+        shifted(same, 1),
+        shifted(same[:half], 2),
+        shifted(same[half:], -2),
+    )
     return placed.reshape(blocks, row_count, block_width)
 
 

time: 146 us -> 144 us (0.986)
  blocking collectives: 94.4 us -> 82.9 us
  starting transfers between devices: 34.2 us -> 42.3 us
    all_gather x1, blocking collectives: 29.5 us -> 18 us  [body(): lax.all_gather(chosen, 'dp', axis=0, tiled=False, axis_index_groups=strid...]
    ppermute x6 -> x8, starting transfers between devices: 34.2 us -> 42.3 us  [shifted(): lax.ppermute(value, 'dp', [(i, (i + step) % size) for i in range(size)])]
    ppermute x6 -> x8, waiting for transfers between devices: 8.62 us -> 9.72 us  [shifted(): lax.ppermute(value, 'dp', [(i, (i + step) % size) for i in range(size)])]
  transfers between devices with their start and end apart: 6 -> 8, of which waited for: 4 -> 4; matrix products, arithmetic and copies ran while one was open for 2% -> 2% of each run, Pallas kernels for 0% -> 0%
where the time goes in v5:
time: 144 us; the launch traced here: 143 us
  blocking collectives  82.9 us (58%)
  starting transfers between devices  42.3 us (29%)
  waiting for transfers between devices  9.72 us (7%)
  Pallas kernels  5.52 us (4%)
    ppermute x8, starting transfers between devices, shifted(): lax.ppermute(value, 'dp', [(i, (i + step) % size) for i in range(size)])  42.3 us
    all_to_all x1, blocking collectives, body(): lax.all_to_all(combine(residue, by_residue, pieces), 'dp', 0, 0, tiled=Tr...  24.9 us
    all_to_all x1, blocking collectives, body(): lax.all_to_all(outgoing.reshape(owners, CAP, row_count, block_width), 'sh...  22.1 us
    all_gather x1, blocking collectives, body(): lax.all_gather(chosen, 'dp', axis=0, tiled=False, axis_index_groups=strid...  18 us
    all_to_all x1, blocking collectives, body(): returned = lax.all_to_all(fresh, 'shard', 0, 0, tiled=True)  17.8 us
    ppermute x8, waiting for transfers between devices, shifted(): lax.ppermute(value, 'dp', [(i, (i + step) % size) for i in range(size)])  9.72 us
  transfers between devices with their start and end apart: 8, of which 4 were waited for; matrix products, arithmetic and copies ran while one was open for 2% of the time, Pallas kernels for 0%

profile of v5, /device:TPU:6, one launch (start us, length us, event | category | flops | bytes accessed | tf_op | source)
XLA Modules:
  0.0 143.4 jit_solution(5697964846223982438)
XLA Ops:
  0.0 0.0 copy-start
  0.0 0.0 copy-start.2
  0.0 1.2 part.1
  1.2 6.1 %collective-permute-start.2 = (bf16[2,32,4,256]{3,2,1,0:T(4,128)(2,1)S(1)}, bf16[2,32,4,256]{3,2,1,0:T(4,128)(2,1)S(1)}, u32[]{:S(2)}, u32[]{:S(2)}) collective-permute-start(bf16[2,32,4,256]{3,2,1,0:T(4,128)(2,1)S(1)} %get-tuple-element.19), channel_id=1, source_target_pairs={{0,128},{64,192},{128,256},{192,320},{256,384},{320,448},{384,512}... | collective-permute-start | bytes 393224 | tf_op jit(solution)/shard_map/ppermute | solution.py:226
  7.3 14.0 %collective-permute-start.3 = (bf16[2,32,4,256]{3,2,1,0:T(4,128)(2,1)S(1)}, bf16[2,32,4,256]{3,2,1,0:T(4,128)(2,1)S(1)}, u32[]{:S(2)}, u32[]{:S(2)}) collective-permute-start(bf16[2,32,4,256]{3,2,1,0:T(4,128)(2,1)S(1)} %get-tuple-element.20), channel_id=1, source_target_pairs={{0,896},{64,960},{128,0},{192,64},{256,128},{320,192},{384,256},{4... | collective-permute-start | bytes 393224 | tf_op jit(solution)/shard_map/ppermute | solution.py:226
  21.4 3.4 %collective-permute-start = (bf16[4,32,4,256]{3,2,1,0:T(4,128)(2,1)S(1)}, bf16[4,32,4,256]{3,2,1,0:T(4,128)(2,1)S(1)}, u32[]{:S(2)}, u32[]{:S(2)}) collective-permute-start(bf16[4,32,4,256]{3,2,1,0:T(4,128)(2,1)S(1)} %get-tuple-element.17), channel_id=1, source_target_pairs={{0,64},{64,128},{128,192},{192,256},{256,320},{320,384},{384,448},... | collective-permute-start | bytes 786440 | tf_op jit(solution)/shard_map/ppermute | solution.py:226
  24.7 3.7 %collective-permute-start.1 = (bf16[4,32,4,256]{3,2,1,0:T(4,128)(2,1)S(1)}, bf16[4,32,4,256]{3,2,1,0:T(4,128)(2,1)S(1)}, u32[]{:S(2)}, u32[]{:S(2)}) collective-permute-start(bf16[4,32,4,256]{3,2,1,0:T(4,128)(2,1)S(1)} %get-tuple-element.18), channel_id=1, source_target_pairs={{0,960},{64,0},{128,64},{192,128},{256,192},{320,256},{384,320},{4... | collective-permute-start | bytes 786440 | tf_op jit(solution)/shard_map/ppermute | solution.py:226
  28.4 0.0 copy-done
  28.5 0.7 dynamic-slice_bitcast_fusion
  29.2 0.1 lt.41
  29.2 0.1 lt.42
  29.4 0.0 copy-done.2
  29.4 0.0 copy-start.1
  29.4 1.2 broadcast_multiply_fusion
  30.6 0.1 select_reduce_fusion
  30.8 0.0 collective-permute-done.2.far_up_ref
  30.8 0.0 collective-permute-done.3.far_down_ref
  30.8 1.4 %collective-permute-done.up_ref = bf16[4,32,4,256]{3,2,1,0:T(4,128)(2,1)S(1)} collective-permute-done((bf16[4,32,4,256]{3,2,1,0:T(4,128)(2,1)S(1)}, bf16[4,32,4,256]{3,2,1,0:T(4,128)(2,1)S(1)}, u32[]{:S(2)}, u32[]{:S(2)}) %collective-permute-start) | collective-permute-done | bytes 262176 | tf_op jit(solution)/shard_map/ppermute | solution.py:226
  32.2 1.9 %collective-permute-done.1.down_ref = bf16[4,32,4,256]{3,2,1,0:T(4,128)(2,1)S(1)} collective-permute-done((bf16[4,32,4,256]{3,2,1,0:T(4,128)(2,1)S(1)}, bf16[4,32,4,256]{3,2,1,0:T(4,128)(2,1)S(1)}, u32[]{:S(2)}, u32[]{:S(2)}) %collective-permute-start.1) | collective-permute-done | bytes 262176 | tf_op jit(solution)/shard_map/ppermute | solution.py:226
  34.1 0.0 copy-done.1
  34.1 0.2 combine.1
  34.3 24.9 %all_to_all.15.parts_ref = bf16[4,32,4,256]{3,2,1,0:T(4,128)(2,1)S(1)} all-to-all(bf16[4,32,4,256]{3,2,1,0:T(4,128)(2,1)S(1)} %combine.1), channel_id=1, replica_groups={{0,256,512,768},{64,320,576,832},{128,384,640,896},{192,448,704,960},{1..., dimensions={0} | all-to-all | bytes 524288 | tf_op jit(solution)/shard_map/all_to_all | solution.py:266
  59.2 0.8 sum_and_gather.1
  60.0 22.1 %all_to_all.16 = bf16[64,2,4,256]{3,2,1,0:T(4,128)(2,1)S(1)} all-to-all(bf16[64,2,4,256]{3,2,1,0:T(4,128)(2,1)S(1)} %bitcast.21), channel_id=1, replica_groups=mesh['dp'=16,'shard'=64] {'shard'}, dimensions={0} | all-to-all | bytes 524288 | tf_op jit(solution)/shard_map/all_to_all | solution.py:275
  82.2 0.1 copy.12
  82.3 0.1 reshape.44.arrived_ref
  82.3 1.8 %refresh.1 = bf16[2,256,256]{2,1,0:T(8,128)(2,1)S(1)} custom-call(bf16[2,256,256]{2,1,0:T(8,128)(2,1)S(1)} %reshape.44.arrived_ref, f32[2,256,256]{2,1,0:T(8,128)S(1)} %get-tuple-element.27.left_ref, f32[2,256,256]{2,1,0:T(8,128)S(1)} %get-tuple-element.28.right_ref), custom_call_target="tpu_custom_call" | custom-call | flops 805306368 | bytes 1572864 | tf_op jit(solution)/shard_map/refresh/pallas_call | solution.py:64
  84.1 0.1 reshape.45
  84.2 0.1 copy.15
  84.3 17.8 %all_to_all.17 = bf16[64,2,4,256]{3,2,1,0:T(4,128)(2,1)S(1)} all-to-all(bf16[64,2,4,256]{3,2,1,0:T(4,128)(2,1)S(1)} %bitcast.24), channel_id=1, replica_groups=mesh['dp'=16,'shard'=64] {'shard'}, dimensions={0} | all-to-all | bytes 524288 | tf_op jit(solution)/shard_map/all_to_all | solution.py:281
  102.1 0.6 choose.1
  102.7 18.0 %all-gather = bf16[128,4,256]{2,1,0:T(4,128)(2,1)S(1)} all-gather(bf16[32,4,256]{2,1,0:T(4,128)(2,1)S(1)} %choose.1), channel_id=2, replica_groups={{0,256,512,768},{64,320,576,832},{128,384,640,896},{192,448,704,960},{1..., dimensions={0}, use_global_device_ids=true | all-gather | bytes 327680 | tf_op jit(solution)/shard_map/all_gather | solution.py:283
  120.7 4.2 %collective-permute-start.5 = (bf16[4,32,4,256]{3,2,1,0:T(4,128)(2,1)S(1)}, bf16[4,32,4,256]{3,2,1,0:T(4,128)(2,1)S(1)}, u32[]{:S(2)}, u32[]{:S(2)}) collective-permute-start(bf16[4,32,4,256]{3,2,1,0:T(4,128)(2,1)S(1)} %bitcast.18), channel_id=1, source_target_pairs={{0,64},{64,128},{128,192},{192,256},{256,320},{320,384},{384,448},... | collective-permute-start | bytes 786440 | tf_op jit(solution)/shard_map/ppermute | solution.py:226
  124.9 3.0 %collective-permute-start.4 = (bf16[4,32,4,256]{3,2,1,0:T(4,128)(2,1)S(1)}, bf16[4,32,4,256]{3,2,1,0:T(4,128)(2,1)S(1)}, u32[]{:S(2)}, u32[]{:S(2)}) collective-permute-start(bf16[4,32,4,256]{3,2,1,0:T(4,128)(2,1)S(1)} %bitcast.19), channel_id=1, source_target_pairs={{0,960},{64,0},{128,64},{192,128},{256,192},{320,256},{384,320},{4... | collective-permute-start | bytes 786440 | tf_op jit(solution)/shard_map/ppermute | solution.py:226
  127.9 0.1 fusion.2
  128.0 4.7 %collective-permute-start.6 = (bf16[2,32,4,256]{3,2,1,0:T(4,128)(2,1)S(1)}, bf16[2,32,4,256]{3,2,1,0:T(4,128)(2,1)S(1)}, u32[]{:S(2)}, u32[]{:S(2)}) collective-permute-start(bf16[2,32,4,256]{3,2,1,0:T(4,128)(2,1)S(1)} %bitcast.26), channel_id=1, source_target_pairs={{0,128},{64,192},{128,256},{192,320},{256,384},{320,448},{384,512}... | collective-permute-start | bytes 393224 | tf_op jit(solution)/shard_map/ppermute | solution.py:226
  132.7 3.3 %collective-permute-start.7 = (bf16[2,32,4,256]{3,2,1,0:T(4,128)(2,1)S(1)}, bf16[2,32,4,256]{3,2,1,0:T(4,128)(2,1)S(1)}, u32[]{:S(2)}, u32[]{:S(2)}) collective-permute-start(bf16[2,32,4,256]{3,2,1,0:T(4,128)(2,1)S(1)} %bitcast.25), channel_id=1, source_target_pairs={{0,896},{64,960},{128,0},{192,64},{256,128},{320,192},{384,256},{4... | collective-permute-start | bytes 393224 | tf_op jit(solution)/shard_map/ppermute | solution.py:226
  136.0 4.0 %collective-permute-done.6.far_low_ref = bf16[2,32,4,256]{3,2,1,0:T(4,128)(2,1)S(1)} collective-permute-done((bf16[2,32,4,256]{3,2,1,0:T(4,128)(2,1)S(1)}, bf16[2,32,4,256]{3,2,1,0:T(4,128)(2,1)S(1)}, u32[]{:S(2)}, u32[]{:S(2)}) %collective-permute-start.6) | collective-permute-done | bytes 131104 | tf_op jit(solution)/shard_map/ppermute | solution.py:226
  140.0 2.4 %collective-permute-done.7.far_high_ref = bf16[2,32,4,256]{3,2,1,0:T(4,128)(2,1)S(1)} collective-permute-done((bf16[2,32,4,256]{3,2,1,0:T(4,128)(2,1)S(1)}, bf16[2,32,4,256]{3,2,1,0:T(4,128)(2,1)S(1)}, u32[]{:S(2)}, u32[]{:S(2)}) %collective-permute-start.7) | collective-permute-done | bytes 131104 | tf_op jit(solution)/shard_map/ppermute | solution.py:226
  142.4 0.0 collective-permute-done.5.below_ref
  142.4 0.0 collective-permute-done.4.above_ref
  142.4 1.0 place.1
  (3 shorter events, 0.0 us)
Async XLA Ops:
  0.0 28.4 %copy-start = (s32[16,128]{1,0:T(8,128)S(1)}, s32[16,128]{1,0:T(8,128)}, u32[]{:S(2)}) copy-start(s32[16,128]{1,0:T(8,128)} %param.6) | copy-start | bytes 24580
  0.0 29.4 %copy-start.2 = (f32[2,256,256]{2,1,0:T(8,128)S(1)}, f32[2,256,256]{2,1,0:T(8,128)}, u32[]{:S(2)}) copy-start(f32[2,256,256]{2,1,0:T(8,128)} %param.9) | copy-start | bytes 1572868
  1.2 29.6 %collective-permute-start.2 = (bf16[2,32,4,256]{3,2,1,0:T(4,128)(2,1)S(1)}, bf16[2,32,4,256]{3,2,1,0:T(4,128)(2,1)S(1)}, u32[]{:S(2)}, u32[]{:S(2)}) collective-permute-start(bf16[2,32,4,256]{3,2,1,0:T(4,128)(2,1)S(1)} %get-tuple-element.19), channel_id=1, source_target_pairs={{0,128},{64,192},{128,256},{192,320},{256,384},{320,448},{384,512}... | collective-permute-start | bytes 393224 | tf_op jit(solution)/shard_map/ppermute | solution.py:226
  7.3 23.5 %collective-permute-start.3 = (bf16[2,32,4,256]{3,2,1,0:T(4,128)(2,1)S(1)}, bf16[2,32,4,256]{3,2,1,0:T(4,128)(2,1)S(1)}, u32[]{:S(2)}, u32[]{:S(2)}) collective-permute-start(bf16[2,32,4,256]{3,2,1,0:T(4,128)(2,1)S(1)} %get-tuple-element.20), channel_id=1, source_target_pairs={{0,896},{64,960},{128,0},{192,64},{256,128},{320,192},{384,256},{4... | collective-permute-start | bytes 393224 | tf_op jit(solution)/shard_map/ppermute | solution.py:226
  21.4 10.9 %collective-permute-start = (bf16[4,32,4,256]{3,2,1,0:T(4,128)(2,1)S(1)}, bf16[4,32,4,256]{3,2,1,0:T(4,128)(2,1)S(1)}, u32[]{:S(2)}, u32[]{:S(2)}) collective-permute-start(bf16[4,32,4,256]{3,2,1,0:T(4,128)(2,1)S(1)} %get-tuple-element.17), channel_id=1, source_target_pairs={{0,64},{64,128},{128,192},{192,256},{256,320},{320,384},{384,448},... | collective-permute-start | bytes 786440 | tf_op jit(solution)/shard_map/ppermute | solution.py:226
  24.7 9.4 %collective-permute-start.1 = (bf16[4,32,4,256]{3,2,1,0:T(4,128)(2,1)S(1)}, bf16[4,32,4,256]{3,2,1,0:T(4,128)(2,1)S(1)}, u32[]{:S(2)}, u32[]{:S(2)}) collective-permute-start(bf16[4,32,4,256]{3,2,1,0:T(4,128)(2,1)S(1)} %get-tuple-element.18), channel_id=1, source_target_pairs={{0,960},{64,0},{128,64},{192,128},{256,192},{320,256},{384,320},{4... | collective-permute-start | bytes 786440 | tf_op jit(solution)/shard_map/ppermute | solution.py:226
  29.4 4.7 %copy-start.1 = (bf16[1,512,4,256]{3,2,1,0:T(4,128)(2,1)S(1)}, bf16[1,512,4,256]{3,2,1,0:T(4,128)(2,1)}, u32[]{:S(2)}) copy-start(bf16[1,512,4,256]{3,2,1,0:T(4,128)(2,1)} %param.5) | copy-start | bytes 3145732
  120.7 21.7 %collective-permute-start.5 = (bf16[4,32,4,256]{3,2,1,0:T(4,128)(2,1)S(1)}, bf16[4,32,4,256]{3,2,1,0:T(4,128)(2,1)S(1)}, u32[]{:S(2)}, u32[]{:S(2)}) collective-permute-start(bf16[4,32,4,256]{3,2,1,0:T(4,128)(2,1)S(1)} %bitcast.18), channel_id=1, source_target_pairs={{0,64},{64,128},{128,192},{192,256},{256,320},{320,384},{384,448},... | collective-permute-start | bytes 786440 | tf_op jit(solution)/shard_map/ppermute | solution.py:226
  124.9 17.5 %collective-permute-start.4 = (bf16[4,32,4,256]{3,2,1,0:T(4,128)(2,1)S(1)}, bf16[4,32,4,256]{3,2,1,0:T(4,128)(2,1)S(1)}, u32[]{:S(2)}, u32[]{:S(2)}) collective-permute-start(bf16[4,32,4,256]{3,2,1,0:T(4,128)(2,1)S(1)} %bitcast.19), channel_id=1, source_target_pairs={{0,960},{64,0},{128,64},{192,128},{256,192},{320,256},{384,320},{4... | collective-permute-start | bytes 786440 | tf_op jit(solution)/shard_map/ppermute | solution.py:226
  128.0 12.0 %collective-permute-start.6 = (bf16[2,32,4,256]{3,2,1,0:T(4,128)(2,1)S(1)}, bf16[2,32,4,256]{3,2,1,0:T(4,128)(2,1)S(1)}, u32[]{:S(2)}, u32[]{:S(2)}) collective-permute-start(bf16[2,32,4,256]{3,2,1,0:T(4,128)(2,1)S(1)} %bitcast.26), channel_id=1, source_target_pairs={{0,128},{64,192},{128,256},{192,320},{256,384},{320,448},{384,512}... | collective-permute-start | bytes 393224 | tf_op jit(solution)/shard_map/ppermute | solution.py:226
  132.7 9.6 %collective-permute-start.7 = (bf16[2,32,4,256]{3,2,1,0:T(4,128)(2,1)S(1)}, bf16[2,32,4,256]{3,2,1,0:T(4,128)(2,1)S(1)}, u32[]{:S(2)}, u32[]{:S(2)}) collective-permute-start(bf16[2,32,4,256]{3,2,1,0:T(4,128)(2,1)S(1)} %bitcast.25), channel_id=1, source_target_pairs={{0,896},{64,960},{128,0},{192,64},{256,128},{320,192},{384,256},{4... | collective-permute-start | bytes 393224 | tf_op jit(solution)/shard_map/ppermute | solution.py:226

commit v6 on v5

--- a/solution.py
+++ b/solution.py
@@ -74,20 +74,15 @@
     )(arrived, prev_left, prev_right)
 
 
-def part_kernel(place_ref, grads_ref, up_ref, down_ref, far_up_ref, far_down_ref, sems):
+def part_kernel(place_ref, grads_ref, up_ref, down_ref, far_ref, sems):
     residue = place_ref[0]
-    half = far_up_ref.shape[0]
-    pieces = (
-        (slice(None), 1, up_ref),
-        (slice(None), RADIX - 1, down_ref),
-        (slice(0, half), 2, far_up_ref),
-        (slice(half, None), 2, far_down_ref),
-    )
     copies = [
         pltpu.make_async_copy(
-            grads_ref.at[where, (residue + step) % RADIX], piece_ref, sems.at[index]
-        )
-        for index, (where, step, piece_ref) in enumerate(pieces)
+            grads_ref.at[:, (residue + step) % RADIX], piece_ref, sems.at[index]
+        )
+        for index, (step, piece_ref) in enumerate(
+            ((1, up_ref), (RADIX - 1, down_ref), (2, far_ref))
+        )
     ]
     for copy in copies:
         copy.start()
@@ -96,31 +91,27 @@
 
 
 def part(residue, by_residue):
-    count = by_residue.shape[0]
-    pieces = [
-        jax.ShapeDtypeStruct((size,) + by_residue.shape[2:], jnp.bfloat16)
-        for size in (count, count, count // 2, count // 2)
-    ]
+    piece = jax.ShapeDtypeStruct(
+        by_residue.shape[:1] + by_residue.shape[2:], jnp.bfloat16
+    )
     return pl.pallas_call(
         part_kernel,
         in_specs=[pl.BlockSpec(memory_space=pltpu.SMEM), pl.BlockSpec(memory_space=pltpu.HBM)],
-        out_shape=pieces,
-        out_specs=[pl.BlockSpec(memory_space=pltpu.VMEM)] * 4,
-        scratch_shapes=[pltpu.SemaphoreType.DMA((4,))],
+        out_shape=[piece] * 3,
+        out_specs=[pl.BlockSpec(memory_space=pltpu.VMEM)] * 3,
+        scratch_shapes=[pltpu.SemaphoreType.DMA((3,))],
         compiler_params=pltpu.CompilerParams(vmem_limit_bytes=VMEM_GRANT),
         name="part",
     )(residue, pltpu.with_memory_space_constraint(by_residue, pltpu.HBM))
 
 
-def combine_kernel(place_ref, grads_ref, up_ref, down_ref, far_up_ref, far_down_ref, out_ref):
+def combine_kernel(place_ref, grads_ref, up_ref, down_ref, far_ref, out_ref):
     residue = place_ref[0]
-    half = far_up_ref.shape[0]
-    for index in range(2 * half):
-        far_ref = far_up_ref if index < half else far_down_ref
+    for index in range(out_ref.shape[0]):
         total = grads_ref[index, residue].astype(jnp.float32)
         total += up_ref[index].astype(jnp.float32)
         total += down_ref[index].astype(jnp.float32)
-        total += far_ref[index % half].astype(jnp.float32)
+        total += far_ref[index].astype(jnp.float32)
         out_ref[index] = total.astype(jnp.bfloat16)
 
 
@@ -128,7 +119,7 @@
     return pl.pallas_call(
         combine_kernel,
         in_specs=[pl.BlockSpec(memory_space=pltpu.SMEM)]
-        + [pl.BlockSpec(memory_space=pltpu.VMEM)] * 5,
+        + [pl.BlockSpec(memory_space=pltpu.VMEM)] * 4,
         out_shape=jax.ShapeDtypeStruct(pieces[0].shape, jnp.bfloat16),
         compiler_params=pltpu.CompilerParams(vmem_limit_bytes=VMEM_GRANT),
         name="combine",
@@ -183,23 +174,15 @@
     )(picks, returned)
 
 
-def place_kernel(
-    place_ref, same_ref, above_ref, below_ref, far_low_ref, far_high_ref, out_ref, sems
-):
+def place_kernel(place_ref, same_ref, above_ref, below_ref, far_ref, out_ref, sems):
     residue = place_ref[0]
-    half = far_low_ref.shape[0]
-    pieces = (
-        (slice(None), 0, same_ref),
-        (slice(None), 1, above_ref),
-        (slice(None), RADIX - 1, below_ref),
-        (slice(0, half), 2, far_low_ref),
-        (slice(half, None), 2, far_high_ref),
-    )
     copies = [
         pltpu.make_async_copy(
-            piece_ref, out_ref.at[where, (residue + step) % RADIX], sems.at[index]
-        )
-        for index, (where, step, piece_ref) in enumerate(pieces)
+            piece_ref, out_ref.at[:, (residue + step) % RADIX], sems.at[index]
+        )
+        for index, (step, piece_ref) in enumerate(
+            ((0, same_ref), (1, above_ref), (RADIX - 1, below_ref), (2, far_ref))
+        )
     ]
     for copy in copies:
         copy.start()
@@ -212,10 +195,10 @@
     return pl.pallas_call(
         place_kernel,
         in_specs=[pl.BlockSpec(memory_space=pltpu.SMEM)]
-        + [pl.BlockSpec(memory_space=pltpu.VMEM)] * 5,
+        + [pl.BlockSpec(memory_space=pltpu.VMEM)] * 4,
         out_specs=pl.BlockSpec(memory_space=pl.ANY),
         out_shape=jax.ShapeDtypeStruct(shape, jnp.bfloat16),
-        scratch_shapes=[pltpu.SemaphoreType.DMA((5,))],
+        scratch_shapes=[pltpu.SemaphoreType.DMA((4,))],
         compiler_params=pltpu.CompilerParams(vmem_limit_bytes=VMEM_GRANT),
         name="place",
     )(residue, same, *others)
@@ -224,6 +207,12 @@
 def shifted(value, step):
     size = lax.axis_size("dp")
     return lax.ppermute(value, "dp", [(i, (i + step) % size) for i in range(size)])
+
+
+def crossed(value):
+    size = lax.axis_size("dp")
+    pairs = [(i, (i + (-2 if i % 2 else 2)) % size) for i in range(size)]
+    return lax.ppermute(value, "dp", pairs)
 
 
 def strided(size, stride):
@@ -238,7 +227,6 @@
     row_count = grads.shape[2]
     block_width = grads.shape[3]
     per_group = blocks // groups
-    half = groups // RADIX // 2
     slot_total = owners * CAP
     slot_ids = jnp.arange(slot_total, dtype=jnp.int32)
     my_table = lax.dynamic_index_in_dim(owner_table, my_group, 0, keepdims=False)
@@ -253,10 +241,10 @@
 
     residue = (my_group % RADIX).reshape(1)
     by_residue = grads.reshape(groups // RADIX, RADIX, per_group, row_count, block_width)
-    up, down, far_up, far_down = part(residue, by_residue)
+    up, down, far = part(residue, by_residue)
     pieces, my_table, picks, old_left, old_right = lax.optimization_barrier(
         (
-            (shifted(up, 1), shifted(down, -1), shifted(far_up, 2), shifted(far_down, -2)),
+            (shifted(up, 1), shifted(down, -1), crossed(far)),
             my_table,
             picks,
             stat_decay * prev_left,
@@ -283,14 +271,7 @@
     same = lax.all_gather(
         chosen, "dp", axis=0, tiled=False, axis_index_groups=strided(groups, RADIX)
     )
-    placed = place(
-        residue,
-        same,
-        shifted(same, -1),
-        shifted(same, 1),
-        shifted(same[:half], 2),
-        shifted(same[half:], -2),
-    )
+    placed = place(residue, same, shifted(same, -1), shifted(same, 1), crossed(same))
     return placed.reshape(blocks, row_count, block_width)
 
 

time: 144 us -> 137 us (0.951)
  starting transfers between devices: 42.3 us -> 31.5 us
  waiting for transfers between devices: 9.72 us -> 13.6 us
    ppermute x8 -> x4, starting transfers between devices: 42.3 us -> 27.4 us  [shifted(): lax.ppermute(value, 'dp', [(i, (i + step) % size) for i in range(size)])]
    ppermute x0 -> x2, starting transfers between devices: none -> 4.09 us  [crossed(): return lax.ppermute(value, 'dp', pairs)]
    ppermute x0 -> x2, waiting for transfers between devices: none -> 3.73 us  [crossed(): return lax.ppermute(value, 'dp', pairs)]
    all_to_all x1, blocking collectives: 24.9 us -> 23.2 us  [body(): lax.all_to_all(combine(residue, by_residue, pieces), 'dp', 0, 0, tiled=Tr...]
    all_gather x1, blocking collectives: 18 us -> 19.6 us  [body(): lax.all_gather(chosen, 'dp', axis=0, tiled=False, axis_index_groups=strid...]
    ppermute x8 -> x4, waiting for transfers between devices: 9.72 us -> 9.9 us  [shifted(): lax.ppermute(value, 'dp', [(i, (i + step) % size) for i in range(size)])]
  transfers between devices with their start and end apart: 8 -> 6, of which waited for: 4 -> 6; matrix products, arithmetic and copies ran while one was open for 2% -> 2% of each run, Pallas kernels for 0% -> 0%
where the time goes in v6:
time: 137 us; the launch traced here: 136 us
  blocking collectives  82.8 us (60%)
  starting transfers between devices  31.5 us (23%)
  waiting for transfers between devices  13.6 us (10%)
  Pallas kernels  5.51 us (4%)
    ppermute x4, starting transfers between devices, shifted(): lax.ppermute(value, 'dp', [(i, (i + step) % size) for i in range(size)])  27.4 us
    all_to_all x1, blocking collectives, body(): lax.all_to_all(combine(residue, by_residue, pieces), 'dp', 0, 0, tiled=Tr...  23.2 us
    all_to_all x1, blocking collectives, body(): lax.all_to_all(outgoing.reshape(owners, CAP, row_count, block_width), 'sh...  22.2 us
    all_gather x1, blocking collectives, body(): lax.all_gather(chosen, 'dp', axis=0, tiled=False, axis_index_groups=strid...  19.6 us
    all_to_all x1, blocking collectives, body(): returned = lax.all_to_all(fresh, 'shard', 0, 0, tiled=True)  17.8 us
    ppermute x4, waiting for transfers between devices, shifted(): lax.ppermute(value, 'dp', [(i, (i + step) % size) for i in range(size)])  9.9 us
    ppermute x2, starting transfers between devices, crossed(): return lax.ppermute(value, 'dp', pairs)  4.09 us
    ppermute x2, waiting for transfers between devices, crossed(): return lax.ppermute(value, 'dp', pairs)  3.73 us
  transfers between devices with their start and end apart: 6, of which 6 were waited for; matrix products, arithmetic and copies ran while one was open for 2% of the time, Pallas kernels for 0%

profile of v6, /device:TPU:6, one launch (start us, length us, event | category | flops | bytes accessed | tf_op | source)
XLA Modules:
  0.0 136.2 jit_solution(13783319378472430417)
XLA Ops:
  0.0 0.0 copy-start
  0.0 0.0 copy-start.2
  0.0 1.2 part.1
  1.2 4.3 %collective-permute-start = (bf16[4,32,4,256]{3,2,1,0:T(4,128)(2,1)S(1)}, bf16[4,32,4,256]{3,2,1,0:T(4,128)(2,1)S(1)}, u32[]{:S(2)}, u32[]{:S(2)}) collective-permute-start(bf16[4,32,4,256]{3,2,1,0:T(4,128)(2,1)S(1)} %get-tuple-element.15), channel_id=1, source_target_pairs={{0,64},{64,128},{128,192},{192,256},{256,320},{320,384},{384,448},... | collective-permute-start | bytes 786440 | tf_op jit(solution)/shard_map/ppermute | solution.py:209
  5.5 15.9 %collective-permute-start.1 = (bf16[4,32,4,256]{3,2,1,0:T(4,128)(2,1)S(1)}, bf16[4,32,4,256]{3,2,1,0:T(4,128)(2,1)S(1)}, u32[]{:S(2)}, u32[]{:S(2)}) collective-permute-start(bf16[4,32,4,256]{3,2,1,0:T(4,128)(2,1)S(1)} %get-tuple-element.16), channel_id=1, source_target_pairs={{0,960},{64,0},{128,64},{192,128},{256,192},{320,256},{384,320},{4... | collective-permute-start | bytes 786440 | tf_op jit(solution)/shard_map/ppermute | solution.py:209
  21.4 1.9 %collective-permute-start.2 = (bf16[4,32,4,256]{3,2,1,0:T(4,128)(2,1)S(1)}, bf16[4,32,4,256]{3,2,1,0:T(4,128)(2,1)S(1)}, u32[]{:S(2)}, u32[]{:S(2)}) collective-permute-start(bf16[4,32,4,256]{3,2,1,0:T(4,128)(2,1)S(1)} %get-tuple-element.17), channel_id=1, source_target_pairs={{0,128},{64,960},{128,256},{192,64},{256,384},{320,192},{384,512},... | collective-permute-start | bytes 786440 | tf_op jit(solution)/shard_map/ppermute | solution.py:215
  23.3 0.0 copy-done
  23.3 0.7 dynamic-slice_bitcast_fusion
  24.0 0.1 lt.41
  24.1 0.1 lt.42
  24.3 0.1 select_reduce_fusion
  24.4 0.0 copy-done.2
  24.4 0.0 copy-start.1
  24.4 1.2 broadcast_multiply_fusion
  25.6 0.1 collective-permute-done.up_ref
  25.7 6.8 %collective-permute-done.1.down_ref = bf16[4,32,4,256]{3,2,1,0:T(4,128)(2,1)S(1)} collective-permute-done((bf16[4,32,4,256]{3,2,1,0:T(4,128)(2,1)S(1)}, bf16[4,32,4,256]{3,2,1,0:T(4,128)(2,1)S(1)}, u32[]{:S(2)}, u32[]{:S(2)}) %collective-permute-start.1) | collective-permute-done | bytes 262176 | tf_op jit(solution)/shard_map/ppermute | solution.py:209
  32.5 0.6 collective-permute-done.2.far_ref
  33.1 0.0 copy-done.1
  33.1 0.2 combine.1
  33.3 23.2 %all_to_all.15.parts_ref = bf16[4,32,4,256]{3,2,1,0:T(4,128)(2,1)S(1)} all-to-all(bf16[4,32,4,256]{3,2,1,0:T(4,128)(2,1)S(1)} %combine.1), channel_id=1, replica_groups={{0,256,512,768},{64,320,576,832},{128,384,640,896},{192,448,704,960},{1..., dimensions={0} | all-to-all | bytes 524288 | tf_op jit(solution)/shard_map/all_to_all | solution.py:254
  56.5 0.8 sum_and_gather.1
  57.3 22.2 %all_to_all.16 = bf16[64,2,4,256]{3,2,1,0:T(4,128)(2,1)S(1)} all-to-all(bf16[64,2,4,256]{3,2,1,0:T(4,128)(2,1)S(1)} %bitcast.20), channel_id=1, replica_groups=mesh['dp'=16,'shard'=64] {'shard'}, dimensions={0} | all-to-all | bytes 524288 | tf_op jit(solution)/shard_map/all_to_all | solution.py:263
  79.5 0.1 copy.12
  79.6 0.1 reshape.44.arrived_ref
  79.7 1.8 %refresh.1 = bf16[2,256,256]{2,1,0:T(8,128)(2,1)S(1)} custom-call(bf16[2,256,256]{2,1,0:T(8,128)(2,1)S(1)} %reshape.44.arrived_ref, f32[2,256,256]{2,1,0:T(8,128)S(1)} %get-tuple-element.23.left_ref, f32[2,256,256]{2,1,0:T(8,128)S(1)} %get-tuple-element.24.right_ref), custom_call_target="tpu_custom_call" | custom-call | flops 805306368 | bytes 1572864 | tf_op jit(solution)/shard_map/refresh/pallas_call | solution.py:64
  81.4 0.1 reshape.45
  81.5 0.1 copy.15
  81.6 17.8 %all_to_all.17 = bf16[64,2,4,256]{3,2,1,0:T(4,128)(2,1)S(1)} all-to-all(bf16[64,2,4,256]{3,2,1,0:T(4,128)(2,1)S(1)} %bitcast.23), channel_id=1, replica_groups=mesh['dp'=16,'shard'=64] {'shard'}, dimensions={0} | all-to-all | bytes 524288 | tf_op jit(solution)/shard_map/all_to_all | solution.py:269
  99.4 0.6 choose.1
  100.0 19.6 %all-gather = bf16[128,4,256]{2,1,0:T(4,128)(2,1)S(1)} all-gather(bf16[32,4,256]{2,1,0:T(4,128)(2,1)S(1)} %choose.1), channel_id=2, replica_groups={{0,256,512,768},{64,320,576,832},{128,384,640,896},{192,448,704,960},{1..., dimensions={0}, use_global_device_ids=true | all-gather | bytes 327680 | tf_op jit(solution)/shard_map/all_gather | solution.py:271
  119.6 2.2 %collective-permute-start.5 = (bf16[4,32,4,256]{3,2,1,0:T(4,128)(2,1)S(1)}, bf16[4,32,4,256]{3,2,1,0:T(4,128)(2,1)S(1)}, u32[]{:S(2)}, u32[]{:S(2)}) collective-permute-start(bf16[4,32,4,256]{3,2,1,0:T(4,128)(2,1)S(1)} %bitcast.16), channel_id=1, source_target_pairs={{0,128},{64,960},{128,256},{192,64},{256,384},{320,192},{384,512},... | collective-permute-start | bytes 786440 | tf_op jit(solution)/shard_map/ppermute | solution.py:215
  121.8 5.1 %collective-permute-start.4 = (bf16[4,32,4,256]{3,2,1,0:T(4,128)(2,1)S(1)}, bf16[4,32,4,256]{3,2,1,0:T(4,128)(2,1)S(1)}, u32[]{:S(2)}, u32[]{:S(2)}) collective-permute-start(bf16[4,32,4,256]{3,2,1,0:T(4,128)(2,1)S(1)} %bitcast.17), channel_id=1, source_target_pairs={{0,64},{64,128},{128,192},{192,256},{256,320},{320,384},{384,448},... | collective-permute-start | bytes 786440 | tf_op jit(solution)/shard_map/ppermute | solution.py:209
  126.9 2.1 %collective-permute-start.3 = (bf16[4,32,4,256]{3,2,1,0:T(4,128)(2,1)S(1)}, bf16[4,32,4,256]{3,2,1,0:T(4,128)(2,1)S(1)}, u32[]{:S(2)}, u32[]{:S(2)}) collective-permute-start(bf16[4,32,4,256]{3,2,1,0:T(4,128)(2,1)S(1)} %bitcast.18), channel_id=1, source_target_pairs={{0,960},{64,0},{128,64},{192,128},{256,192},{320,256},{384,320},{4... | collective-permute-start | bytes 786440 | tf_op jit(solution)/shard_map/ppermute | solution.py:209
  129.1 3.1 %collective-permute-done.5.far_ref = bf16[4,32,4,256]{3,2,1,0:T(4,128)(2,1)S(1)} collective-permute-done((bf16[4,32,4,256]{3,2,1,0:T(4,128)(2,1)S(1)}, bf16[4,32,4,256]{3,2,1,0:T(4,128)(2,1)S(1)}, u32[]{:S(2)}, u32[]{:S(2)}) %collective-permute-start.5) | collective-permute-done | bytes 262176 | tf_op jit(solution)/shard_map/ppermute | solution.py:215
  132.2 2.8 %collective-permute-done.4.below_ref = bf16[4,32,4,256]{3,2,1,0:T(4,128)(2,1)S(1)} collective-permute-done((bf16[4,32,4,256]{3,2,1,0:T(4,128)(2,1)S(1)}, bf16[4,32,4,256]{3,2,1,0:T(4,128)(2,1)S(1)}, u32[]{:S(2)}, u32[]{:S(2)}) %collective-permute-start.4) | collective-permute-done | bytes 262176 | tf_op jit(solution)/shard_map/ppermute | solution.py:209
  135.0 0.2 collective-permute-done.3.above_ref
  135.2 1.0 place.1
  (3 shorter events, 0.0 us)
Async XLA Ops:
  0.0 23.3 %copy-start = (s32[16,128]{1,0:T(8,128)S(1)}, s32[16,128]{1,0:T(8,128)}, u32[]{:S(2)}) copy-start(s32[16,128]{1,0:T(8,128)} %param.6) | copy-start | bytes 24580
  0.0 24.4 %copy-start.2 = (f32[2,256,256]{2,1,0:T(8,128)S(1)}, f32[2,256,256]{2,1,0:T(8,128)}, u32[]{:S(2)}) copy-start(f32[2,256,256]{2,1,0:T(8,128)} %param.9) | copy-start | bytes 1572868
  1.2 24.5 %collective-permute-start = (bf16[4,32,4,256]{3,2,1,0:T(4,128)(2,1)S(1)}, bf16[4,32,4,256]{3,2,1,0:T(4,128)(2,1)S(1)}, u32[]{:S(2)}, u32[]{:S(2)}) collective-permute-start(bf16[4,32,4,256]{3,2,1,0:T(4,128)(2,1)S(1)} %get-tuple-element.15), channel_id=1, source_target_pairs={{0,64},{64,128},{128,192},{192,256},{256,320},{320,384},{384,448},... | collective-permute-start | bytes 786440 | tf_op jit(solution)/shard_map/ppermute | solution.py:209
  5.5 27.0 %collective-permute-start.1 = (bf16[4,32,4,256]{3,2,1,0:T(4,128)(2,1)S(1)}, bf16[4,32,4,256]{3,2,1,0:T(4,128)(2,1)S(1)}, u32[]{:S(2)}, u32[]{:S(2)}) collective-permute-start(bf16[4,32,4,256]{3,2,1,0:T(4,128)(2,1)S(1)} %get-tuple-element.16), channel_id=1, source_target_pairs={{0,960},{64,0},{128,64},{192,128},{256,192},{320,256},{384,320},{4... | collective-permute-start | bytes 786440 | tf_op jit(solution)/shard_map/ppermute | solution.py:209
  21.4 11.8 %collective-permute-start.2 = (bf16[4,32,4,256]{3,2,1,0:T(4,128)(2,1)S(1)}, bf16[4,32,4,256]{3,2,1,0:T(4,128)(2,1)S(1)}, u32[]{:S(2)}, u32[]{:S(2)}) collective-permute-start(bf16[4,32,4,256]{3,2,1,0:T(4,128)(2,1)S(1)} %get-tuple-element.17), channel_id=1, source_target_pairs={{0,128},{64,960},{128,256},{192,64},{256,384},{320,192},{384,512},... | collective-permute-start | bytes 786440 | tf_op jit(solution)/shard_map/ppermute | solution.py:215
  24.4 8.7 %copy-start.1 = (bf16[1,512,4,256]{3,2,1,0:T(4,128)(2,1)S(1)}, bf16[1,512,4,256]{3,2,1,0:T(4,128)(2,1)}, u32[]{:S(2)}) copy-start(bf16[1,512,4,256]{3,2,1,0:T(4,128)(2,1)} %param.5) | copy-start | bytes 3145732
  119.6 12.6 %collective-permute-start.5 = (bf16[4,32,4,256]{3,2,1,0:T(4,128)(2,1)S(1)}, bf16[4,32,4,256]{3,2,1,0:T(4,128)(2,1)S(1)}, u32[]{:S(2)}, u32[]{:S(2)}) collective-permute-start(bf16[4,32,4,256]{3,2,1,0:T(4,128)(2,1)S(1)} %bitcast.16), channel_id=1, source_target_pairs={{0,128},{64,960},{128,256},{192,64},{256,384},{320,192},{384,512},... | collective-permute-start | bytes 786440 | tf_op jit(solution)/shard_map/ppermute | solution.py:215
  121.8 13.2 %collective-permute-start.4 = (bf16[4,32,4,256]{3,2,1,0:T(4,128)(2,1)S(1)}, bf16[4,32,4,256]{3,2,1,0:T(4,128)(2,1)S(1)}, u32[]{:S(2)}, u32[]{:S(2)}) collective-permute-start(bf16[4,32,4,256]{3,2,1,0:T(4,128)(2,1)S(1)} %bitcast.17), channel_id=1, source_target_pairs={{0,64},{64,128},{128,192},{192,256},{256,320},{320,384},{384,448},... | collective-permute-start | bytes 786440 | tf_op jit(solution)/shard_map/ppermute | solution.py:209
  126.9 8.3 %collective-permute-start.3 = (bf16[4,32,4,256]{3,2,1,0:T(4,128)(2,1)S(1)}, bf16[4,32,4,256]{3,2,1,0:T(4,128)(2,1)S(1)}, u32[]{:S(2)}, u32[]{:S(2)}) collective-permute-start(bf16[4,32,4,256]{3,2,1,0:T(4,128)(2,1)S(1)} %bitcast.18), channel_id=1, source_target_pairs={{0,960},{64,0},{128,64},{192,128},{256,192},{320,256},{384,320},{4... | collective-permute-start | bytes 786440 | tf_op jit(solution)/shard_map/ppermute | solution.py:209

commit v7 on v6

--- a/solution.py
+++ b/solution.py
@@ -1,3 +1,5 @@
+import functools
+
 import jax
 import jax.numpy as jnp
 from jax import lax
@@ -74,15 +76,14 @@
     )(arrived, prev_left, prev_right)
 
 
-def part_kernel(place_ref, grads_ref, up_ref, down_ref, far_ref, sems):
+def part_kernel(steps, place_ref, grads_ref, *refs):
     residue = place_ref[0]
+    piece_refs, sems = refs[-1 - len(steps) : -1], refs[-1]
     copies = [
         pltpu.make_async_copy(
             grads_ref.at[:, (residue + step) % RADIX], piece_ref, sems.at[index]
         )
-        for index, (step, piece_ref) in enumerate(
-            ((1, up_ref), (RADIX - 1, down_ref), (2, far_ref))
-        )
+        for index, (step, piece_ref) in enumerate(zip(steps, piece_refs))
     ]
     for copy in copies:
         copy.start()
@@ -90,19 +91,20 @@
         copy.wait()
 
 
-def part(residue, by_residue):
+def part(residue, by_residue, steps, *after):
     piece = jax.ShapeDtypeStruct(
         by_residue.shape[:1] + by_residue.shape[2:], jnp.bfloat16
     )
     return pl.pallas_call(
-        part_kernel,
-        in_specs=[pl.BlockSpec(memory_space=pltpu.SMEM), pl.BlockSpec(memory_space=pltpu.HBM)],
-        out_shape=[piece] * 3,
-        out_specs=[pl.BlockSpec(memory_space=pltpu.VMEM)] * 3,
-        scratch_shapes=[pltpu.SemaphoreType.DMA((3,))],
+        functools.partial(part_kernel, steps),
+        in_specs=[pl.BlockSpec(memory_space=pltpu.SMEM), pl.BlockSpec(memory_space=pltpu.HBM)]
+        + [pl.BlockSpec(memory_space=pl.ANY)] * len(after),
+        out_shape=[piece] * len(steps),
+        out_specs=[pl.BlockSpec(memory_space=pltpu.VMEM)] * len(steps),
+        scratch_shapes=[pltpu.SemaphoreType.DMA((len(steps),))],
         compiler_params=pltpu.CompilerParams(vmem_limit_bytes=VMEM_GRANT),
         name="part",
-    )(residue, pltpu.with_memory_space_constraint(by_residue, pltpu.HBM))
+    )(residue, pltpu.with_memory_space_constraint(by_residue, pltpu.HBM), *after)
 
 
 def combine_kernel(place_ref, grads_ref, up_ref, down_ref, far_ref, out_ref):
@@ -241,7 +243,8 @@
 
     residue = (my_group % RADIX).reshape(1)
     by_residue = grads.reshape(groups // RADIX, RADIX, per_group, row_count, block_width)
-    up, down, far = part(residue, by_residue)
+    (far,) = part(residue, by_residue, (2,))
+    up, down = part(residue, by_residue, (1, RADIX - 1), far)
     pieces, my_table, picks, old_left, old_right = lax.optimization_barrier(
         (
             (shifted(up, 1), shifted(down, -1), crossed(far)),

time: 137 us -> 139 us (1.015)
  starting transfers between devices: 31.5 us -> 37.4 us
  waiting for transfers between devices: 13.6 us -> 8.96 us
    ppermute x2, starting transfers between devices: 4.09 us -> 12.9 us  [crossed(): return lax.ppermute(value, 'dp', pairs)]
    ppermute x2, waiting for transfers between devices: 3.73 us -> 0.01 us  [crossed(): return lax.ppermute(value, 'dp', pairs)]
    ppermute x4, starting transfers between devices: 27.4 us -> 24.5 us  [shifted(): lax.ppermute(value, 'dp', [(i, (i + step) % size) for i in range(size)])]
  transfers between devices with their start and end apart: 6 -> 6, of which waited for: 6 -> 4; matrix products, arithmetic and copies ran while one was open for 2% -> 2% of each run, Pallas kernels for 0% -> 1%
where the time goes in v7:
time: 139 us; the launch traced here: 138 us
  blocking collectives  82.2 us (59%)
  starting transfers between devices  37.4 us (27%)
  waiting for transfers between devices  8.96 us (6%)
  Pallas kernels  6.35 us (5%)
    ppermute x4, starting transfers between devices, shifted(): lax.ppermute(value, 'dp', [(i, (i + step) % size) for i in range(size)])  24.5 us
    all_to_all x1, blocking collectives, body(): lax.all_to_all(combine(residue, by_residue, pieces), 'dp', 0, 0, tiled=Tr...  23.1 us
    all_to_all x1, blocking collectives, body(): lax.all_to_all(outgoing.reshape(owners, CAP, row_count, block_width), 'sh...  22.1 us
    all_gather x1, blocking collectives, body(): lax.all_gather(chosen, 'dp', axis=0, tiled=False, axis_index_groups=strid...  19.1 us
    all_to_all x1, blocking collectives, body(): returned = lax.all_to_all(fresh, 'shard', 0, 0, tiled=True)  17.8 us
    ppermute x2, starting transfers between devices, crossed(): return lax.ppermute(value, 'dp', pairs)  12.9 us
    ppermute x4, waiting for transfers between devices, shifted(): lax.ppermute(value, 'dp', [(i, (i + step) % size) for i in range(size)])  8.96 us
  transfers between devices with their start and end apart: 6, of which 4 were waited for; matrix products, arithmetic and copies ran while one was open for 2% of the time, Pallas kernels for 1%

profile of v7, /device:TPU:6, one launch (start us, length us, event | category | flops | bytes accessed | tf_op | source)
XLA Modules:
  0.0 137.7 jit_solution(12476262595698635630)
XLA Ops:
  0.0 0.0 copy-start
  0.0 1.0 part.2.refs_0_
  1.0 0.0 copy-start.2
  1.0 6.2 %collective-permute-start.2 = (bf16[4,32,4,256]{3,2,1,0:T(4,128)(2,1)S(1)}, bf16[4,32,4,256]{3,2,1,0:T(4,128)(2,1)S(1)}, u32[]{:S(2)}, u32[]{:S(2)}) collective-permute-start(bf16[4,32,4,256]{3,2,1,0:T(4,128)(2,1)S(1)} %part.2.refs_0_), channel_id=1, source_target_pairs={{0,128},{64,960},{128,256},{192,64},{256,384},{320,192},{384,512},... | collective-permute-start | bytes 786440 | tf_op jit(solution)/shard_map/ppermute | solution.py:217
  7.2 1.1 part.3
  8.3 15.5 %collective-permute-start = (bf16[4,32,4,256]{3,2,1,0:T(4,128)(2,1)S(1)}, bf16[4,32,4,256]{3,2,1,0:T(4,128)(2,1)S(1)}, u32[]{:S(2)}, u32[]{:S(2)}) collective-permute-start(bf16[4,32,4,256]{3,2,1,0:T(4,128)(2,1)S(1)} %get-tuple-element.14), channel_id=1, source_target_pairs={{0,64},{64,128},{128,192},{192,256},{256,320},{320,384},{384,448},... | collective-permute-start | bytes 786440 | tf_op jit(solution)/shard_map/ppermute | solution.py:211
  23.8 1.9 %collective-permute-start.1 = (bf16[4,32,4,256]{3,2,1,0:T(4,128)(2,1)S(1)}, bf16[4,32,4,256]{3,2,1,0:T(4,128)(2,1)S(1)}, u32[]{:S(2)}, u32[]{:S(2)}) collective-permute-start(bf16[4,32,4,256]{3,2,1,0:T(4,128)(2,1)S(1)} %get-tuple-element.15), channel_id=1, source_target_pairs={{0,960},{64,0},{128,64},{192,128},{256,192},{320,256},{384,320},{4... | collective-permute-start | bytes 786440 | tf_op jit(solution)/shard_map/ppermute | solution.py:211
  25.7 0.0 copy-done
  25.8 0.7 dynamic-slice_bitcast_fusion
  26.5 0.1 lt.41
  26.5 0.1 lt.42
  26.7 0.1 select_reduce_fusion
  26.8 0.0 copy-done.2
  26.8 0.0 copy-start.1
  26.8 1.2 broadcast_multiply_fusion
  28.1 0.0 collective-permute-done.2.far_ref
  28.1 3.2 %collective-permute-done.up_ref = bf16[4,32,4,256]{3,2,1,0:T(4,128)(2,1)S(1)} collective-permute-done((bf16[4,32,4,256]{3,2,1,0:T(4,128)(2,1)S(1)}, bf16[4,32,4,256]{3,2,1,0:T(4,128)(2,1)S(1)}, u32[]{:S(2)}, u32[]{:S(2)}) %collective-permute-start) | collective-permute-done | bytes 262176 | tf_op jit(solution)/shard_map/ppermute | solution.py:211
  31.3 1.9 %collective-permute-done.1.down_ref = bf16[4,32,4,256]{3,2,1,0:T(4,128)(2,1)S(1)} collective-permute-done((bf16[4,32,4,256]{3,2,1,0:T(4,128)(2,1)S(1)}, bf16[4,32,4,256]{3,2,1,0:T(4,128)(2,1)S(1)}, u32[]{:S(2)}, u32[]{:S(2)}) %collective-permute-start.1) | collective-permute-done | bytes 262176 | tf_op jit(solution)/shard_map/ppermute | solution.py:211
  33.2 0.0 copy-done.1
  33.2 0.2 combine.1
  33.3 23.1 %all_to_all.15.parts_ref = bf16[4,32,4,256]{3,2,1,0:T(4,128)(2,1)S(1)} all-to-all(bf16[4,32,4,256]{3,2,1,0:T(4,128)(2,1)S(1)} %combine.1), channel_id=1, replica_groups={{0,256,512,768},{64,320,576,832},{128,384,640,896},{192,448,704,960},{1..., dimensions={0} | all-to-all | bytes 524288 | tf_op jit(solution)/shard_map/all_to_all | solution.py:257
  56.5 0.8 sum_and_gather.1
  57.3 22.1 %all_to_all.16 = bf16[64,2,4,256]{3,2,1,0:T(4,128)(2,1)S(1)} all-to-all(bf16[64,2,4,256]{3,2,1,0:T(4,128)(2,1)S(1)} %bitcast.21), channel_id=1, replica_groups=mesh['dp'=16,'shard'=64] {'shard'}, dimensions={0} | all-to-all | bytes 524288 | tf_op jit(solution)/shard_map/all_to_all | solution.py:266
  79.4 0.1 copy.12
  79.5 0.1 reshape.44.arrived_ref
  79.6 1.8 %refresh.1 = bf16[2,256,256]{2,1,0:T(8,128)(2,1)S(1)} custom-call(bf16[2,256,256]{2,1,0:T(8,128)(2,1)S(1)} %reshape.44.arrived_ref, f32[2,256,256]{2,1,0:T(8,128)S(1)} %get-tuple-element.21.left_ref, f32[2,256,256]{2,1,0:T(8,128)S(1)} %get-tuple-element.22.right_ref), custom_call_target="tpu_custom_call" | custom-call | flops 805306368 | bytes 1572864 | tf_op jit(solution)/shard_map/refresh/pallas_call | solution.py:66
  81.3 0.1 reshape.45
  81.4 0.1 copy.15
  81.5 17.8 %all_to_all.17 = bf16[64,2,4,256]{3,2,1,0:T(4,128)(2,1)S(1)} all-to-all(bf16[64,2,4,256]{3,2,1,0:T(4,128)(2,1)S(1)} %bitcast.24), channel_id=1, replica_groups=mesh['dp'=16,'shard'=64] {'shard'}, dimensions={0} | all-to-all | bytes 524288 | tf_op jit(solution)/shard_map/all_to_all | solution.py:272
  99.3 0.6 choose.1
  99.9 19.1 %all-gather = bf16[128,4,256]{2,1,0:T(4,128)(2,1)S(1)} all-gather(bf16[32,4,256]{2,1,0:T(4,128)(2,1)S(1)} %choose.1), channel_id=2, replica_groups={{0,256,512,768},{64,320,576,832},{128,384,640,896},{192,448,704,960},{1..., dimensions={0}, use_global_device_ids=true | all-gather | bytes 327680 | tf_op jit(solution)/shard_map/all_gather | solution.py:274
  119.1 6.7 %collective-permute-start.5 = (bf16[4,32,4,256]{3,2,1,0:T(4,128)(2,1)S(1)}, bf16[4,32,4,256]{3,2,1,0:T(4,128)(2,1)S(1)}, u32[]{:S(2)}, u32[]{:S(2)}) collective-permute-start(bf16[4,32,4,256]{3,2,1,0:T(4,128)(2,1)S(1)} %bitcast.17), channel_id=1, source_target_pairs={{0,128},{64,960},{128,256},{192,64},{256,384},{320,192},{384,512},... | collective-permute-start | bytes 786440 | tf_op jit(solution)/shard_map/ppermute | solution.py:217
  125.8 2.0 %collective-permute-start.4 = (bf16[4,32,4,256]{3,2,1,0:T(4,128)(2,1)S(1)}, bf16[4,32,4,256]{3,2,1,0:T(4,128)(2,1)S(1)}, u32[]{:S(2)}, u32[]{:S(2)}) collective-permute-start(bf16[4,32,4,256]{3,2,1,0:T(4,128)(2,1)S(1)} %bitcast.18), channel_id=1, source_target_pairs={{0,64},{64,128},{128,192},{192,256},{256,320},{320,384},{384,448},... | collective-permute-start | bytes 786440 | tf_op jit(solution)/shard_map/ppermute | solution.py:211
  127.8 5.1 %collective-permute-start.3 = (bf16[4,32,4,256]{3,2,1,0:T(4,128)(2,1)S(1)}, bf16[4,32,4,256]{3,2,1,0:T(4,128)(2,1)S(1)}, u32[]{:S(2)}, u32[]{:S(2)}) collective-permute-start(bf16[4,32,4,256]{3,2,1,0:T(4,128)(2,1)S(1)} %bitcast.19), channel_id=1, source_target_pairs={{0,960},{64,0},{128,64},{192,128},{256,192},{320,256},{384,320},{4... | collective-permute-start | bytes 786440 | tf_op jit(solution)/shard_map/ppermute | solution.py:211
  132.9 0.0 collective-permute-done.5.far_ref
  132.9 2.5 %collective-permute-done.4.below_ref = bf16[4,32,4,256]{3,2,1,0:T(4,128)(2,1)S(1)} collective-permute-done((bf16[4,32,4,256]{3,2,1,0:T(4,128)(2,1)S(1)}, bf16[4,32,4,256]{3,2,1,0:T(4,128)(2,1)S(1)}, u32[]{:S(2)}, u32[]{:S(2)}) %collective-permute-start.4) | collective-permute-done | bytes 262176 | tf_op jit(solution)/shard_map/ppermute | solution.py:211
  135.4 1.3 collective-permute-done.3.above_ref
  136.7 1.0 place.1
  (3 shorter events, 0.0 us)
Async XLA Ops:
  0.0 25.7 %copy-start = (s32[16,128]{1,0:T(8,128)S(1)}, s32[16,128]{1,0:T(8,128)}, u32[]{:S(2)}) copy-start(s32[16,128]{1,0:T(8,128)} %param.6) | copy-start | bytes 24580
  1.0 25.8 %copy-start.2 = (f32[2,256,256]{2,1,0:T(8,128)S(1)}, f32[2,256,256]{2,1,0:T(8,128)}, u32[]{:S(2)}) copy-start(f32[2,256,256]{2,1,0:T(8,128)} %param.9) | copy-start | bytes 1572868
  1.0 27.1 %collective-permute-start.2 = (bf16[4,32,4,256]{3,2,1,0:T(4,128)(2,1)S(1)}, bf16[4,32,4,256]{3,2,1,0:T(4,128)(2,1)S(1)}, u32[]{:S(2)}, u32[]{:S(2)}) collective-permute-start(bf16[4,32,4,256]{3,2,1,0:T(4,128)(2,1)S(1)} %part.2.refs_0_), channel_id=1, source_target_pairs={{0,128},{64,960},{128,256},{192,64},{256,384},{320,192},{384,512},... | collective-permute-start | bytes 786440 | tf_op jit(solution)/shard_map/ppermute | solution.py:217
  8.3 23.0 %collective-permute-start = (bf16[4,32,4,256]{3,2,1,0:T(4,128)(2,1)S(1)}, bf16[4,32,4,256]{3,2,1,0:T(4,128)(2,1)S(1)}, u32[]{:S(2)}, u32[]{:S(2)}) collective-permute-start(bf16[4,32,4,256]{3,2,1,0:T(4,128)(2,1)S(1)} %get-tuple-element.14), channel_id=1, source_target_pairs={{0,64},{64,128},{128,192},{192,256},{256,320},{320,384},{384,448},... | collective-permute-start | bytes 786440 | tf_op jit(solution)/shard_map/ppermute | solution.py:211
  23.8 9.4 %collective-permute-start.1 = (bf16[4,32,4,256]{3,2,1,0:T(4,128)(2,1)S(1)}, bf16[4,32,4,256]{3,2,1,0:T(4,128)(2,1)S(1)}, u32[]{:S(2)}, u32[]{:S(2)}) collective-permute-start(bf16[4,32,4,256]{3,2,1,0:T(4,128)(2,1)S(1)} %get-tuple-element.15), channel_id=1, source_target_pairs={{0,960},{64,0},{128,64},{192,128},{256,192},{320,256},{384,320},{4... | collective-permute-start | bytes 786440 | tf_op jit(solution)/shard_map/ppermute | solution.py:211
  26.8 6.4 %copy-start.1 = (bf16[1,512,4,256]{3,2,1,0:T(4,128)(2,1)S(1)}, bf16[1,512,4,256]{3,2,1,0:T(4,128)(2,1)}, u32[]{:S(2)}) copy-start(bf16[1,512,4,256]{3,2,1,0:T(4,128)(2,1)} %param.5) | copy-start | bytes 3145732
  119.1 13.8 %collective-permute-start.5 = (bf16[4,32,4,256]{3,2,1,0:T(4,128)(2,1)S(1)}, bf16[4,32,4,256]{3,2,1,0:T(4,128)(2,1)S(1)}, u32[]{:S(2)}, u32[]{:S(2)}) collective-permute-start(bf16[4,32,4,256]{3,2,1,0:T(4,128)(2,1)S(1)} %bitcast.17), channel_id=1, source_target_pairs={{0,128},{64,960},{128,256},{192,64},{256,384},{320,192},{384,512},... | collective-permute-start | bytes 786440 | tf_op jit(solution)/shard_map/ppermute | solution.py:217
  125.8 9.6 %collective-permute-start.4 = (bf16[4,32,4,256]{3,2,1,0:T(4,128)(2,1)S(1)}, bf16[4,32,4,256]{3,2,1,0:T(4,128)(2,1)S(1)}, u32[]{:S(2)}, u32[]{:S(2)}) collective-permute-start(bf16[4,32,4,256]{3,2,1,0:T(4,128)(2,1)S(1)} %bitcast.18), channel_id=1, source_target_pairs={{0,64},{64,128},{128,192},{192,256},{256,320},{320,384},{384,448},... | collective-permute-start | bytes 786440 | tf_op jit(solution)/shard_map/ppermute | solution.py:211
  127.8 8.9 %collective-permute-start.3 = (bf16[4,32,4,256]{3,2,1,0:T(4,128)(2,1)S(1)}, bf16[4,32,4,256]{3,2,1,0:T(4,128)(2,1)S(1)}, u32[]{:S(2)}, u32[]{:S(2)}) collective-permute-start(bf16[4,32,4,256]{3,2,1,0:T(4,128)(2,1)S(1)} %bitcast.19), channel_id=1, source_target_pairs={{0,960},{64,0},{128,64},{192,128},{256,192},{320,256},{384,320},{4... | collective-permute-start | bytes 786440 | tf_op jit(solution)/shard_map/ppermute | solution.py:211

commit v8 on v6

--- a/solution.py
+++ b/solution.py
@@ -1,3 +1,5 @@
+import functools
+
 import jax
 import jax.numpy as jnp
 from jax import lax
@@ -174,15 +176,14 @@
     )(picks, returned)
 
 
-def place_kernel(place_ref, same_ref, above_ref, below_ref, far_ref, out_ref, sems):
+def place_kernel(steps, place_ref, *refs):
     residue = place_ref[0]
+    piece_refs, (out_ref, sems) = refs[: len(steps)], refs[-2:]
     copies = [
         pltpu.make_async_copy(
             piece_ref, out_ref.at[:, (residue + step) % RADIX], sems.at[index]
         )
-        for index, (step, piece_ref) in enumerate(
-            ((0, same_ref), (1, above_ref), (RADIX - 1, below_ref), (2, far_ref))
-        )
+        for index, (step, piece_ref) in enumerate(zip(steps, piece_refs))
     ]
     for copy in copies:
         copy.start()
@@ -190,18 +191,25 @@
         copy.wait()
 
 
-def place(residue, same, *others):
-    shape = (same.shape[0], RADIX) + same.shape[1:]
-    return pl.pallas_call(
-        place_kernel,
+def place(residue, steps, pieces, *begun):
+    shape = pieces[0].shape[:1] + (RADIX,) + pieces[0].shape[1:]
+    return pl.pallas_call(
+        functools.partial(place_kernel, steps),
         in_specs=[pl.BlockSpec(memory_space=pltpu.SMEM)]
-        + [pl.BlockSpec(memory_space=pltpu.VMEM)] * 4,
+        + [pl.BlockSpec(memory_space=pltpu.VMEM)] * len(pieces)
+        + [pl.BlockSpec(memory_space=pl.ANY)] * len(begun),
         out_specs=pl.BlockSpec(memory_space=pl.ANY),
         out_shape=jax.ShapeDtypeStruct(shape, jnp.bfloat16),
-        scratch_shapes=[pltpu.SemaphoreType.DMA((4,))],
-        compiler_params=pltpu.CompilerParams(vmem_limit_bytes=VMEM_GRANT),
+        input_output_aliases={1 + len(pieces): 0} if begun else {},
+        scratch_shapes=[pltpu.SemaphoreType.DMA((len(steps),))],
+        compiler_params=pltpu.CompilerParams(vmem_limit_bytes=VMEM_GRANT),
+        cost_estimate=pl.CostEstimate(
+            flops=0,
+            bytes_accessed=4 * len(pieces) * pieces[0].size,
+            transcendentals=0,
+        ),
         name="place",
-    )(residue, same, *others)
+    )(residue, *pieces, *begun)
 
 
 def shifted(value, step):
@@ -271,7 +279,11 @@
     same = lax.all_gather(
         chosen, "dp", axis=0, tiled=False, axis_index_groups=strided(groups, RADIX)
     )
-    placed = place(residue, same, shifted(same, -1), shifted(same, 1), crossed(same))
+    near = (shifted(same, -1), shifted(same, 1))
+    far = crossed(same)
+    begun = place(residue, (0,), (same,))
+    begun = place(residue, (2,), (far,), begun)
+    placed = place(residue, (1, RADIX - 1), near, begun)
     return placed.reshape(blocks, row_count, block_width)
 
 

time: 137 us -> 138 us (level)
    ppermute x4, waiting for transfers between devices: 9.9 us -> 13 us  [shifted(): lax.ppermute(value, 'dp', [(i, (i + step) % size) for i in range(size)])]
    ppermute x2, waiting for transfers between devices: 3.73 us -> 0.77 us  [crossed(): return lax.ppermute(value, 'dp', pairs)]
  transfers between devices with their start and end apart: 6 -> 6, of which waited for: 6 -> 6; matrix products, arithmetic and copies ran while one was open for 2% -> 2% of each run, Pallas kernels for 0% -> 1%
where the time goes in v8:
time: 138 us
  blocking collectives  82.8 us (60%)
  starting transfers between devices  31.5 us (23%)
  waiting for transfers between devices  13.8 us (10%)
  Pallas kernels  6.75 us (5%)
    ppermute x4, starting transfers between devices, shifted(): lax.ppermute(value, 'dp', [(i, (i + step) % size) for i in range(size)])  27.4 us
    all_to_all x1, blocking collectives, body(): lax.all_to_all(combine(residue, by_residue, pieces), 'dp', 0, 0, tiled=Tr...  23.2 us
    all_to_all x1, blocking collectives, body(): lax.all_to_all(outgoing.reshape(owners, CAP, row_count, block_width), 'sh...  22.2 us
    all_gather x1, blocking collectives, body(): lax.all_gather(chosen, 'dp', axis=0, tiled=False, axis_index_groups=strid...  19.6 us
    all_to_all x1, blocking collectives, body(): returned = lax.all_to_all(fresh, 'shard', 0, 0, tiled=True)  17.8 us
    ppermute x4, waiting for transfers between devices, shifted(): lax.ppermute(value, 'dp', [(i, (i + step) % size) for i in range(size)])  13 us
    ppermute x2, starting transfers between devices, crossed(): return lax.ppermute(value, 'dp', pairs)  4.09 us
  transfers between devices with their start and end apart: 6, of which 6 were waited for; matrix products, arithmetic and copies ran while one was open for 2% of the time, Pallas kernels for 1%

profile of v8, /device:TPU:6, one launch (start us, length us, event | category | flops | bytes accessed | tf_op | source)
XLA Modules:
  0.0 137.6 jit_solution(9873034206446544051)
XLA Ops:
  0.0 0.0 copy-start
  0.0 0.0 copy-start.2
  0.0 1.2 part.1
  1.2 4.3 %collective-permute-start = (bf16[4,32,4,256]{3,2,1,0:T(4,128)(2,1)S(1)}, bf16[4,32,4,256]{3,2,1,0:T(4,128)(2,1)S(1)}, u32[]{:S(2)}, u32[]{:S(2)}) collective-permute-start(bf16[4,32,4,256]{3,2,1,0:T(4,128)(2,1)S(1)} %get-tuple-element.15), channel_id=1, source_target_pairs={{0,64},{64,128},{128,192},{192,256},{256,320},{320,384},{384,448},... | collective-permute-start | bytes 786440 | tf_op jit(solution)/shard_map/ppermute | solution.py:217
  5.5 15.9 %collective-permute-start.1 = (bf16[4,32,4,256]{3,2,1,0:T(4,128)(2,1)S(1)}, bf16[4,32,4,256]{3,2,1,0:T(4,128)(2,1)S(1)}, u32[]{:S(2)}, u32[]{:S(2)}) collective-permute-start(bf16[4,32,4,256]{3,2,1,0:T(4,128)(2,1)S(1)} %get-tuple-element.16), channel_id=1, source_target_pairs={{0,960},{64,0},{128,64},{192,128},{256,192},{320,256},{384,320},{4... | collective-permute-start | bytes 786440 | tf_op jit(solution)/shard_map/ppermute | solution.py:217
  21.4 1.9 %collective-permute-start.2 = (bf16[4,32,4,256]{3,2,1,0:T(4,128)(2,1)S(1)}, bf16[4,32,4,256]{3,2,1,0:T(4,128)(2,1)S(1)}, u32[]{:S(2)}, u32[]{:S(2)}) collective-permute-start(bf16[4,32,4,256]{3,2,1,0:T(4,128)(2,1)S(1)} %get-tuple-element.17), channel_id=1, source_target_pairs={{0,128},{64,960},{128,256},{192,64},{256,384},{320,192},{384,512},... | collective-permute-start | bytes 786440 | tf_op jit(solution)/shard_map/ppermute | solution.py:223
  23.3 0.0 copy-done
  23.3 0.7 dynamic-slice_bitcast_fusion
  24.0 0.1 lt.41
  24.1 0.1 lt.42
  24.3 0.1 select_reduce_fusion
  24.4 0.0 copy-done.2
  24.4 0.0 copy-start.1
  24.4 1.2 broadcast_multiply_fusion
  25.6 0.1 collective-permute-done.up_ref
  25.7 6.8 %collective-permute-done.1.down_ref = bf16[4,32,4,256]{3,2,1,0:T(4,128)(2,1)S(1)} collective-permute-done((bf16[4,32,4,256]{3,2,1,0:T(4,128)(2,1)S(1)}, bf16[4,32,4,256]{3,2,1,0:T(4,128)(2,1)S(1)}, u32[]{:S(2)}, u32[]{:S(2)}) %collective-permute-start.1) | collective-permute-done | bytes 262176 | tf_op jit(solution)/shard_map/ppermute | solution.py:217
  32.5 0.6 collective-permute-done.2.far_ref
  33.1 0.0 copy-done.1
  33.1 0.2 combine.1
  33.3 23.2 %all_to_all.15.parts_ref = bf16[4,32,4,256]{3,2,1,0:T(4,128)(2,1)S(1)} all-to-all(bf16[4,32,4,256]{3,2,1,0:T(4,128)(2,1)S(1)} %combine.1), channel_id=1, replica_groups={{0,256,512,768},{64,320,576,832},{128,384,640,896},{192,448,704,960},{1..., dimensions={0} | all-to-all | bytes 524288 | tf_op jit(solution)/shard_map/all_to_all | solution.py:262
  56.5 0.8 sum_and_gather.1
  57.3 22.2 %all_to_all.16 = bf16[64,2,4,256]{3,2,1,0:T(4,128)(2,1)S(1)} all-to-all(bf16[64,2,4,256]{3,2,1,0:T(4,128)(2,1)S(1)} %bitcast.20), channel_id=1, replica_groups=mesh['dp'=16,'shard'=64] {'shard'}, dimensions={0} | all-to-all | bytes 524288 | tf_op jit(solution)/shard_map/all_to_all | solution.py:271
  79.5 0.1 copy.14
  79.6 0.1 reshape.44.arrived_ref
  79.7 1.8 %refresh.1 = bf16[2,256,256]{2,1,0:T(8,128)(2,1)S(1)} custom-call(bf16[2,256,256]{2,1,0:T(8,128)(2,1)S(1)} %reshape.44.arrived_ref, f32[2,256,256]{2,1,0:T(8,128)S(1)} %get-tuple-element.23.left_ref, f32[2,256,256]{2,1,0:T(8,128)S(1)} %get-tuple-element.24.right_ref), custom_call_target="tpu_custom_call" | custom-call | flops 805306368 | bytes 1572864 | tf_op jit(solution)/shard_map/refresh/pallas_call | solution.py:66
  81.4 0.1 reshape.45
  81.5 0.1 copy.17
  81.6 17.8 %all_to_all.17 = bf16[64,2,4,256]{3,2,1,0:T(4,128)(2,1)S(1)} all-to-all(bf16[64,2,4,256]{3,2,1,0:T(4,128)(2,1)S(1)} %bitcast.23), channel_id=1, replica_groups=mesh['dp'=16,'shard'=64] {'shard'}, dimensions={0} | all-to-all | bytes 524288 | tf_op jit(solution)/shard_map/all_to_all | solution.py:277
  99.4 0.6 choose.1
  100.0 19.6 %all-gather = bf16[128,4,256]{2,1,0:T(4,128)(2,1)S(1)} all-gather(bf16[32,4,256]{2,1,0:T(4,128)(2,1)S(1)} %choose.1), channel_id=2, replica_groups={{0,256,512,768},{64,320,576,832},{128,384,640,896},{192,448,704,960},{1..., dimensions={0}, use_global_device_ids=true | all-gather | bytes 327680 | tf_op jit(solution)/shard_map/all_gather | solution.py:279
  119.6 2.2 %collective-permute-start.5 = (bf16[4,32,4,256]{3,2,1,0:T(4,128)(2,1)S(1)}, bf16[4,32,4,256]{3,2,1,0:T(4,128)(2,1)S(1)}, u32[]{:S(2)}, u32[]{:S(2)}) collective-permute-start(bf16[4,32,4,256]{3,2,1,0:T(4,128)(2,1)S(1)} %bitcast.16), channel_id=1, source_target_pairs={{0,128},{64,960},{128,256},{192,64},{256,384},{320,192},{384,512},... | collective-permute-start | bytes 786440 | tf_op jit(solution)/shard_map/ppermute | solution.py:223
  121.8 5.4 %collective-permute-start.3 = (bf16[4,32,4,256]{3,2,1,0:T(4,128)(2,1)S(1)}, bf16[4,32,4,256]{3,2,1,0:T(4,128)(2,1)S(1)}, u32[]{:S(2)}, u32[]{:S(2)}) collective-permute-start(bf16[4,32,4,256]{3,2,1,0:T(4,128)(2,1)S(1)} %bitcast.17), channel_id=1, source_target_pairs={{0,960},{64,0},{128,64},{192,128},{256,192},{320,256},{384,320},{4... | collective-permute-start | bytes 786440 | tf_op jit(solution)/shard_map/ppermute | solution.py:217
  127.1 1.9 %collective-permute-start.4 = (bf16[4,32,4,256]{3,2,1,0:T(4,128)(2,1)S(1)}, bf16[4,32,4,256]{3,2,1,0:T(4,128)(2,1)S(1)}, u32[]{:S(2)}, u32[]{:S(2)}) collective-permute-start(bf16[4,32,4,256]{3,2,1,0:T(4,128)(2,1)S(1)} %bitcast.18), channel_id=1, source_target_pairs={{0,64},{64,128},{128,192},{192,256},{256,320},{320,384},{384,448},... | collective-permute-start | bytes 786440 | tf_op jit(solution)/shard_map/ppermute | solution.py:217
  129.1 0.7 place.3.refs_1_
  129.8 0.2 collective-permute-done.5.refs_0_
  130.0 0.7 place.4.refs_2_
  130.7 3.8 %collective-permute-done.3.refs_0_ = bf16[4,32,4,256]{3,2,1,0:T(4,128)(2,1)S(1)} collective-permute-done((bf16[4,32,4,256]{3,2,1,0:T(4,128)(2,1)S(1)}, bf16[4,32,4,256]{3,2,1,0:T(4,128)(2,1)S(1)}, u32[]{:S(2)}, u32[]{:S(2)}) %collective-permute-start.3) | collective-permute-done | bytes 262176 | tf_op jit(solution)/shard_map/ppermute | solution.py:217
  134.5 2.3 %collective-permute-done.4.refs_1_ = bf16[4,32,4,256]{3,2,1,0:T(4,128)(2,1)S(1)} collective-permute-done((bf16[4,32,4,256]{3,2,1,0:T(4,128)(2,1)S(1)}, bf16[4,32,4,256]{3,2,1,0:T(4,128)(2,1)S(1)}, u32[]{:S(2)}, u32[]{:S(2)}) %collective-permute-start.4) | collective-permute-done | bytes 262176 | tf_op jit(solution)/shard_map/ppermute | solution.py:217
  136.8 0.8 place.5
  (3 shorter events, 0.0 us)
Async XLA Ops:
  0.0 23.3 %copy-start = (s32[16,128]{1,0:T(8,128)S(1)}, s32[16,128]{1,0:T(8,128)}, u32[]{:S(2)}) copy-start(s32[16,128]{1,0:T(8,128)} %param.6) | copy-start | bytes 24580
  0.0 24.4 %copy-start.2 = (f32[2,256,256]{2,1,0:T(8,128)S(1)}, f32[2,256,256]{2,1,0:T(8,128)}, u32[]{:S(2)}) copy-start(f32[2,256,256]{2,1,0:T(8,128)} %param.9) | copy-start | bytes 1572868
  1.2 24.5 %collective-permute-start = (bf16[4,32,4,256]{3,2,1,0:T(4,128)(2,1)S(1)}, bf16[4,32,4,256]{3,2,1,0:T(4,128)(2,1)S(1)}, u32[]{:S(2)}, u32[]{:S(2)}) collective-permute-start(bf16[4,32,4,256]{3,2,1,0:T(4,128)(2,1)S(1)} %get-tuple-element.15), channel_id=1, source_target_pairs={{0,64},{64,128},{128,192},{192,256},{256,320},{320,384},{384,448},... | collective-permute-start | bytes 786440 | tf_op jit(solution)/shard_map/ppermute | solution.py:217
  5.5 27.0 %collective-permute-start.1 = (bf16[4,32,4,256]{3,2,1,0:T(4,128)(2,1)S(1)}, bf16[4,32,4,256]{3,2,1,0:T(4,128)(2,1)S(1)}, u32[]{:S(2)}, u32[]{:S(2)}) collective-permute-start(bf16[4,32,4,256]{3,2,1,0:T(4,128)(2,1)S(1)} %get-tuple-element.16), channel_id=1, source_target_pairs={{0,960},{64,0},{128,64},{192,128},{256,192},{320,256},{384,320},{4... | collective-permute-start | bytes 786440 | tf_op jit(solution)/shard_map/ppermute | solution.py:217
  21.4 11.8 %collective-permute-start.2 = (bf16[4,32,4,256]{3,2,1,0:T(4,128)(2,1)S(1)}, bf16[4,32,4,256]{3,2,1,0:T(4,128)(2,1)S(1)}, u32[]{:S(2)}, u32[]{:S(2)}) collective-permute-start(bf16[4,32,4,256]{3,2,1,0:T(4,128)(2,1)S(1)} %get-tuple-element.17), channel_id=1, source_target_pairs={{0,128},{64,960},{128,256},{192,64},{256,384},{320,192},{384,512},... | collective-permute-start | bytes 786440 | tf_op jit(solution)/shard_map/ppermute | solution.py:223
  24.4 8.7 %copy-start.1 = (bf16[1,512,4,256]{3,2,1,0:T(4,128)(2,1)S(1)}, bf16[1,512,4,256]{3,2,1,0:T(4,128)(2,1)}, u32[]{:S(2)}) copy-start(bf16[1,512,4,256]{3,2,1,0:T(4,128)(2,1)} %param.5) | copy-start | bytes 3145732
  119.6 10.4 %collective-permute-start.5 = (bf16[4,32,4,256]{3,2,1,0:T(4,128)(2,1)S(1)}, bf16[4,32,4,256]{3,2,1,0:T(4,128)(2,1)S(1)}, u32[]{:S(2)}, u32[]{:S(2)}) collective-permute-start(bf16[4,32,4,256]{3,2,1,0:T(4,128)(2,1)S(1)} %bitcast.16), channel_id=1, source_target_pairs={{0,128},{64,960},{128,256},{192,64},{256,384},{320,192},{384,512},... | collective-permute-start | bytes 786440 | tf_op jit(solution)/shard_map/ppermute | solution.py:223
  121.8 12.7 %collective-permute-start.3 = (bf16[4,32,4,256]{3,2,1,0:T(4,128)(2,1)S(1)}, bf16[4,32,4,256]{3,2,1,0:T(4,128)(2,1)S(1)}, u32[]{:S(2)}, u32[]{:S(2)}) collective-permute-start(bf16[4,32,4,256]{3,2,1,0:T(4,128)(2,1)S(1)} %bitcast.17), channel_id=1, source_target_pairs={{0,960},{64,0},{128,64},{192,128},{256,192},{320,256},{384,320},{4... | collective-permute-start | bytes 786440 | tf_op jit(solution)/shard_map/ppermute | solution.py:217
  127.1 9.6 %collective-permute-start.4 = (bf16[4,32,4,256]{3,2,1,0:T(4,128)(2,1)S(1)}, bf16[4,32,4,256]{3,2,1,0:T(4,128)(2,1)S(1)}, u32[]{:S(2)}, u32[]{:S(2)}) collective-permute-start(bf16[4,32,4,256]{3,2,1,0:T(4,128)(2,1)S(1)} %bitcast.18), channel_id=1, source_target_pairs={{0,64},{64,128},{128,192},{192,256},{256,320},{320,384},{384,448},... | collective-permute-start | bytes 786440 | tf_op jit(solution)/shard_map/ppermute | solution.py:217

commit v9 on v6

--- a/solution.py
+++ b/solution.py
@@ -136,7 +136,7 @@
         out_ref[slot] = sum_ref[table_ref[slot]]
         return carry
 
-    lax.fori_loop(0, out_ref.shape[0], step, 0, unroll=8)
+    lax.fori_loop(0, out_ref.shape[0], step, 0, unroll=32)
 
 
 def sum_and_gather(table, parts):

time: 137 us -> 137 us (level)
  no operation moved by 1% of the time
where the time goes in v9:
time: 137 us; the launch traced here: 136 us
  blocking collectives  82.7 us (60%)
  starting transfers between devices  31.4 us (23%)
  waiting for transfers between devices  13.8 us (10%)
  Pallas kernels  5.45 us (4%)
    ppermute x4, starting transfers between devices, shifted(): lax.ppermute(value, 'dp', [(i, (i + step) % size) for i in range(size)])  27.2 us
    all_to_all x1, blocking collectives, body(): lax.all_to_all(combine(residue, by_residue, pieces), 'dp', 0, 0, tiled=Tr...  23.2 us
    all_to_all x1, blocking collectives, body(): lax.all_to_all(outgoing.reshape(owners, CAP, row_count, block_width), 'sh...  22.2 us
    all_gather x1, blocking collectives, body(): lax.all_gather(chosen, 'dp', axis=0, tiled=False, axis_index_groups=strid...  19.5 us
    all_to_all x1, blocking collectives, body(): returned = lax.all_to_all(fresh, 'shard', 0, 0, tiled=True)  17.8 us
    ppermute x4, waiting for transfers between devices, shifted(): lax.ppermute(value, 'dp', [(i, (i + step) % size) for i in range(size)])  10.2 us
    ppermute x2, starting transfers between devices, crossed(): return lax.ppermute(value, 'dp', pairs)  4.15 us
    ppermute x2, waiting for transfers between devices, crossed(): return lax.ppermute(value, 'dp', pairs)  3.66 us
  transfers between devices with their start and end apart: 6, of which 6 were waited for; matrix products, arithmetic and copies ran while one was open for 2% of the time, Pallas kernels for 0%

profile of v9, /device:TPU:6, one launch (start us, length us, event | category | flops | bytes accessed | tf_op | source)
XLA Modules:
  0.0 136.1 jit_solution(11599715694812361415)
XLA Ops:
  0.0 0.0 copy-start
  0.0 0.0 copy-start.2
  0.0 1.2 part.1
  1.2 4.3 %collective-permute-start = (bf16[4,32,4,256]{3,2,1,0:T(4,128)(2,1)S(1)}, bf16[4,32,4,256]{3,2,1,0:T(4,128)(2,1)S(1)}, u32[]{:S(2)}, u32[]{:S(2)}) collective-permute-start(bf16[4,32,4,256]{3,2,1,0:T(4,128)(2,1)S(1)} %get-tuple-element.15), channel_id=1, source_target_pairs={{0,64},{64,128},{128,192},{192,256},{256,320},{320,384},{384,448},... | collective-permute-start | bytes 786440 | tf_op jit(solution)/shard_map/ppermute | solution.py:209
  5.5 15.9 %collective-permute-start.1 = (bf16[4,32,4,256]{3,2,1,0:T(4,128)(2,1)S(1)}, bf16[4,32,4,256]{3,2,1,0:T(4,128)(2,1)S(1)}, u32[]{:S(2)}, u32[]{:S(2)}) collective-permute-start(bf16[4,32,4,256]{3,2,1,0:T(4,128)(2,1)S(1)} %get-tuple-element.16), channel_id=1, source_target_pairs={{0,960},{64,0},{128,64},{192,128},{256,192},{320,256},{384,320},{4... | collective-permute-start | bytes 786440 | tf_op jit(solution)/shard_map/ppermute | solution.py:209
  21.4 1.9 %collective-permute-start.2 = (bf16[4,32,4,256]{3,2,1,0:T(4,128)(2,1)S(1)}, bf16[4,32,4,256]{3,2,1,0:T(4,128)(2,1)S(1)}, u32[]{:S(2)}, u32[]{:S(2)}) collective-permute-start(bf16[4,32,4,256]{3,2,1,0:T(4,128)(2,1)S(1)} %get-tuple-element.17), channel_id=1, source_target_pairs={{0,128},{64,960},{128,256},{192,64},{256,384},{320,192},{384,512},... | collective-permute-start | bytes 786440 | tf_op jit(solution)/shard_map/ppermute | solution.py:215
  23.3 0.0 copy-done
  23.3 0.7 dynamic-slice_bitcast_fusion
  24.0 0.1 lt.41
  24.1 0.1 lt.42
  24.3 0.1 select_reduce_fusion
  24.4 0.0 copy-done.2
  24.4 0.0 copy-start.1
  24.4 1.2 broadcast_multiply_fusion
  25.6 0.1 collective-permute-done.up_ref
  25.7 6.8 %collective-permute-done.1.down_ref = bf16[4,32,4,256]{3,2,1,0:T(4,128)(2,1)S(1)} collective-permute-done((bf16[4,32,4,256]{3,2,1,0:T(4,128)(2,1)S(1)}, bf16[4,32,4,256]{3,2,1,0:T(4,128)(2,1)S(1)}, u32[]{:S(2)}, u32[]{:S(2)}) %collective-permute-start.1) | collective-permute-done | bytes 262176 | tf_op jit(solution)/shard_map/ppermute | solution.py:209
  32.5 0.6 collective-permute-done.2.far_ref
  33.1 0.0 copy-done.1
  33.1 0.2 combine.1
  33.3 23.2 %all_to_all.15.parts_ref = bf16[4,32,4,256]{3,2,1,0:T(4,128)(2,1)S(1)} all-to-all(bf16[4,32,4,256]{3,2,1,0:T(4,128)(2,1)S(1)} %combine.1), channel_id=1, replica_groups={{0,256,512,768},{64,320,576,832},{128,384,640,896},{192,448,704,960},{1..., dimensions={0} | all-to-all | bytes 524288 | tf_op jit(solution)/shard_map/all_to_all | solution.py:254
  56.5 0.7 sum_and_gather.1
  57.3 22.2 %all_to_all.16 = bf16[64,2,4,256]{3,2,1,0:T(4,128)(2,1)S(1)} all-to-all(bf16[64,2,4,256]{3,2,1,0:T(4,128)(2,1)S(1)} %bitcast.20), channel_id=1, replica_groups=mesh['dp'=16,'shard'=64] {'shard'}, dimensions={0} | all-to-all | bytes 524288 | tf_op jit(solution)/shard_map/all_to_all | solution.py:263
  79.4 0.1 copy.12
  79.5 0.1 reshape.44.arrived_ref
  79.6 1.8 %refresh.1 = bf16[2,256,256]{2,1,0:T(8,128)(2,1)S(1)} custom-call(bf16[2,256,256]{2,1,0:T(8,128)(2,1)S(1)} %reshape.44.arrived_ref, f32[2,256,256]{2,1,0:T(8,128)S(1)} %get-tuple-element.23.left_ref, f32[2,256,256]{2,1,0:T(8,128)S(1)} %get-tuple-element.24.right_ref), custom_call_target="tpu_custom_call" | custom-call | flops 805306368 | bytes 1572864 | tf_op jit(solution)/shard_map/refresh/pallas_call | solution.py:64
  81.4 0.1 reshape.45
  81.4 0.1 copy.15
  81.5 17.8 %all_to_all.17 = bf16[64,2,4,256]{3,2,1,0:T(4,128)(2,1)S(1)} all-to-all(bf16[64,2,4,256]{3,2,1,0:T(4,128)(2,1)S(1)} %bitcast.23), channel_id=1, replica_groups=mesh['dp'=16,'shard'=64] {'shard'}, dimensions={0} | all-to-all | bytes 524288 | tf_op jit(solution)/shard_map/all_to_all | solution.py:269
  99.3 0.6 choose.1
  99.9 19.5 %all-gather = bf16[128,4,256]{2,1,0:T(4,128)(2,1)S(1)} all-gather(bf16[32,4,256]{2,1,0:T(4,128)(2,1)S(1)} %choose.1), channel_id=2, replica_groups={{0,256,512,768},{64,320,576,832},{128,384,640,896},{192,448,704,960},{1..., dimensions={0}, use_global_device_ids=true | all-gather | bytes 327680 | tf_op jit(solution)/shard_map/all_gather | solution.py:271
  119.5 2.2 %collective-permute-start.5 = (bf16[4,32,4,256]{3,2,1,0:T(4,128)(2,1)S(1)}, bf16[4,32,4,256]{3,2,1,0:T(4,128)(2,1)S(1)}, u32[]{:S(2)}, u32[]{:S(2)}) collective-permute-start(bf16[4,32,4,256]{3,2,1,0:T(4,128)(2,1)S(1)} %bitcast.16), channel_id=1, source_target_pairs={{0,128},{64,960},{128,256},{192,64},{256,384},{320,192},{384,512},... | collective-permute-start | bytes 786440 | tf_op jit(solution)/shard_map/ppermute | solution.py:215
  121.7 5.2 %collective-permute-start.4 = (bf16[4,32,4,256]{3,2,1,0:T(4,128)(2,1)S(1)}, bf16[4,32,4,256]{3,2,1,0:T(4,128)(2,1)S(1)}, u32[]{:S(2)}, u32[]{:S(2)}) collective-permute-start(bf16[4,32,4,256]{3,2,1,0:T(4,128)(2,1)S(1)} %bitcast.17), channel_id=1, source_target_pairs={{0,64},{64,128},{128,192},{192,256},{256,320},{320,384},{384,448},... | collective-permute-start | bytes 786440 | tf_op jit(solution)/shard_map/ppermute | solution.py:209
  126.9 1.9 %collective-permute-start.3 = (bf16[4,32,4,256]{3,2,1,0:T(4,128)(2,1)S(1)}, bf16[4,32,4,256]{3,2,1,0:T(4,128)(2,1)S(1)}, u32[]{:S(2)}, u32[]{:S(2)}) collective-permute-start(bf16[4,32,4,256]{3,2,1,0:T(4,128)(2,1)S(1)} %bitcast.18), channel_id=1, source_target_pairs={{0,960},{64,0},{128,64},{192,128},{256,192},{320,256},{384,320},{4... | collective-permute-start | bytes 786440 | tf_op jit(solution)/shard_map/ppermute | solution.py:209
  128.8 3.1 %collective-permute-done.5.far_ref = bf16[4,32,4,256]{3,2,1,0:T(4,128)(2,1)S(1)} collective-permute-done((bf16[4,32,4,256]{3,2,1,0:T(4,128)(2,1)S(1)}, bf16[4,32,4,256]{3,2,1,0:T(4,128)(2,1)S(1)}, u32[]{:S(2)}, u32[]{:S(2)}) %collective-permute-start.5) | collective-permute-done | bytes 262176 | tf_op jit(solution)/shard_map/ppermute | solution.py:215
  131.9 3.2 %collective-permute-done.4.below_ref = bf16[4,32,4,256]{3,2,1,0:T(4,128)(2,1)S(1)} collective-permute-done((bf16[4,32,4,256]{3,2,1,0:T(4,128)(2,1)S(1)}, bf16[4,32,4,256]{3,2,1,0:T(4,128)(2,1)S(1)}, u32[]{:S(2)}, u32[]{:S(2)}) %collective-permute-start.4) | collective-permute-done | bytes 262176 | tf_op jit(solution)/shard_map/ppermute | solution.py:209
  135.1 0.1 collective-permute-done.3.above_ref
  135.2 1.0 place.1
  (3 shorter events, 0.0 us)
Async XLA Ops:
  0.0 23.3 %copy-start = (s32[16,128]{1,0:T(8,128)S(1)}, s32[16,128]{1,0:T(8,128)}, u32[]{:S(2)}) copy-start(s32[16,128]{1,0:T(8,128)} %param.6) | copy-start | bytes 24580
  0.0 24.4 %copy-start.2 = (f32[2,256,256]{2,1,0:T(8,128)S(1)}, f32[2,256,256]{2,1,0:T(8,128)}, u32[]{:S(2)}) copy-start(f32[2,256,256]{2,1,0:T(8,128)} %param.9) | copy-start | bytes 1572868
  1.2 24.5 %collective-permute-start = (bf16[4,32,4,256]{3,2,1,0:T(4,128)(2,1)S(1)}, bf16[4,32,4,256]{3,2,1,0:T(4,128)(2,1)S(1)}, u32[]{:S(2)}, u32[]{:S(2)}) collective-permute-start(bf16[4,32,4,256]{3,2,1,0:T(4,128)(2,1)S(1)} %get-tuple-element.15), channel_id=1, source_target_pairs={{0,64},{64,128},{128,192},{192,256},{256,320},{320,384},{384,448},... | collective-permute-start | bytes 786440 | tf_op jit(solution)/shard_map/ppermute | solution.py:209
  5.5 27.0 %collective-permute-start.1 = (bf16[4,32,4,256]{3,2,1,0:T(4,128)(2,1)S(1)}, bf16[4,32,4,256]{3,2,1,0:T(4,128)(2,1)S(1)}, u32[]{:S(2)}, u32[]{:S(2)}) collective-permute-start(bf16[4,32,4,256]{3,2,1,0:T(4,128)(2,1)S(1)} %get-tuple-element.16), channel_id=1, source_target_pairs={{0,960},{64,0},{128,64},{192,128},{256,192},{320,256},{384,320},{4... | collective-permute-start | bytes 786440 | tf_op jit(solution)/shard_map/ppermute | solution.py:209
  21.4 11.8 %collective-permute-start.2 = (bf16[4,32,4,256]{3,2,1,0:T(4,128)(2,1)S(1)}, bf16[4,32,4,256]{3,2,1,0:T(4,128)(2,1)S(1)}, u32[]{:S(2)}, u32[]{:S(2)}) collective-permute-start(bf16[4,32,4,256]{3,2,1,0:T(4,128)(2,1)S(1)} %get-tuple-element.17), channel_id=1, source_target_pairs={{0,128},{64,960},{128,256},{192,64},{256,384},{320,192},{384,512},... | collective-permute-start | bytes 786440 | tf_op jit(solution)/shard_map/ppermute | solution.py:215
  24.4 8.7 %copy-start.1 = (bf16[1,512,4,256]{3,2,1,0:T(4,128)(2,1)S(1)}, bf16[1,512,4,256]{3,2,1,0:T(4,128)(2,1)}, u32[]{:S(2)}) copy-start(bf16[1,512,4,256]{3,2,1,0:T(4,128)(2,1)} %param.5) | copy-start | bytes 3145732
  119.5 12.4 %collective-permute-start.5 = (bf16[4,32,4,256]{3,2,1,0:T(4,128)(2,1)S(1)}, bf16[4,32,4,256]{3,2,1,0:T(4,128)(2,1)S(1)}, u32[]{:S(2)}, u32[]{:S(2)}) collective-permute-start(bf16[4,32,4,256]{3,2,1,0:T(4,128)(2,1)S(1)} %bitcast.16), channel_id=1, source_target_pairs={{0,128},{64,960},{128,256},{192,64},{256,384},{320,192},{384,512},... | collective-permute-start | bytes 786440 | tf_op jit(solution)/shard_map/ppermute | solution.py:215
  121.7 13.4 %collective-permute-start.4 = (bf16[4,32,4,256]{3,2,1,0:T(4,128)(2,1)S(1)}, bf16[4,32,4,256]{3,2,1,0:T(4,128)(2,1)S(1)}, u32[]{:S(2)}, u32[]{:S(2)}) collective-permute-start(bf16[4,32,4,256]{3,2,1,0:T(4,128)(2,1)S(1)} %bitcast.17), channel_id=1, source_target_pairs={{0,64},{64,128},{128,192},{192,256},{256,320},{320,384},{384,448},... | collective-permute-start | bytes 786440 | tf_op jit(solution)/shard_map/ppermute | solution.py:209
  126.9 8.3 %collective-permute-start.3 = (bf16[4,32,4,256]{3,2,1,0:T(4,128)(2,1)S(1)}, bf16[4,32,4,256]{3,2,1,0:T(4,128)(2,1)S(1)}, u32[]{:S(2)}, u32[]{:S(2)}) collective-permute-start(bf16[4,32,4,256]{3,2,1,0:T(4,128)(2,1)S(1)} %bitcast.18), channel_id=1, source_target_pairs={{0,960},{64,0},{128,64},{192,128},{256,192},{320,256},{384,320},{4... | collective-permute-start | bytes 786440 | tf_op jit(solution)/shard_map/ppermute | solution.py:209
